TPU v7x, 32 devices: a whole 2x2x4 slice. The times are simulated.
32 devices in a mesh: dp: 2 (over core), row: 4 (over y, x), col: 4 (over z).
Axes of the slice: x: 2, y: 2, z: 4, core: 2. Of those that a mesh axis runs over, the one named last changes fastest.
Arguments:
- layer_input: bfloat16 [11664, 1152], P(('dp', 'col'), 'row'), may hold values from -6 to 6
- teacher: bfloat16 [11664, 1152], P(('dp', 'col'), 'row'), may hold values from -6 to 6
- valid: int32 [11664], P(('dp', 'col')), may hold values 0 or 1
- proj_in: bfloat16 [1152, 3456], P('row', 'col'), may hold values from -0.1875 to 0.1875
- bias_query: bfloat16 [1152], P('col'), may hold values from -4 to 4
- bias_value: bfloat16 [1152], P('col'), may hold values from -0.4375 to 0.4375
- proj_out: bfloat16 [1152, 1152], P('col', 'row'), may hold values from -3 to 3
- bias_out: bfloat16 [1152], P('row'), may hold values from -4 to 4
- norm1_gain: bfloat16 [1152], P('row'), may hold values from 0.25 to 1.75
- norm1_shift: bfloat16 [1152], P('row'), may hold values from -4 to 4
- norm2_gain: bfloat16 [1152], P('row'), may hold values from 0.25 to 1.75
- norm2_shift: bfloat16 [1152], P('row'), may hold values from -4 to 4
- w_up: bfloat16 [1152, 4304], P('row', 'col'), may hold values from -0.1875 to 0.1875
- bias_up: bfloat16 [4304], P('col'), may hold values from -4 to 4
- w_down: bfloat16 [4304, 1152], P('col', 'row'), may hold values from -0.09375 to 0.09375
- bias_down: bfloat16 [1152], P('row'), may hold values from -4 to 4
Outputs:
- layer_output: bfloat16 [11664, 1152], P(('dp', 'col'), 'row')
- loss_value: float32 [], replicated
- grad_input: float32 [11664, 1152], P(('dp', 'col'), 'row')
- grad_proj_in: float32 [4, 288, 3456], P('row', 'dp', 'col')
- grad_bias_query: float32 [1152], P('col')
- grad_bias_value: float32 [1152], P('col')
- grad_proj_out: float32 [1152, 4, 288], P('col', 'row', 'dp')
- grad_bias_out: float32 [1152], P('row')
- grad_norm1_gain: float32 [1152], P('row')
- grad_norm1_shift: float32 [1152], P('row')
- grad_norm2_gain: float32 [1152], P('row')
- grad_norm2_shift: float32 [1152], P('row')
- grad_w_up: float32 [4, 288, 4304], P('row', 'dp', 'col')
- grad_bias_up: float32 [4304], P('col')
- grad_w_down: float32 [4304, 4, 288], P('col', 'row', 'dp')
- grad_bias_down: float32 [1152], P('row')
All inputs are finite; a program needn't handle non-finite values. No bound on the sum of `valid` on one device may be relied on, other than what follows from the above.
Results may differ from a plain program's by a relative error of at most 0.012.
Values may be sent and summed in bfloat16 or wider, within the bound.
A program may use at most 256 MiB of HBM per device.

v0:
```python
import jax
import jax.numpy as jnp
from jax import lax
from jax.sharding import PartitionSpec as P

D = 1152
H = 16
HD = 72
FF = 4304
SEQ = 729


EPS = 1e-06


def feature_totals(left, right):
    return lax.psum(
        (jnp.sum(left, axis=-1, keepdims=True), jnp.sum(right, axis=-1, keepdims=True)), "row"
    )


def norm_forward(values, gain, shift):
    first_sum, second_sum = feature_totals(values, values * values)
    mean_rows = first_sum / D
    var_rows = second_sum / D - mean_rows * mean_rows
    inv_scale = lax.rsqrt(var_rows + EPS)
    normed = (values - mean_rows) * inv_scale
    return (normed, inv_scale, normed * gain + shift)


def norm_backward(grad_out, normed, inv_scale, gain):
    grad_normed = grad_out * gain
    first_sum, second_sum = feature_totals(grad_normed, grad_normed * normed)
    return inv_scale * (grad_normed - first_sum / D - normed * second_sum / D)


def first_section(local_rows, weight):
    gathered = lax.all_gather(local_rows, "col", axis=0, tiled=True)
    share_rows = gathered.shape[0] // lax.axis_size("row")

    def partial_term(row_start, row_count):
        return jnp.dot(gathered, weight, preferred_element_type=jnp.float32)

    result = lax.psum_scatter(
        partial_term(jnp.int32(0), lax.axis_size("row") * share_rows),
        "row",
        scatter_dimension=0,
        tiled=True,
    )
    return (gathered, result)


def second_section(quarter_rows, weight):
    gathered = lax.all_gather(quarter_rows, "row", axis=0, tiled=True)
    share_rows = gathered.shape[0] // lax.axis_size("col")

    def partial_term(row_start, row_count):
        return jnp.dot(gathered, weight, preferred_element_type=jnp.float32)

    result = lax.psum_scatter(
        partial_term(jnp.int32(0), lax.axis_size("col") * share_rows),
        "col",
        scatter_dimension=0,
        tiled=True,
    )
    return (gathered, result)


def second_section_back(grad_local, gathered, weight):
    grad_all = lax.all_gather(grad_local, "col", axis=0, tiled=True)
    grad_weight = lax.dot_general(
        gathered, grad_all, (((0,), (0,)), ((), ())), preferred_element_type=jnp.float32
    )
    share_rows = grad_all.shape[0] // lax.axis_size("row")

    def partial_term(row_start, row_count):
        return lax.dot_general(
            grad_all, weight, (((1,), (1,)), ((), ())), preferred_element_type=jnp.float32
        )

    result = lax.psum_scatter(
        partial_term(jnp.int32(0), lax.axis_size("row") * share_rows),
        "row",
        scatter_dimension=0,
        tiled=True,
    )
    return (grad_weight, result)


def first_section_back(grad_quarter, gathered, weight):
    grad_all = lax.all_gather(grad_quarter, "row", axis=0, tiled=True)
    grad_weight = lax.dot_general(
        gathered, grad_all, (((0,), (0,)), ((), ())), preferred_element_type=jnp.float32
    )
    share_rows = grad_all.shape[0] // lax.axis_size("col")

    def partial_term(row_start, row_count):
        return lax.dot_general(
            grad_all, weight, (((1,), (1,)), ((), ())), preferred_element_type=jnp.float32
        )

    result = lax.psum_scatter(
        partial_term(jnp.int32(0), lax.axis_size("col") * share_rows).astype(jnp.bfloat16),
        "col",
        scatter_dimension=0,
        tiled=True,
    ).astype(jnp.float32)
    return (grad_weight, result)


def attend(triple_img):
    score_scale = HD ** (-0.5)
    query_rows = triple_img[:, :, 0]
    key_rows = triple_img[:, :, 1]
    value_rows = triple_img[:, :, 2]
    raw_scores = jnp.einsum(
        "qhd,khd->hqk", query_rows, key_rows, preferred_element_type=jnp.float32
    )
    scaled = raw_scores * score_scale
    peak_score = jnp.max(scaled, axis=-1, keepdims=True)
    exp_scores = jnp.exp(scaled - peak_score)
    exp_total = jnp.sum(exp_scores, axis=-1, keepdims=True)
    soft_weights = (exp_scores / exp_total).astype(jnp.bfloat16)
    mixed_rows = jnp.einsum(
        "hqk,khd->qhd", soft_weights, value_rows, preferred_element_type=jnp.float32
    )
    return (mixed_rows.astype(jnp.bfloat16), peak_score + jnp.log(exp_total))


def attend_back(packed):
    triple_img, log_total, grad_mixed = packed
    score_scale = HD ** (-0.5)
    query_rows = triple_img[:, :, 0]
    key_rows = triple_img[:, :, 1]
    value_rows = triple_img[:, :, 2]
    raw_scores = jnp.einsum(
        "qhd,khd->hqk", query_rows, key_rows, preferred_element_type=jnp.float32
    )
    soft_weights = jnp.exp(raw_scores * score_scale - log_total)
    weights_low = soft_weights.astype(jnp.bfloat16)
    grad_values = jnp.einsum(
        "hqk,qhd->khd", weights_low, grad_mixed, preferred_element_type=jnp.float32
    )
    grad_soft = jnp.einsum(
        "qhd,khd->hqk", grad_mixed, value_rows, preferred_element_type=jnp.float32
    )
    inner_prod = jnp.sum(grad_soft * soft_weights, axis=-1, keepdims=True)
    grad_raw = (score_scale * soft_weights * (grad_soft - inner_prod)).astype(jnp.bfloat16)
    grad_query = jnp.einsum("hqk,khd->qhd", grad_raw, key_rows, preferred_element_type=jnp.float32)
    grad_keys = jnp.einsum("hqk,qhd->khd", grad_raw, query_rows, preferred_element_type=jnp.float32)
    return jnp.stack([grad_query, grad_keys, grad_values], axis=2).astype(jnp.bfloat16)


def on_device(
    layer_input,
    teacher,
    valid,
    proj_in,
    bias_query,
    bias_value,
    proj_out,
    bias_out,
    norm1_gain,
    norm1_shift,
    norm2_gain,
    norm2_shift,
    w_up,
    bias_up,
    w_down,
    bias_down,
):
    heads_here = H // lax.axis_size("col")
    head_width = heads_here * HD
    feat_here = layer_input.shape[1]
    units_here = w_up.shape[1]
    gain_one = norm1_gain.astype(jnp.float32)
    gain_two = norm2_gain.astype(jnp.float32)
    residual_in = layer_input.astype(jnp.float32)
    normed1, scale1, mid_one = norm_forward(residual_in, gain_one, norm1_shift.astype(jnp.float32))
    norm1_all, projected = first_section(mid_one.astype(jnp.bfloat16), proj_in)
    quarter = projected.shape[0]
    images = quarter // SEQ
    bias_shift = jnp.stack(
        [
            bias_query.astype(jnp.float32).reshape(heads_here, HD),
            jnp.zeros((heads_here, HD), jnp.float32),
            bias_value.astype(jnp.float32).reshape(heads_here, HD),
        ],
        axis=1,
    )
    triple = (projected.reshape(quarter, heads_here, 3, HD) + bias_shift).astype(jnp.bfloat16)
    triple_imgs = triple.reshape(images, SEQ, heads_here, 3, HD)
    mixed_imgs, log_totals = lax.map(attend, triple_imgs)
    mixed_all, attn_part = second_section(mixed_imgs.reshape(quarter, head_width), proj_out)
    resid1 = residual_in + attn_part + bias_out.astype(jnp.float32)
    normed2, scale2, mid_two = norm_forward(resid1, gain_two, norm2_shift.astype(jnp.float32))
    norm2_all, pre_part = first_section(mid_two.astype(jnp.bfloat16), w_up)
    pre = pre_part + bias_up.astype(jnp.float32)
    activated, gelu_pull = jax.vjp(lambda entry: jax.nn.gelu(entry, approximate=True), pre)
    act_all, down_part = second_section(activated.astype(jnp.bfloat16), w_down)
    result = resid1 + down_part + bias_down.astype(jnp.float32)
    mask_rows = valid.astype(jnp.float32)
    error_rows = result - teacher.astype(jnp.float32)
    err_part = jnp.sum(mask_rows[:, None] * error_rows * error_rows)
    count_part = jnp.sum(mask_rows) / lax.axis_size("row")
    err_total, valid_count = lax.psum((err_part, count_part), ("dp", "row", "col"))
    loss_value = err_total / (valid_count * D)
    tokens_all = layer_input.shape[0] * lax.axis_size("dp") * lax.axis_size("col")
    factor = tokens_all / (2.0 * valid_count)
    grad_result = 2.0 * error_rows * (mask_rows[:, None] * factor)
    grad_branch2 = grad_result.astype(jnp.bfloat16)
    grad_w_down, grad_act = second_section_back(grad_branch2, act_all, w_down)
    grad_pre = gelu_pull(grad_act)[0].astype(jnp.bfloat16)
    grad_w_up, grad_norm2 = first_section_back(grad_pre, norm2_all, w_up)
    grad_resid1 = grad_result + norm_backward(grad_norm2, normed2, scale2, gain_two)
    grad_branch1 = grad_resid1.astype(jnp.bfloat16)
    grad_proj_out, grad_mixed = second_section_back(grad_branch1, mixed_all, proj_out)
    grad_mixed_imgs = grad_mixed.astype(jnp.bfloat16).reshape(images, SEQ, heads_here, HD)
    grad_triple = lax.map(attend_back, (triple_imgs, log_totals, grad_mixed_imgs))
    grad_triple = grad_triple.reshape(quarter, heads_here, 3, HD)
    grad_proj_in, grad_norm1 = first_section_back(
        grad_triple.reshape(quarter, 3 * head_width), norm1_all, proj_in
    )
    grad_input = grad_resid1 + norm_backward(grad_norm1, normed1, scale1, gain_one)
    row_at = lax.axis_index("row") * feat_here
    col_at = lax.axis_index("col") * head_width
    feature_terms = jnp.stack(
        [
            jnp.sum(grad_norm1 * normed1, axis=0),
            jnp.sum(grad_norm1, axis=0),
            jnp.sum(grad_norm2 * normed2, axis=0),
            jnp.sum(grad_norm2, axis=0),
            jnp.sum(grad_branch1.astype(jnp.float32), axis=0),
            jnp.sum(grad_branch2.astype(jnp.float32), axis=0),
        ]
    )
    feature_full = lax.dynamic_update_slice_in_dim(
        jnp.zeros((6, D), jnp.float32), feature_terms, row_at, 1
    )
    grad_float = grad_triple.astype(jnp.float32)
    head_terms = jnp.stack(
        [
            jnp.sum(grad_float[:, :, 0], axis=0).reshape(head_width),
            jnp.sum(grad_float[:, :, 2], axis=0).reshape(head_width),
        ]
    )
    head_full = lax.dynamic_update_slice_in_dim(
        jnp.zeros((2, H * HD), jnp.float32), head_terms, col_at, 1
    )
    unit_terms = jnp.sum(grad_pre.astype(jnp.float32), axis=0)
    unit_full = lax.dynamic_update_slice_in_dim(
        jnp.zeros((FF,), jnp.float32), unit_terms, lax.axis_index("col") * units_here, 0
    )
    feature_full, head_full, unit_full = lax.psum(
        (feature_full, head_full, unit_full), ("dp", "row", "col")
    )
    feature_mine = lax.dynamic_slice_in_dim(feature_full, row_at, feat_here, 1)
    head_mine = lax.dynamic_slice_in_dim(head_full, col_at, head_width, 1)
    unit_mine = lax.dynamic_slice_in_dim(
        unit_full, lax.axis_index("col") * units_here, units_here, 0
    )
    grad_proj_in, grad_w_up = (
        lax.psum_scatter(
            grad_proj_in.astype(jnp.bfloat16), "dp", scatter_dimension=0, tiled=True
        ).astype(jnp.float32),
        lax.psum_scatter(
            grad_w_up.astype(jnp.bfloat16), "dp", scatter_dimension=0, tiled=True
        ).astype(jnp.float32),
    )
    grad_proj_out, grad_w_down = (
        lax.psum_scatter(
            grad_proj_out.astype(jnp.bfloat16), "dp", scatter_dimension=1, tiled=True
        ).astype(jnp.float32),
        lax.psum_scatter(
            grad_w_down.astype(jnp.bfloat16), "dp", scatter_dimension=1, tiled=True
        ).astype(jnp.float32),
    )
    grad_proj_in = grad_proj_in.reshape(1, grad_proj_in.shape[0], grad_proj_in.shape[1])
    grad_w_up = grad_w_up.reshape(1, grad_w_up.shape[0], grad_w_up.shape[1])
    grad_proj_out = grad_proj_out.reshape(grad_proj_out.shape[0], 1, grad_proj_out.shape[1])
    grad_w_down = grad_w_down.reshape(grad_w_down.shape[0], 1, grad_w_down.shape[1])
    return (
        result.astype(jnp.bfloat16),
        loss_value,
        grad_input,
        grad_proj_in,
        head_mine[0],
        head_mine[1],
        grad_proj_out,
        feature_mine[4],
        feature_mine[0],
        feature_mine[1],
        feature_mine[2],
        feature_mine[3],
        grad_w_up,
        unit_mine,
        grad_w_down,
        feature_mine[5],
    )


def solution(mesh):
    placed = (
        P(("dp", "col"), "row"),
        P(("dp", "col"), "row"),
        P(("dp", "col")),
        P("row", "col"),
        P("col"),
        P("col"),
        P("col", "row"),
        P("row"),
        P("row"),
        P("row"),
        P("row"),
        P("row"),
        P("row", "col"),
        P("col"),
        P("col", "row"),
        P("row"),
    )
    return jax.shard_map(
        on_device,
        mesh=mesh,
        in_specs=placed,
        out_specs=(
            P(("dp", "col"), "row"),
            P(),
            P(("dp", "col"), "row"),
            P("row", "dp", "col"),
            P("col"),
            P("col"),
            P("col", "row", "dp"),
            P("row"),
            P("row"),
            P("row"),
            P("row"),
            P("row"),
            P("row", "dp", "col"),
            P("col"),
            P("col", "row", "dp"),
            P("row"),
        ),
        check_vma=False,
    )
```

profile of v0, /device:TPU:0, one launch (start us, length us, event | category | flops | bytes accessed | tf_op | source)
XLA Modules:
  0.0 3435.1 jit_solution(14643462860390527923)
XLA Ops:
  10.2 17.4 all-reduce.13
  32.3 67.9 %all-gather.17.cloned.1.call-done = bf16[4,1458,288]{1,2,0:T(8,128)(2,1)} async-done(((bf16[1,1458,288]{1,2,0:T(8,128)(2,1)}), bf16[4,1458,288]{1,2,0:T(8,128)(2,1)}) %all-gather.17.cloned.1.call-update) | async-done | bytes 3359248 | tf_op jit(solution)/shard_map/all_gather | solution.py:38
  100.2 6.5 copy.61
  106.7 7.0 reshape.178
  113.7 12.4 fusion.72
  126.1 218.8 %fusion = f32[1472,864]{1,0:T(8,128)} fusion(f32[5832,864]{1,0:T(8,128)} %fusion.72), kind=kCustom, calls=%all-reduce-scatter | all-reduce-scatter fusion | flops 5087233 | bytes 25243136
  351.3 14.0 concatenate.8
  370.5 6.1 copy.62
  376.7 8.5 reshape.153
  390.1 11.8 while.22
  404.9 15.3 reshape.179
  420.3 49.3 %all-gather.19.cloned.1.call-done = bf16[4,1458,288]{1,2,0:T(8,128)(2,1)} async-done(((bf16[1,1458,288]{1,2,0:T(8,128)(2,1)}), bf16[4,1458,288]{1,2,0:T(8,128)(2,1)}) %all-gather.19.cloned.1.call-update) | async-done | bytes 3359248 | tf_op jit(solution)/shard_map/all_gather | solution.py:54
  469.6 6.5 copy.65
  476.1 6.9 reshape.180
  483.0 6.8 fusion.73
  492.8 235.9 %all-reduce.22.cloned.1.call-done = f32[5832,288]{0,1:T(8,128)} async-done(((f32[5832,288]{0,1:T(8,128)}), f32[5832,288]{0,1:T(8,128)}) %all-reduce.22.cloned.1.call-update) | async-done | bytes 6718480
  732.3 16.5 all-reduce.12
  752.3 67.2 %all-gather.21.cloned.1.call-done = bf16[4,1458,288]{1,2,0:T(8,128)(2,1)} async-done(((bf16[1,1458,288]{1,2,0:T(8,128)(2,1)}), bf16[4,1458,288]{1,2,0:T(8,128)(2,1)}) %all-gather.21.cloned.1.call-update) | async-done | bytes 3359248 | tf_op jit(solution)/shard_map/all_gather | solution.py:38
  819.5 6.5 copy.66
  826.0 6.9 reshape.182
  832.9 13.7 fusion.74
  848.6 444.2 %all-reduce.24.cloned.1.call-done = f32[5832,1076]{0,1:T(8,128)} async-done(((f32[5832,1076]{0,1:T(8,128)}), f32[5832,1076]{0,1:T(8,128)}) %all-reduce.24.cloned.1.call-update) | async-done | bytes 25100944
  1292.8 6.1 fusion.37
  1299.1 128.5 %all-gather.23.cloned.1.call-done = bf16[4,1458,1076]{1,2,0:T(8,128)(2,1)} async-done(((bf16[1,1458,1076]{1,2,0:T(8,128)(2,1)}), bf16[4,1458,1076]{1,2,0:T(8,128)(2,1)}) %all-gather.23.cloned.1.call-update) | async-done | bytes 12550480 | tf_op jit(solution)/shard_map/all_gather | solution.py:54
  1427.6 42.2 %copy.67 = bf16[4,1458,1076]{1,0,2:T(4,128)(2,1)} copy(bf16[4,1458,1076]{1,2,0:T(8,128)(2,1)} %all-gather.23.cloned.1.call-done) | data formatting | bytes 25100928 | tf_op jit(solution)/shard_map/all_gather | solution.py:54
  1469.8 25.3 reshape.184
  1495.1 11.1 fusion.75
  1508.3 45.8 %psum.96 = f32[]{:T(128)} all-reduce(f32[]{:T(128)S(6)} %div.45), channel_id=1, replica_groups=mesh['dp'=2,'row'=4,'col'=4] {'dp','row','col'}, use_global_device_ids=true, to_apply=%region_19.20 | all-reduce | flops 1 | bytes 8 | tf_op jit(solution)/shard_map/psum | solution.py:206
  1557.3 188.9 %all-reduce.26.cloned.1.call-done = f32[5832,288]{0,1:T(8,128)} async-done(((f32[5832,288]{0,1:T(8,128)}), f32[5832,288]{0,1:T(8,128)}) %all-reduce.26.cloned.1.call-update) | async-done | bytes 6718480
  1751.5 69.0 %all-gather.25.cloned.1.call-done = bf16[4,1458,288]{1,2,0:T(8,128)(2,1)} async-done(((bf16[1,1458,288]{1,2,0:T(8,128)(2,1)}), bf16[4,1458,288]{1,2,0:T(8,128)(2,1)}) %all-gather.25.cloned.1.call-update) | async-done | bytes 3359248 | tf_op jit(solution)/shard_map/all_gather | solution.py:70
  1820.5 6.5 copy.68
  1827.0 7.0 reshape.186
  1834.0 13.5 fusion.76
  1847.6 446.1 %all-reduce.28.cloned.1.call-done = f32[5832,1076]{0,1:T(8,128)} async-done(((f32[5832,1076]{0,1:T(8,128)}), f32[5832,1076]{0,1:T(8,128)}) %all-reduce.28.cloned.1.call-update) | async-done | bytes 25100944
  2293.8 11.6 convert_reduce_fusion
  2305.4 128.4 %all-gather.27.cloned.1.call-done = bf16[4,1458,1076]{1,2,0:T(8,128)(2,1)} async-done(((bf16[1,1458,1076]{1,2,0:T(8,128)(2,1)}), bf16[4,1458,1076]{1,2,0:T(8,128)(2,1)}) %all-gather.27.cloned.1.call-update) | async-done | bytes 12550480 | tf_op jit(solution)/shard_map/all_gather | solution.py:91
  2433.8 41.9 %copy.69 = bf16[4,1458,1076]{1,0,2:T(4,128)(2,1)} copy(bf16[4,1458,1076]{1,2,0:T(8,128)(2,1)} %all-gather.27.cloned.1.call-done) | data formatting | bytes 25100928 | tf_op jit(solution)/shard_map/all_gather | solution.py:91
  2475.8 25.4 reshape.188
  2501.1 10.6 convolution_convert_fusion.3
  2512.4 128.7 %all-reduce.30.cloned.1.call-done = bf16[5832,288]{0,1:T(8,128)(2,1)} async-done(((bf16[5832,288]{0,1:T(8,128)(2,1)}), bf16[5832,288]{0,1:T(8,128)(2,1)}) %all-reduce.30.cloned.1.call-update) | async-done | bytes 3359248
  2644.7 15.9 all-reduce.11
  2660.6 6.0 convert_reduce_fusion.5
  2669.4 66.9 %all-gather.29.cloned.1.call-done = bf16[4,1458,288]{1,2,0:T(8,128)(2,1)} async-done(((bf16[1,1458,288]{1,2,0:T(8,128)(2,1)}), bf16[4,1458,288]{1,2,0:T(8,128)(2,1)}) %all-gather.29.cloned.1.call-update) | async-done | bytes 3359248 | tf_op jit(solution)/shard_map/all_gather | solution.py:70
  2736.2 6.5 copy.70
  2742.7 6.8 reshape.190
  2749.6 6.7 fusion.77
  2756.2 229.4 %all-reduce.33 = bf16[5832,288]{0,1:T(8,128)(2,1)} all-reduce(f32[5832,288]{0,1:T(8,128)} %fusion.77), channel_id=8, replica_groups=mesh['dp'=2,'row'=4,'col'=4] {'row'}, use_global_device_ids=true, to_apply=%region_26.27.clone | all-reduce | flops 1679616 | bytes 10077696
  2994.0 62.8 %while.23 = (s32[]{:T(128)}, bf16[2,729,4,3,72]{1,4,2,3,0:T(8,128)(2,1)}, bf16[2,729,4,3,72]{1,4,2,3,0:T(8,128)(2,1)S(1)}, f32[2,4,729,1]{2,1,3,0:T(4,128)S(1)}, bf16[2,729,4,72]{1,3,2,0:T(8,128)(2,1)}, /*index=5*/s32[]{:T(128)}) while((s32[]{:T(128)}, bf16[2,729,4,3,72]{1,4,2,3,0:T(8,128)(2,1)}, ...), condition=%wide.region_29.30_spmd, body=%wide.region_27.29_spmd.sunk | while | flops 1562591232 | bytes 169299232 | solution.py:219
  3004.5 10.4 multiply_convert_fusion.5
  3035.9 10.4 multiply_convert_fusion.5
  3056.9 10.4 copy.80
  3067.3 13.0 reshape.195
  3080.6 11.7 convolution_convert_fusion.4
  3092.4 11.1 convolution_convert_fusion.5
  3103.5 5.6 convolution_convert_fusion.7
  3109.2 74.5 %all-gather.31.cloned.1.call-done = bf16[4,1458,864]{2,1,0:T(8,128)(2,1)} async-done(((bf16[1,1458,864]{2,1,0:T(8,128)(2,1)}), bf16[4,1458,864]{2,1,0:T(8,128)(2,1)}) %all-gather.31.cloned.1.call-update) | async-done | bytes 10077712 | tf_op jit(solution)/shard_map/all_gather | solution.py:91
  3183.7 14.7 reshape.192
  3198.5 9.5 convolution_convert_fusion.6
  3208.2 11.2 convolution_convert_fusion.2
  3224.3 6.8 copy.75
  3231.1 8.2 reshape.170
  3245.7 117.0 %all-reduce.32.cloned.1.call-done = bf16[5832,288]{0,1:T(8,128)(2,1)} async-done(((bf16[5832,288]{0,1:T(8,128)(2,1)}), bf16[5832,288]{0,1:T(8,128)(2,1)}) %all-reduce.32.cloned.1.call-update) | async-done | bytes 3359248
  3365.3 15.9 all-reduce.10
  3381.6 39.7 %all-reduce.9 = (f32[]{:T(128)}, f32[2,1152]{1,0:T(2,128)S(1)}, f32[6,1152]{1,0:T(8,128)S(1)}, f32[4304]{0:T(1024)S(1)}) all-reduce(f32[]{:T(128)} %get-tuple-element.160, f32[2,1152]{1,0:T(2,128)S(1)} %dynamic_update_slice.21, f32[6,1152]{1,0:T(8,128)S(1)} %dynamic_update_slice.22, ...), channel_id=1, replica_groups=mesh['dp'=2,'row'=4,'col'=4] {'dp','row','col'}, use_global_device_ids=true, to_apply=%region_17.18 | all-reduce | flops 13521 | bytes 108168 | tf_op jit(solution)/shard_map/psum | solution.py:206
  (227 shorter events, 134.2 us)
Async XLA Ops:
  7.2 1487.9 %copy-start = (bf16[1076,288]{0,1:T(8,128)(2,1)S(1)}, bf16[1076,288]{0,1:T(8,128)(2,1)}, u32[]{:S(2)}) copy-start(bf16[1076,288]{0,1:T(8,128)(2,1)} %param.34) | copy-start | bytes 1859332
  7.2 23.8 copy-start.32
  7.2 23.6 copy-start.33
  7.2 23.7 copy-start.34
  7.2 93.0 %all-gather.17.cloned.1.call-start = ((), (), s32[]{:S(2)}) async-start(), calls=%async_computation.8 | async-start | bytes 4423680 | tf_op jit(solution)/shard_map/all_gather | solution.py:38
  9.5 90.7 %copy-start.24 = (f32[288]{0:T(512)}, f32[288]{0:T(512)S(1)}, u32[]{:S(2)}) copy-start(f32[288]{0:T(512)S(1)} %convert_element_type.127) | copy-start | bytes 3460
  27.6 0.6 copy-start.17
  27.6 0.6 copy-start.19
  30.7 438.9 %all-gather.19.cloned.1.call-start = ((), (), s32[]{:S(2)}) async-start(), calls=%async_computation.9 | async-start | bytes 4423680 | tf_op jit(solution)/shard_map/all_gather | solution.py:54
  106.7 7.0 copy-start.13
  345.9 5.4 collective-permute-start
  401.9 67.7 %copy-start.15 = (f32[2,4,729,1]{2,1,3,0:T(4,128)}, f32[2,4,729,1]{2,1,3,0:T(4,128)S(1)}, u32[]{:S(2)}) copy-start(f32[2,4,729,1]{2,1,3,0:T(4,128)S(1)} %get-tuple-element.248) | copy-start | bytes 69988
  420.2 308.5 %all-reduce.22.cloned.1.call-start = ((), (), s32[]{:S(2)}) async-start(), calls=%async_computation.16 | async-start | bytes 13565952
  476.1 6.9 copy-start.11
  489.8 0.7 copy-start.38
  489.8 1.2 copy-start.35
  489.8 1.2 copy-start.36
  489.8 1.8 copy-start.37
  489.8 329.7 %all-gather.21.cloned.1.call-start = ((), (), s32[]{:S(2)}) async-start(), calls=%async_computation.10 | async-start | bytes 4423680 | tf_op jit(solution)/shard_map/all_gather | solution.py:38
  752.3 540.6 %all-reduce.24.cloned.1.call-start = ((), (), s32[]{:S(2)}) async-start(), calls=%async_computation.17 | async-start | bytes 50872320
  846.6 580.9 %all-gather.23.cloned.1.call-start = ((), (), s32[]{:S(2)}) async-start(), calls=%async_computation.11 | async-start | bytes 16588800 | tf_op jit(solution)/shard_map/all_gather | solution.py:54
  1299.0 447.2 %all-reduce.26.cloned.1.call-start = ((), (), s32[]{:S(2)}) async-start(), calls=%async_computation.18 | async-start | bytes 13565952
  1506.3 314.3 %all-gather.25.cloned.1.call-start = ((), (), s32[]{:S(2)}) async-start(), calls=%async_computation.12 | async-start | bytes 4423680 | tf_op jit(solution)/shard_map/all_gather | solution.py:70
  1751.4 542.3 %all-reduce.28.cloned.1.call-start = ((), (), s32[]{:S(2)}) async-start(), calls=%async_computation.19 | async-start | bytes 50872320
  1847.5 446.2 %copy-start.21 = (f32[1076]{0:T(1024)S(1)}, f32[1076]{0:T(1024)}, u32[]{:S(2)}) copy-start(f32[1076]{0:T(1024)} %convert_element_type.135) | copy-start | bytes 12916
  1847.6 586.3 %all-gather.27.cloned.1.call-start = ((), (), s32[]{:S(2)}) async-start(), calls=%async_computation.13 | async-start | bytes 16588800 | tf_op jit(solution)/shard_map/all_gather | solution.py:91
  2305.4 335.8 %all-reduce.30.cloned.1.call-start = ((), (), s32[]{:S(2)}) async-start(), calls=%async_computation.20 | async-start | bytes 6782976
  2475.8 25.4 copy-start.12
  2511.7 0.7 copy-start.22
  2511.7 129.4 %copy-start.27 = (f32[288]{0:T(512)S(1)}, f32[288]{0:T(512)}, u32[]{:S(2)}) copy-start(f32[288]{0:T(512)} %convert_element_type.132) | copy-start | bytes 3460
  2511.7 148.9 %copy-start.23 = (f32[1458]{0:T(1024)S(1)}, f32[1458]{0:T(1024)}, u32[]{:S(2)}) copy-start(f32[1458]{0:T(1024)} %multiply_multiply_fusion.3) | copy-start | bytes 17500
  2511.8 224.5 %all-gather.29.cloned.1.call-start = ((), (), s32[]{:S(2)}) async-start(), calls=%async_computation.14 | async-start | bytes 4423680 | tf_op jit(solution)/shard_map/all_gather | solution.py:70
  2666.7 1.2 copy-start.9
  2668.9 514.8 %all-gather.31.cloned.1.call-start = ((), (), s32[]{:S(2)}) async-start(), calls=%async_computation.15 | async-start | bytes 13117440 | tf_op jit(solution)/shard_map/all_gather | solution.py:91
  2985.6 8.4 copy-start.16
  2994.0 1.5 copy-start.4
  2997.0 1.4 copy-start.6
  2998.4 6.1 copy-start.2
  3014.9 7.7 copy-start.3
  3018.2 4.4 copy-start.7
  3022.6 2.8 copy-start.5
  3025.4 1.5 copy-start.4
  3028.4 1.4 copy-start.6
  3029.8 6.1 copy-start.2
  3046.3 7.7 copy-start.3
  3049.6 4.4 copy-start.7
  3054.0 2.9 copy-start.5
  3080.3 139.9 %reduce-scatter.20.cloned.1.call-start = ((), (), s32[]{:S(2)}) async-start(), calls=%async_computation.7 | async-start | bytes 995328 | tf_op jit(solution)/shard_map/reduce_scatter | solution.py:274
  3092.3 130.1 %reduce-scatter.18.cloned.1.call-start = ((), (), s32[]{:S(2)}) async-start(), calls=%async_computation.6 | async-start | bytes 995328 | tf_op jit(solution)/shard_map/reduce_scatter | solution.py:266
  3103.5 138.7 %reduce-scatter.16.cloned.1.call-start = ((), (), s32[]{:S(2)}) async-start(), calls=%async_computation.5 | async-start | bytes 331776 | tf_op jit(solution)/shard_map/reduce_scatter | solution.py:271
  3109.1 134.7 %reduce-scatter.14.cloned.1.call-start = ((), (), s32[]{:S(2)}) async-start(), calls=%async_computation.4 | async-start | bytes 774144 | tf_op jit(solution)/shard_map/reduce_scatter | solution.py:263
  3198.5 9.8 copy-start.14
  3208.0 154.7 %all-reduce.32.cloned.1.call-start = ((), (), s32[]{:S(2)}) async-start(), calls=%async_computation.21 | async-start | bytes 6782976
  3219.5 0.7 copy-start.30
  3219.5 2.6 copy-start.26
  3219.5 4.8 copy-start.31
  3219.5 4.8 copy-start.29
  3219.5 4.8 copy-start.28
  3239.4 123.3 %copy-start.8 = (bf16[1458,288]{0,1:T(8,128)(2,1)S(1)}, bf16[1458,288]{0,1:T(8,128)(2,1)}, u32[]{:S(2)}) copy-start(bf16[1458,288]{0,1:T(8,128)(2,1)} %param.20) | copy-start | bytes 2519428
  3239.4 123.3 %copy-start.18 = (f32[1458]{0:T(1024)S(1)}, f32[1458]{0:T(1024)}, u32[]{:S(2)}) copy-start(f32[1458]{0:T(1024)} %copy-done.17) | copy-start | bytes 17500
  3239.4 123.3 %copy-start.20 = (f32[1458]{0:T(1024)S(1)}, f32[1458]{0:T(1024)}, u32[]{:S(2)}) copy-start(f32[1458]{0:T(1024)} %copy-done.19) | copy-start | bytes 17500
  3239.4 123.3 %copy-start.25 = (f32[288]{0:T(512)S(1)}, f32[288]{0:T(512)}, u32[]{:S(2)}) copy-start(f32[288]{0:T(512)} %copy-done.24) | copy-start | bytes 3460
  3239.4 184.0 %copy-start.10 = (f32[1458,288]{0,1:T(8,128)S(1)}, f32[1458,288]{0,1:T(8,128)}, u32[]{:S(2)}) copy-start(f32[1458,288]{0,1:T(8,128)} %copy-done.9) | copy-start | bytes 5038852
  3243.8 182.9 %copy-start.1 = (bf16[1076,288]{0,1:T(8,128)(2,1)S(1)}, bf16[1076,288]{0,1:T(8,128)(2,1)}, u32[]{:S(2)}) copy-start(bf16[1076,288]{0,1:T(8,128)(2,1)} %param.34) | copy-start | bytes 1859332
Sparse Core Ops, SparseCore 0:
  30.8 69.3 all-gather.16
  420.3 49.1 all-gather.18
  489.9 238.7 all-reduce.21
  752.4 67.0 all-gather.20
  846.8 446.0 all-reduce.23
  1299.1 128.4 all-gather.22
  1506.4 239.7 all-reduce.25
  1751.6 68.9 all-gather.24
  1847.7 446.0 all-reduce.27
  2305.5 128.2 all-gather.26
  2511.9 129.2 all-reduce.29
  2669.0 67.1 all-gather.28
  3080.5 103.2 all-gather.30
  3186.4 8.1 reduce-scatter.19
  3197.3 9.2 reduce-scatter.17
  3209.3 8.7 reduce-scatter.15
  3220.8 9.0 reduce-scatter.13
  3232.3 130.3 all-reduce.31
where the time goes:
time: 3450 us; the launch traced here: 3440 us
  waiting for transfers between devices  2220 us (64%)
  blocking collectives  600 us (17%)
  local copies, waits for them, and re-layouts  332 us (10%)
  matrix products  164 us (5%)
  other arithmetic  98.6 us (3%)
    unnamed x25, waiting for transfers between devices  1560 us
    unnamed x2, blocking collectives  448 us
    all_gather x2, waiting for transfers between devices, first_section_back(): grad_all = lax.all_gather(grad_quarter, 'row', axis=0, tiled=True)  203 us
    all_gather x2, waiting for transfers between devices, second_section(): gathered = lax.all_gather(quarter_rows, 'row', axis=0, tiled=True)  178 us
    unnamed x82, local copies, waits for them, and re-layouts  163 us
    all_gather x2, waiting for transfers between devices, second_section_back(): grad_all = lax.all_gather(grad_local, 'col', axis=0, tiled=True)  136 us
    all_gather x2, waiting for transfers between devices, first_section(): gathered = lax.all_gather(local_rows, 'col', axis=0, tiled=True)  135 us
    psum x2, blocking collectives, on_device(): lax.psum((err_part, count_part), ('dp', 'row', 'col'))  85.5 us
  transfers between devices with their start and end apart: 19, of which 15 were waited for; matrix products, arithmetic and copies ran while one was open for 3% of the time, Pallas kernels for 0%

commit v1 on v0

--- a/solution.py
+++ b/solution.py
@@ -299,6 +299,384 @@
     )
 
 
+def pair_swap(values):
+    return lax.ppermute(values, "dp", [(0, 1), (1, 0)])
+
+
+def row_swap(values, bit):
+    return lax.ppermute(values, "row", [(i, i ^ bit) for i in range(lax.axis_size("row"))])
+
+
+def ring_order(size):
+    return list(range(0, size, 2)) + list(range(1, size, 2))[::-1]
+
+
+def ring_shift(values, step):
+    order = ring_order(lax.axis_size("col"))
+    size = len(order)
+    return lax.ppermute(
+        values, "col", [(order[i], order[(i + step) % size]) for i in range(size)]
+    )
+
+
+def gather_ring(shard):
+    shards = [shard]
+    for _ in range(lax.axis_size("col") - 1):
+        shards.append(ring_shift(shards[-1], 1))
+    return shards
+
+
+def gather_plane(block):
+    half = block.shape[0] // 2
+    one = row_swap(block, 1)
+    two = row_swap(block, 2)
+    three_low = row_swap(one[:half], 2)
+    three_high = row_swap(two[half:], 1)
+    return jnp.concatenate([block, one, two, three_low, three_high], axis=0)
+
+
+def add_low(left, right):
+    return (left.astype(jnp.float32) + right.astype(jnp.float32)).astype(jnp.bfloat16)
+
+
+def scatter_plane(grad):
+    rows = grad.shape[0] // 4
+    half = rows // 2
+    part = [grad[i * half : (i + 1) * half] for i in range(8)]
+    one_high = row_swap(part[3], 1)
+    two_low = row_swap(part[4], 2)
+    one_low = row_swap(add_low(part[2], row_swap(part[6], 2)), 1)
+    two_high = row_swap(add_low(part[5], row_swap(part[7], 1)), 2)
+    low = part[0].astype(jnp.float32) + one_low.astype(jnp.float32) + two_low.astype(jnp.float32)
+    high = part[1].astype(jnp.float32) + one_high.astype(jnp.float32) + two_high.astype(jnp.float32)
+    return jnp.concatenate([low, high], axis=0)
+
+
+def layer_norm(values):
+    mean_rows = jnp.mean(values, axis=-1, keepdims=True)
+    centered = values - mean_rows
+    inv_scale = lax.rsqrt(jnp.mean(centered * centered, axis=-1, keepdims=True) + EPS)
+    return centered * inv_scale, inv_scale
+
+
+def layer_norm_back(grad_out, normed, inv_scale, gain):
+    grad_normed = grad_out * gain
+    first = jnp.mean(grad_normed, axis=-1, keepdims=True)
+    second = jnp.mean(grad_normed * normed, axis=-1, keepdims=True)
+    return inv_scale * (grad_normed - first - normed * second)
+
+
+def dot_nn(left, right):
+    return jnp.dot(left, right, preferred_element_type=jnp.float32)
+
+
+def dot_nt(left, right):
+    return lax.dot_general(left, right, (((1,), (1,)), ((), ())), preferred_element_type=jnp.float32)
+
+
+def dot_tn(left, right):
+    return lax.dot_general(left, right, (((0,), (0,)), ((), ())), preferred_element_type=jnp.float32)
+
+
+def fast_attend(triple, key_bias):
+    score_scale = HD ** (-0.5)
+    raw = jnp.einsum("qhd,khd->hqk", triple[:, :, 0], triple[:, :, 1], preferred_element_type=jnp.float32)
+    scaled = raw * score_scale + key_bias
+    peak = jnp.max(scaled, axis=-1, keepdims=True)
+    exps = jnp.exp(scaled - peak)
+    total = jnp.sum(exps, axis=-1, keepdims=True)
+    weights = (exps / total).astype(jnp.bfloat16)
+    mixed = jnp.einsum("hqk,khd->qhd", weights, triple[:, :, 2], preferred_element_type=jnp.float32)
+    return mixed.astype(jnp.bfloat16), peak + jnp.log(total)
+
+
+def fast_attend_back(triple, log_total, grad_mixed, key_bias):
+    score_scale = HD ** (-0.5)
+    query, key, value = triple[:, :, 0], triple[:, :, 1], triple[:, :, 2]
+    raw = jnp.einsum("qhd,khd->hqk", query, key, preferred_element_type=jnp.float32)
+    weights = jnp.exp(raw * score_scale + key_bias - log_total)
+    grad_value = jnp.einsum(
+        "hqk,qhd->khd", weights.astype(jnp.bfloat16), grad_mixed, preferred_element_type=jnp.float32
+    )
+    grad_soft = jnp.einsum("qhd,khd->hqk", grad_mixed, value, preferred_element_type=jnp.float32)
+    inner = jnp.sum(grad_soft * weights, axis=-1, keepdims=True)
+    grad_raw = (score_scale * weights * (grad_soft - inner)).astype(jnp.bfloat16)
+    grad_query = jnp.einsum("hqk,khd->qhd", grad_raw, key, preferred_element_type=jnp.float32)
+    grad_key = jnp.einsum("hqk,qhd->khd", grad_raw, query, preferred_element_type=jnp.float32)
+    return jnp.stack([grad_query, grad_key, grad_value], axis=2).astype(jnp.bfloat16)
+
+
+def on_chip(
+    layer_input,
+    teacher,
+    valid,
+    proj_in,
+    bias_query,
+    bias_value,
+    proj_out,
+    bias_out,
+    norm1_gain,
+    norm1_shift,
+    norm2_gain,
+    norm2_shift,
+    w_up,
+    bias_up,
+    w_down,
+    bias_down,
+):
+    core = lax.axis_index("dp")
+    row = lax.axis_index("row")
+    cols = lax.axis_size("col")
+    feat = layer_input.shape[1]
+    images = layer_input.shape[0] // SEQ
+    half_seq = (SEQ + 31) // 32 * 16
+    pad_seq = 2 * half_seq
+    units = w_up.shape[1] // 2
+    width = proj_out.shape[0] // 2
+    heads = width // HD
+
+    def core_half(values, axis):
+        size = values.shape[axis] // 2
+        return lax.dynamic_slice_in_dim(values, core * size, size, axis)
+
+    def to_chip(values):
+        imgs = jnp.pad(values.reshape(images, SEQ, -1), ((0, 0), (0, pad_seq - SEQ), (0, 0)))
+        imgs = imgs.reshape(images, 2, half_seq, -1)
+        keep = lax.dynamic_index_in_dim(imgs, core, 1, False)
+        give = lax.dynamic_index_in_dim(imgs, 1 - core, 1, False)
+        got = pair_swap(give)
+        first = core == 0
+        every = jnp.concatenate([jnp.where(first, keep, got), jnp.where(first, got, keep)], axis=0)
+        parts = []
+        for k in range(4):
+            part = lax.dynamic_index_in_dim(every, row ^ k, 0, False)
+            parts.append(row_swap(part, k) if k else part)
+        return jnp.concatenate(parts, axis=1)
+
+    def from_chip(values):
+        parts = []
+        for k in range(4):
+            part = values[:, k * feat : (k + 1) * feat]
+            parts.append(row_swap(part, k) if k else part)
+        stacked = jnp.stack(parts)
+        every = jnp.stack([lax.dynamic_index_in_dim(stacked, row ^ i, 0, False) for i in range(4)])
+        every = every.reshape(2, images, half_seq, feat)
+        mine = lax.dynamic_index_in_dim(every, core, 0, False)
+        got = pair_swap(lax.dynamic_index_in_dim(every, 1 - core, 0, False))
+        first = core == 0
+        both = jnp.stack([jnp.where(first, mine, got), jnp.where(first, got, mine)], axis=1)
+        return both.reshape(images, pad_seq, feat)[:, :SEQ].reshape(images * SEQ, feat)
+
+    attn_shard = jnp.concatenate([core_half(proj_in, 1), core_half(proj_out, 0).T], axis=1)
+    ff_shard = jnp.concatenate([core_half(w_up, 1), core_half(w_down, 0).T], axis=1)
+    features = jnp.stack([norm1_gain, norm1_shift, norm2_gain, norm2_shift, bias_out, bias_down])
+    features = jnp.concatenate([features] + [row_swap(features, k) for k in (1, 2, 3)], axis=1)
+    features = features.astype(jnp.float32)
+    gain1, shift1, gain2, shift2, bias_out_all, bias_down_all = (features[i : i + 1] for i in range(6))
+    col_biases = gather_ring(
+        jnp.concatenate([core_half(bias_query, 0), core_half(bias_value, 0), core_half(bias_up, 0)])[None]
+    )
+
+    x_half = to_chip(layer_input).astype(jnp.float32)
+    attn_weights = [gather_plane(block) for block in gather_ring(attn_shard)]
+    ff_weights = [gather_plane(block) for block in gather_ring(ff_shard)]
+    teacher_half = to_chip(teacher).astype(jnp.float32)
+    count = lax.psum(jnp.sum(valid.astype(jnp.float32)), ("dp", "col"))
+    valid_imgs = jnp.pad(valid.reshape(images, SEQ), ((0, 0), (0, pad_seq - SEQ)))
+    other_valid = pair_swap(valid_imgs)
+    from_here = (row // images) == core
+    chip_valid = lax.dynamic_index_in_dim(
+        jnp.where(from_here, valid_imgs, other_valid), lax.rem(row, images), 0, False
+    )
+    mask_half = lax.dynamic_slice_in_dim(chip_valid, core * half_seq, half_seq, 0)
+    mask_half = mask_half.astype(jnp.float32)[:, None]
+
+    place = jnp.arange(pad_seq)
+    token = jnp.where(place < half_seq, place + core * half_seq, place - core * half_seq)
+    key_bias = jnp.where(token < SEQ, 0.0, -1e30).astype(jnp.float32)
+
+    def both_cores(values):
+        return jnp.concatenate([values, pair_swap(values)], axis=0)
+
+    def sum_cores(values):
+        return values[:half_seq] + pair_swap(values[half_seq:])
+
+    normed1, scale1 = layer_norm(x_half)
+    norm1_all = both_cores((normed1 * gain1 + shift1).astype(jnp.bfloat16))
+    triples, log_totals, mixes = [], [], []
+    attn_part = 0.0
+    for s in range(cols):
+        weight = attn_weights[s]
+        triple = dot_nn(norm1_all, weight[:, : 3 * width]).reshape(pad_seq, heads, 3, HD)
+        bias = col_biases[s][0].astype(jnp.float32)
+        bias_shift = jnp.stack(
+            [
+                bias[:width].reshape(heads, HD),
+                jnp.zeros((heads, HD), jnp.float32),
+                bias[width : 2 * width].reshape(heads, HD),
+            ],
+            axis=1,
+        )
+        triple = (triple + bias_shift).astype(jnp.bfloat16)
+        mixed, log_total = fast_attend(triple, key_bias)
+        mixed = mixed.reshape(pad_seq, width)
+        attn_part = attn_part + dot_nt(mixed, weight[:, 3 * width :])
+        triples.append(triple)
+        log_totals.append(log_total)
+        mixes.append(mixed)
+    resid1 = x_half + sum_cores(attn_part) + bias_out_all
+    normed2, scale2 = layer_norm(resid1)
+    norm2_all = both_cores((normed2 * gain2 + shift2).astype(jnp.bfloat16))
+    pres, acts = [], []
+    down_part = 0.0
+    for s in range(cols):
+        weight = ff_weights[s]
+        pre = dot_nn(norm2_all, weight[:, :units]) + col_biases[s][:, 2 * width :].astype(jnp.float32)
+        act = jax.nn.gelu(pre, approximate=True).astype(jnp.bfloat16)
+        down_part = down_part + dot_nt(act, weight[:, units:])
+        pres.append(pre)
+        acts.append(act)
+    result = resid1 + sum_cores(down_part) + bias_down_all
+    layer_output = from_chip(result.astype(jnp.bfloat16))
+
+    error = result - teacher_half
+    err_part = jnp.sum(mask_half * error * error)
+    tokens_all = layer_input.shape[0] * lax.axis_size("dp") * cols
+    factor = tokens_all / (2.0 * count)
+    grad_result = 2.0 * error * (mask_half * factor)
+    branch2 = grad_result.astype(jnp.bfloat16)
+    branch2_all = both_cores(branch2)
+    norm2_part = 0.0
+    ff_sum, bias_sum = 0.0, 0.0
+    bias_up_sum = None
+    for s in reversed(range(cols)):
+        weight = ff_weights[s]
+        grad_act = dot_nn(branch2_all, weight[:, units:])
+        _, pull = jax.vjp(lambda entry: jax.nn.gelu(entry, approximate=True), pres[s])
+        grad_pre = pull(grad_act)[0].astype(jnp.bfloat16)
+        norm2_part = norm2_part + dot_nt(grad_pre, weight[:, :units])
+        grad_block = jnp.concatenate(
+            [dot_tn(norm2_all, grad_pre), dot_tn(branch2_all, acts[s])], axis=1
+        ).astype(jnp.bfloat16)
+        mine = scatter_plane(grad_block)
+        bias_mine = jnp.sum(grad_pre.astype(jnp.float32), axis=0, keepdims=True)
+        if s < cols - 1:
+            mine = mine + ring_shift(ff_sum, -1).astype(jnp.float32)
+            bias_mine = bias_mine + ring_shift(bias_up_sum, -1)
+        ff_sum = mine.astype(jnp.bfloat16)
+        bias_up_sum = bias_mine
+    grad_norm2 = sum_cores(norm2_part)
+    grad_resid1 = grad_result + layer_norm_back(grad_norm2, normed2, scale2, gain2)
+    branch1 = grad_resid1.astype(jnp.bfloat16)
+    branch1_all = both_cores(branch1)
+    norm1_part = 0.0
+    attn_sum, head_sum = 0.0, 0.0
+    for s in reversed(range(cols)):
+        weight = attn_weights[s]
+        grad_mixed = dot_nn(branch1_all, weight[:, 3 * width :]).astype(jnp.bfloat16)
+        grad_triple = fast_attend_back(
+            triples[s], log_totals[s], grad_mixed.reshape(pad_seq, heads, HD), key_bias
+        )
+        grad_float = grad_triple.astype(jnp.float32)
+        head_mine = jnp.stack(
+            [
+                jnp.sum(grad_float[:, :, 0], axis=0).reshape(width),
+                jnp.sum(grad_float[:, :, 2], axis=0).reshape(width),
+            ]
+        )
+        grad_triple = grad_triple.reshape(pad_seq, 3 * width)
+        norm1_part = norm1_part + dot_nt(grad_triple, weight[:, : 3 * width])
+        grad_block = jnp.concatenate(
+            [dot_tn(norm1_all, grad_triple), dot_tn(branch1_all, mixes[s])], axis=1
+        ).astype(jnp.bfloat16)
+        mine = scatter_plane(grad_block)
+        if s < cols - 1:
+            mine = mine + ring_shift(attn_sum, -1).astype(jnp.float32)
+            head_mine = head_mine + ring_shift(head_sum, -1)
+        attn_sum = mine.astype(jnp.bfloat16)
+        head_sum = head_mine
+    grad_norm1 = sum_cores(norm1_part)
+    grad_in = grad_resid1 + layer_norm_back(grad_norm1, normed1, scale1, gain1)
+    grad_input = from_chip(grad_in.astype(jnp.bfloat16)).astype(jnp.float32)
+
+    terms = jnp.stack(
+        [
+            jnp.sum(grad_norm1 * normed1, axis=0),
+            jnp.sum(grad_norm1, axis=0),
+            jnp.sum(grad_norm2 * normed2, axis=0),
+            jnp.sum(grad_norm2, axis=0),
+            jnp.sum(branch1.astype(jnp.float32), axis=0),
+            jnp.sum(branch2.astype(jnp.float32), axis=0),
+        ]
+    )
+    near = terms[:, : 2 * feat] + row_swap(terms[:, 2 * feat :], 2)
+    terms = near[:, :feat] + row_swap(near[:, feat:], 1)
+
+    def plane_sum(values):
+        values = values + row_swap(values, 1)
+        return values + row_swap(values, 2)
+
+    err_plane = plane_sum(err_part.reshape(1, 1))
+    sums = jnp.concatenate([terms, jnp.broadcast_to(err_plane, (1, feat))], axis=0)
+    for bit in (1, 2):
+        sums = sums + lax.ppermute(sums, "col", [(i, i ^ bit) for i in range(cols)])
+    sums = sums + pair_swap(sums)
+    loss_value = sums[6, 0] / (count * D)
+
+    def both_halves(values):
+        got = pair_swap(values)
+        first = core == 0
+        return jnp.concatenate(
+            [jnp.where(first, values, got), jnp.where(first, got, values)], axis=-1
+        )
+
+    unit_mine = both_halves(plane_sum(bias_up_sum))[0]
+    head_mine = both_halves(plane_sum(head_sum))
+
+    def weight_rows(total):
+        size = feat // 2
+        keep = lax.dynamic_slice_in_dim(total, core * size, size, 0)
+        give = lax.dynamic_slice_in_dim(total, (1 - core) * size, size, 0)
+        return keep, pair_swap(give)
+
+    def joined(keep, got, axis):
+        first = core == 0
+        return jnp.concatenate(
+            [jnp.where(first, keep, got), jnp.where(first, got, keep)], axis=axis
+        ).astype(jnp.float32)
+
+    ff_keep, ff_got = weight_rows(ff_sum)
+    attn_keep, attn_got = weight_rows(attn_sum)
+    grad_w_up = joined(ff_keep[:, :units], ff_got[:, :units], 1)
+    grad_w_down = joined(ff_keep[:, units:].T, ff_got[:, units:].T, 0)
+    grad_proj_in = joined(attn_keep[:, : 3 * width], attn_got[:, : 3 * width], 1)
+    grad_proj_out = joined(attn_keep[:, 3 * width :].T, attn_got[:, 3 * width :].T, 0)
+    return (
+        layer_output,
+        loss_value,
+        grad_input,
+        grad_proj_in[None],
+        head_mine[0],
+        head_mine[1],
+        grad_proj_out[:, None],
+        sums[4],
+        sums[0],
+        sums[1],
+        sums[2],
+        sums[3],
+        grad_w_up[None],
+        unit_mine,
+        grad_w_down[:, None],
+        sums[5],
+    )
+
+
+def one_image_a_chip(mesh, tokens):
+    sizes = mesh.shape
+    pairs = sizes["dp"] == 2 and sizes["row"] == 4 and sizes["col"] == 4
+    return pairs and tokens == SEQ * sizes["row"] * sizes["col"]
+
+
 def solution(mesh):
     placed = (
         P(("dp", "col"), "row"),
@@ -318,11 +696,7 @@
         P("col", "row"),
         P("row"),
     )
-    return jax.shard_map(
-        on_device,
-        mesh=mesh,
-        in_specs=placed,
-        out_specs=(
+    returned = (
             P(("dp", "col"), "row"),
             P(),
             P(("dp", "col"), "row"),
@@ -339,6 +713,12 @@
             P("col"),
             P("col", "row", "dp"),
             P("row"),
-        ),
-        check_vma=False,
-    )
+        )
+
+    def whole(layer_input, *others):
+        body = on_chip if one_image_a_chip(mesh, layer_input.shape[0]) else on_device
+        return jax.shard_map(
+            body, mesh=mesh, in_specs=placed, out_specs=returned, check_vma=False
+        )(layer_input, *others)
+
+    return whole

time: 3450 us -> 668 us (0.19)
  waiting for transfers between devices: 2220 us -> 241 us
  blocking collectives: 600 us -> 16.6 us
  local copies, waits for them, and re-layouts: 332 us -> 85.3 us
  starting transfers between devices: 4.27 us -> 140 us
  matrix products: 164 us -> 107 us
  other arithmetic: 98.6 us -> 59 us
    unnamed x25 -> x0, waiting for transfers between devices: 1560 us -> none
    all_gather x8 -> x0, waiting for transfers between devices: 652 us -> none  [the longest x2 203 us: first_section_back(): grad_all = lax.all_gather(grad_quarter, 'row', axis=0, tiled=True)]
    unnamed x2 -> x0, blocking collectives: 448 us -> none
    ppermute x0 -> x144, waiting for transfers between devices: none -> 241 us  [the longest x103 213 us: row_swap(): lax.ppermute(values, 'row', [(i, i ^ bit) for i in range(lax.axis_size('r...]
    ppermute x0 -> x144, starting transfers between devices: none -> 140 us  [the longest x103 110 us: row_swap(): lax.ppermute(values, 'row', [(i, i ^ bit) for i in range(lax.axis_size('r...]
    psum x6 -> x1, blocking collectives: 151 us -> 16.6 us  [on_chip(): count = lax.psum(jnp.sum(valid.astype(jnp.float32)), ('dp', 'col'))]
    unnamed x82 -> x318, local copies, waits for them, and re-layouts: 163 us -> 30.9 us
    all_gather x7 -> x0, local copies, waits for them, and re-layouts: 117 us -> none  [the longest x2 48.7 us: second_section(): gathered = lax.all_gather(quarter_rows, 'row', axis=0, tiled=True)]
  transfers between devices with their start and end apart: 19 -> 144, of which waited for: 15 -> 62; matrix products, arithmetic and copies ran while one was open for 3% -> 22% of each run, Pallas kernels for 0% -> 0%
where the time goes in v1:
time: 668 us; the launch traced here: 658 us
  waiting for transfers between devices  241 us (36%)
  starting transfers between devices  140 us (21%)
  matrix products  107 us (16%)
  local copies, waits for them, and re-layouts  85.3 us (13%)
  other arithmetic  59 us (9%)
  blocking collectives  16.6 us (2%)
  between operations  9.48 us (1%)
    ppermute x103, waiting for transfers between devices, row_swap(): lax.ppermute(values, 'row', [(i, i ^ bit) for i in range(lax.axis_size('r...  213 us
    ppermute x103, starting transfers between devices, row_swap(): lax.ppermute(values, 'row', [(i, i ^ bit) for i in range(lax.axis_size('r...  110 us
    dot_general x16, matrix products, dot_nt(): lax.dot_general(left, right, (((1,), (1,)), ((), ())), preferred_element_...  36.2 us
    unnamed x318, local copies, waits for them, and re-layouts  30.9 us
    dot_general x16, matrix products, dot_nn(): return jnp.dot(left, right, preferred_element_type=jnp.float32)  27.4 us
    ppermute x21, starting transfers between devices, ring_shift(): lax.ppermute(values, 'col', [(order[i], order[(i + step) % size]) for i i...  25 us
    ppermute x21, waiting for transfers between devices, ring_shift(): lax.ppermute(values, 'col', [(order[i], order[(i + step) % size]) for i i...  24.6 us
    dot_general x16, matrix products, dot_tn(): lax.dot_general(left, right, (((0,), (0,)), ((), ())), preferred_element_...  23.6 us
  transfers between devices with their start and end apart: 144, of which 62 were waited for; matrix products, arithmetic and copies ran while one was open for 22% of the time, Pallas kernels for 0%

profile of v1, /device:TPU:0, one launch (start us, length us, event | category | flops | bytes accessed | tf_op | source)
XLA Modules:
  0.0 658.0 jit_solution(11988579948240505588)
XLA Ops:
  4.9 3.0 collective-permute-start.4
  12.7 3.0 collective-permute-start.12
  32.1 2.9 collective-permute-start.29
  38.5 3.2 collective-permute-start.36
  51.2 6.5 collective-permute-done.10
  57.7 2.9 collective-permute-start.18
  74.2 5.7 collective-permute-done.1
  87.4 4.2 collective-permute-done.14
  94.3 5.8 collective-permute-done.15
  105.0 7.3 %collective-permute-done.19 = bf16[288,576]{1,0:T(8,128)(2,1)S(1)} collective-permute-done((bf16[288,576]{1,0:T(8,128)(2,1)S(1)}, bf16[288,576]{1,0:T(8,128)(2,1)S(1)}, u32[]{:S(2)}, u32[]{:S(2)}) %collective-permute-start.19) | collective-permute-done | bytes 331808 | tf_op jit(solution)/shard_map/ppermute | solution.py:307
  117.1 11.3 %collective-permute-done.21 = bf16[144,576]{1,0:T(8,128)(2,1)S(1)} collective-permute-done((bf16[144,576]{1,0:T(8,128)(2,1)S(1)}, bf16[144,576]{1,0:T(8,128)(2,1)S(1)}, u32[]{:S(2)}, u32[]{:S(2)}) %collective-permute-start.21) | collective-permute-done | bytes 165920 | tf_op jit(solution)/shard_map/ppermute | solution.py:307
  133.2 6.8 %collective-permute-done.25 = bf16[288,576]{1,0:T(8,128)(2,1)S(1)} collective-permute-done((bf16[288,576]{1,0:T(8,128)(2,1)S(1)}, bf16[288,576]{1,0:T(8,128)(2,1)S(1)}, u32[]{:S(2)}, u32[]{:S(2)}) %collective-permute-start.25) | collective-permute-done | bytes 331808 | tf_op jit(solution)/shard_map/ppermute | solution.py:307
  171.7 5.1 collective-permute-done.42
  182.7 5.0 collective-permute-done.44
  187.7 2.5 collective-permute-done.45
  190.3 9.2 %collective-permute-done.47 = bf16[288,1076]{1,0:T(8,128)(2,1)S(1)} collective-permute-done((bf16[288,1076]{1,0:T(8,128)(2,1)S(1)}, bf16[288,1076]{1,0:T(8,128)(2,1)S(1)}, u32[]{:S(2)}, u32[]{:S(2)}) %collective-permute-start.47) | collective-permute-done | bytes 619808 | tf_op jit(solution)/shard_map/ppermute | solution.py:307
  203.9 2.8 collective-permute-done.49
  210.4 2.5 fusion.88
  214.5 2.5 fusion.97
  223.5 2.7 fusion.8
  229.3 3.3 reshape.373
  233.6 2.6 reshape.374
  236.3 2.7 constant_dynamic-slice_fusion.9
  241.1 16.6 %psum.7 = f32[]{:T(128)} all-reduce(f32[]{:T(128)} %convert_reduce_fusion.7), channel_id=1, replica_groups=mesh['dp'=2,'row'=4,'col'=4] {'dp','col'}, use_global_device_ids=true, to_apply=%region_13.14 | all-reduce | flops 1 | bytes 8 | tf_op jit(solution)/shard_map/psum | solution.py:484
  266.6 5.0 collective-permute-done.57
  271.6 6.4 collective-permute-done.58
  279.9 3.5 fusion.48
  294.0 3.0 convert_reduce_fusion.6
  299.2 3.0 convert_reduce_fusion.5
  304.4 3.2 convert_reduce_fusion.4
  321.1 3.4 convert_reduce_fusion.3
  326.4 3.3 convolution_convert_fusion.2
  336.1 2.8 collective-permute-done.140
  352.9 5.5 collective-permute-done.120
  359.3 11.8 %collective-permute-done.128 = bf16[144,1076]{1,0:T(8,128)(2,1)S(1)} collective-permute-done((bf16[144,1076]{1,0:T(8,128)(2,1)S(1)}, bf16[144,1076]{1,0:T(8,128)(2,1)S(1)}, u32[]{:S(2)}, u32[]{:S(2)}) %collective-permute-start.128) | collective-permute-done | bytes 309920 | tf_op jit(solution)/shard_map/ppermute | solution.py:307
  375.9 6.0 collective-permute-done.130
  383.9 6.2 collective-permute-done.129
  392.0 5.1 collective-permute-done.119
  399.2 5.1 collective-permute-done.117
  405.6 5.8 collective-permute-done.125
  412.3 4.6 collective-permute-done.123
  424.3 11.6 %collective-permute-done.135 = bf16[288,1076]{1,0:T(8,128)(2,1)S(1)} collective-permute-done((bf16[288,1076]{1,0:T(8,128)(2,1)S(1)}, bf16[288,1076]{1,0:T(8,128)(2,1)S(1)}, u32[]{:S(2)}, u32[]{:S(2)}) %collective-permute-start.135) | collective-permute-done | bytes 619808 | tf_op jit(solution)/shard_map/ppermute | solution.py:317
  440.3 4.7 collective-permute-done.54
  445.0 2.9 collective-permute-done.53
  449.2 3.9 collective-permute-done.136
  480.2 3.0 fusion.151
  484.5 3.0 fusion.147
  488.8 3.0 fusion.143
  508.4 5.9 fusion.11
  525.2 2.6 convolution_convert_fusion.8
  538.0 5.8 collective-permute-done.94
  544.6 4.2 collective-permute-done.98
  554.4 4.3 collective-permute-done.97
  559.5 5.5 collective-permute-done.95
  568.5 2.8 collective-permute-done.86
  573.4 4.3 collective-permute-done.91
  578.5 4.2 collective-permute-done.89
  587.3 5.4 collective-permute-done.85
  593.5 3.3 collective-permute-done.83
  602.1 4.6 collective-permute-done.79
  606.7 3.2 collective-permute-done.77
  616.5 2.6 collective-permute-done.65
  634.1 3.0 collective-permute-done.73
  653.7 2.7 reshape.387
  (876 shorter events, 348.4 us)
Async XLA Ops:
  4.9 25.6 %collective-permute-start.4 = (bf16[6,288]{1,0:T(8,128)(2,1)S(1)}, bf16[6,288]{1,0:T(8,128)(2,1)S(1)}, u32[]{:S(2)}, u32[]{:S(2)}) collective-permute-start(bf16[6,288]{1,0:T(8,128)(2,1)S(1)} %stack.182), channel_id=1, source_target_pairs={{0,4},{4,0},{8,12},{12,8},{1,5},{5,1},{9,13},{13,9},{2,6},{6,2},{1... | collective-permute-start | bytes 10376 | tf_op jit(solution)/shard_map/ppermute | solution.py:307
  7.9 24.1 %collective-permute-start.5 = (bf16[6,288]{1,0:T(8,128)(2,1)S(1)}, bf16[6,288]{1,0:T(8,128)(2,1)S(1)}, u32[]{:S(2)}, u32[]{:S(2)}) collective-permute-start(bf16[6,288]{1,0:T(8,128)(2,1)S(1)} %stack.182), channel_id=1, source_target_pairs={{0,8},{4,12},{8,0},{12,4},{1,9},{5,13},{9,1},{13,5},{2,10},{6,14},... | collective-permute-start | bytes 10376 | tf_op jit(solution)/shard_map/ppermute | solution.py:307
  9.5 22.6 %collective-permute-start.6 = (bf16[6,288]{1,0:T(8,128)(2,1)S(1)}, bf16[6,288]{1,0:T(8,128)(2,1)S(1)}, u32[]{:S(2)}, u32[]{:S(2)}) collective-permute-start(bf16[6,288]{1,0:T(8,128)(2,1)S(1)} %stack.182), channel_id=1, source_target_pairs={{0,12},{4,8},{8,4},{12,0},{1,13},{5,9},{9,5},{13,1},{2,14},{6,10},... | collective-permute-start | bytes 10376 | tf_op jit(solution)/shard_map/ppermute | solution.py:307
  12.7 29.1 %collective-permute-start.12 = (bf16[288,576]{1,0:T(8,128)(2,1)}, bf16[288,576]{1,0:T(8,128)(2,1)}, u32[]{:S(2)}, u32[]{:S(2)}) collective-permute-start(bf16[288,576]{1,0:T(8,128)(2,1)} %get-tuple-element.186), channel_id=1, source_target_pairs={{0,2},{2,3},{3,1},{1,0},{4,6},{6,7},{7,5},{5,4},{8,10},{10,11},{11... | collective-permute-start | bytes 995336 | tf_op jit(solution)/shard_map/ppermute | solution.py:317
  32.0 14.6 %collective-permute-start = (bf16[2,368,288]{1,2,0:T(8,128)(2,1)}, bf16[2,368,288]{1,2,0:T(8,128)(2,1)}, u32[]{:S(2)}, u32[]{:S(2)}) collective-permute-start(bf16[2,368,288]{1,2,0:T(8,128)(2,1)} %bitcast.289), channel_id=1, source_target_pairs={{0,16},{16,0},{1,17},{17,1},{2,18},{18,2},{3,19},{19,3},{4,20},{20... | collective-permute-start | bytes 1271816 | tf_op jit(solution)/shard_map/ppermute | solution.py:303
  36.3 29.1 %collective-permute-start.32 = (bf16[288,1076]{1,0:T(8,128)(2,1)}, bf16[288,1076]{1,0:T(8,128)(2,1)S(1)}, u32[]{:S(2)}, u32[]{:S(2)}) collective-permute-start(bf16[288,1076]{1,0:T(8,128)(2,1)} %get-tuple-element.182), channel_id=1, source_target_pairs={{0,4},{4,0},{8,12},{12,8},{1,5},{5,1},{9,13},{13,9},{2,6},{6,2},{1... | collective-permute-start | bytes 1859336 | tf_op jit(solution)/shard_map/ppermute | solution.py:307
  37.3 29.4 %collective-permute-start.33 = (bf16[288,1076]{1,0:T(8,128)(2,1)}, bf16[288,1076]{1,0:T(8,128)(2,1)S(1)}, u32[]{:S(2)}, u32[]{:S(2)}) collective-permute-start(bf16[288,1076]{1,0:T(8,128)(2,1)} %get-tuple-element.182), channel_id=1, source_target_pairs={{0,8},{4,12},{8,0},{12,4},{1,9},{5,13},{9,1},{13,5},{2,10},{6,14},... | collective-permute-start | bytes 1859336 | tf_op jit(solution)/shard_map/ppermute | solution.py:307
  38.5 31.2 %collective-permute-start.36 = (bf16[288,1076]{1,0:T(8,128)(2,1)}, bf16[288,1076]{1,0:T(8,128)(2,1)}, u32[]{:S(2)}, u32[]{:S(2)}) collective-permute-start(bf16[288,1076]{1,0:T(8,128)(2,1)} %get-tuple-element.182), channel_id=1, source_target_pairs={{0,2},{2,3},{3,1},{1,0},{4,6},{6,7},{7,5},{5,4},{8,10},{10,11},{11... | collective-permute-start | bytes 1859336 | tf_op jit(solution)/shard_map/ppermute | solution.py:317
  41.7 16.0 %collective-permute-start.10 = (bf16[144,576]{1,0:T(8,128)(2,1)}, bf16[144,576]{1,0:T(8,128)(2,1)}, u32[]{:S(2)}, u32[]{:S(2)}) collective-permute-start(bf16[144,576]{1,0:T(8,128)(2,1)} %slice.728), channel_id=1, source_target_pairs={{0,8},{4,12},{8,0},{12,4},{1,9},{5,13},{9,1},{13,5},{2,10},{6,14},... | collective-permute-start | bytes 497672 | tf_op jit(solution)/shard_map/ppermute | solution.py:307
  46.6 15.6 %collective-permute-start.11 = (bf16[144,576]{1,0:T(8,128)(2,1)S(1)}, bf16[144,576]{1,0:T(8,128)(2,1)}, u32[]{:S(2)}, u32[]{:S(2)}) collective-permute-start(bf16[144,576]{1,0:T(8,128)(2,1)S(1)} %slice.729), channel_id=1, source_target_pairs={{0,4},{4,0},{8,12},{12,8},{1,5},{5,1},{9,13},{13,9},{2,6},{6,2},{1... | collective-permute-start | bytes 497672 | tf_op jit(solution)/shard_map/ppermute | solution.py:307
  57.7 34.8 %collective-permute-start.18 = (bf16[288,576]{1,0:T(8,128)(2,1)}, bf16[288,576]{1,0:T(8,128)(2,1)S(1)}, u32[]{:S(2)}, u32[]{:S(2)}) collective-permute-start(bf16[288,576]{1,0:T(8,128)(2,1)} %collective-permute-done.12), channel_id=1, source_target_pairs={{0,2},{2,3},{3,1},{1,0},{4,6},{6,7},{7,5},{5,4},{8,10},{10,11},{11... | collective-permute-start | bytes 995336 | tf_op jit(solution)/shard_map/ppermute | solution.py:317
  62.2 24.8 %collective-permute-start.13 = (bf16[288,576]{1,0:T(8,128)(2,1)}, bf16[288,576]{1,0:T(8,128)(2,1)S(1)}, u32[]{:S(2)}, u32[]{:S(2)}) collective-permute-start(bf16[288,576]{1,0:T(8,128)(2,1)} %collective-permute-done.12), channel_id=1, source_target_pairs={{0,4},{4,0},{8,12},{12,8},{1,5},{5,1},{9,13},{13,9},{2,6},{6,2},{1... | collective-permute-start | bytes 995336 | tf_op jit(solution)/shard_map/ppermute | solution.py:307
  65.4 14.5 %collective-permute-start.1 = (bf16[368,288]{1,0:T(8,128)(2,1)}, bf16[368,288]{1,0:T(8,128)(2,1)S(1)}, u32[]{:S(2)}, u32[]{:S(2)}) collective-permute-start(bf16[368,288]{1,0:T(8,128)(2,1)} %bitcast.334), channel_id=1, source_target_pairs={{0,4},{4,0},{8,12},{12,8},{1,5},{5,1},{9,13},{13,9},{2,6},{6,2},{1... | collective-permute-start | bytes 635912 | tf_op jit(solution)/shard_map/ppermute | solution.py:307
  80.4 21.9 %collective-permute-start.34 = (bf16[144,1076]{1,0:T(8,128)(2,1)}, bf16[144,1076]{1,0:T(8,128)(2,1)}, u32[]{:S(2)}, u32[]{:S(2)}) collective-permute-start(bf16[144,1076]{1,0:T(8,128)(2,1)} %slice.767), channel_id=1, source_target_pairs={{0,8},{4,12},{8,0},{12,4},{1,9},{5,13},{9,1},{13,5},{2,10},{6,14},... | collective-permute-start | bytes 929672 | tf_op jit(solution)/shard_map/ppermute | solution.py:307
  82.9 21.4 %collective-permute-start.35 = (bf16[144,1076]{1,0:T(8,128)(2,1)}, bf16[144,1076]{1,0:T(8,128)(2,1)}, u32[]{:S(2)}, u32[]{:S(2)}) collective-permute-start(bf16[144,1076]{1,0:T(8,128)(2,1)} %slice.768), channel_id=1, source_target_pairs={{0,4},{4,0},{8,12},{12,8},{1,5},{5,1},{9,13},{13,9},{2,6},{6,2},{1... | collective-permute-start | bytes 929672 | tf_op jit(solution)/shard_map/ppermute | solution.py:307
  87.1 44.3 %collective-permute-start.41 = (bf16[288,1076]{1,0:T(8,128)(2,1)}, bf16[288,1076]{1,0:T(8,128)(2,1)S(1)}, u32[]{:S(2)}, u32[]{:S(2)}) collective-permute-start(bf16[288,1076]{1,0:T(8,128)(2,1)} %collective-permute-done.36), channel_id=1, source_target_pairs={{0,2},{2,3},{3,1},{1,0},{4,6},{6,7},{7,5},{5,4},{8,10},{10,11},{11... | collective-permute-start | bytes 1859336 | tf_op jit(solution)/shard_map/ppermute | solution.py:317
  100.1 15.4 %collective-permute-start.24 = (bf16[288,576]{1,0:T(8,128)(2,1)S(1)}, bf16[288,576]{1,0:T(8,128)(2,1)S(1)}, u32[]{:S(2)}, u32[]{:S(2)}) collective-permute-start(bf16[288,576]{1,0:T(8,128)(2,1)S(1)} %collective-permute-done.18), channel_id=1, source_target_pairs={{0,2},{2,3},{3,1},{1,0},{4,6},{6,7},{7,5},{5,4},{8,10},{10,11},{11... | collective-permute-start | bytes 995336 | tf_op jit(solution)/shard_map/ppermute | solution.py:317
  104.4 24.8 %collective-permute-start.37 = (bf16[288,1076]{1,0:T(8,128)(2,1)}, bf16[288,1076]{1,0:T(8,128)(2,1)S(1)}, u32[]{:S(2)}, u32[]{:S(2)}) collective-permute-start(bf16[288,1076]{1,0:T(8,128)(2,1)} %collective-permute-done.36), channel_id=1, source_target_pairs={{0,4},{4,0},{8,12},{12,8},{1,5},{5,1},{9,13},{13,9},{2,6},{6,2},{1... | collective-permute-start | bytes 1859336 | tf_op jit(solution)/shard_map/ppermute | solution.py:307
  112.3 18.1 %collective-permute-start.38 = (bf16[288,1076]{1,0:T(8,128)(2,1)}, bf16[288,1076]{1,0:T(8,128)(2,1)S(1)}, u32[]{:S(2)}, u32[]{:S(2)}) collective-permute-start(bf16[288,1076]{1,0:T(8,128)(2,1)} %collective-permute-done.36), channel_id=1, source_target_pairs={{0,8},{4,12},{8,0},{12,4},{1,9},{5,13},{9,1},{13,5},{2,10},{6,14},... | collective-permute-start | bytes 1859336 | tf_op jit(solution)/shard_map/ppermute | solution.py:307
  130.3 41.2 %collective-permute-start.39 = (bf16[144,1076]{1,0:T(8,128)(2,1)S(1)}, bf16[144,1076]{1,0:T(8,128)(2,1)S(1)}, u32[]{:S(2)}, u32[]{:S(2)}) collective-permute-start(bf16[144,1076]{1,0:T(8,128)(2,1)S(1)} %slice.772), channel_id=1, source_target_pairs={{0,8},{4,12},{8,0},{12,4},{1,9},{5,13},{9,1},{13,5},{2,10},{6,14},... | collective-permute-start | bytes 929672 | tf_op jit(solution)/shard_map/ppermute | solution.py:307
  131.4 40.3 %collective-permute-start.40 = (bf16[144,1076]{1,0:T(8,128)(2,1)S(1)}, bf16[144,1076]{1,0:T(8,128)(2,1)S(1)}, u32[]{:S(2)}, u32[]{:S(2)}) collective-permute-start(bf16[144,1076]{1,0:T(8,128)(2,1)S(1)} %slice.773), channel_id=1, source_target_pairs={{0,4},{4,0},{8,12},{12,8},{1,5},{5,1},{9,13},{13,9},{2,6},{6,2},{1... | collective-permute-start | bytes 929672 | tf_op jit(solution)/shard_map/ppermute | solution.py:307
  139.9 39.6 %collective-permute-start.46 = (bf16[288,1076]{1,0:T(8,128)(2,1)S(1)}, bf16[288,1076]{1,0:T(8,128)(2,1)S(1)}, u32[]{:S(2)}, u32[]{:S(2)}) collective-permute-start(bf16[288,1076]{1,0:T(8,128)(2,1)S(1)} %collective-permute-done.41), channel_id=1, source_target_pairs={{0,2},{2,3},{3,1},{1,0},{4,6},{6,7},{7,5},{5,4},{8,10},{10,11},{11... | collective-permute-start | bytes 1859336 | tf_op jit(solution)/shard_map/ppermute | solution.py:317
  141.3 20.5 %collective-permute-start.27 = (bf16[144,576]{1,0:T(8,128)(2,1)S(1)}, bf16[144,576]{1,0:T(8,128)(2,1)S(1)}, u32[]{:S(2)}, u32[]{:S(2)}) collective-permute-start(bf16[144,576]{1,0:T(8,128)(2,1)S(1)} %slice.753), channel_id=1, source_target_pairs={{0,8},{4,12},{8,0},{12,4},{1,9},{5,13},{9,1},{13,5},{2,10},{6,14},... | collective-permute-start | bytes 497672 | tf_op jit(solution)/shard_map/ppermute | solution.py:307
  142.5 20.5 %collective-permute-start.28 = (bf16[144,576]{1,0:T(8,128)(2,1)S(1)}, bf16[144,576]{1,0:T(8,128)(2,1)S(1)}, u32[]{:S(2)}, u32[]{:S(2)}) collective-permute-start(bf16[144,576]{1,0:T(8,128)(2,1)S(1)} %slice.754), channel_id=1, source_target_pairs={{0,4},{4,0},{8,12},{12,8},{1,5},{5,1},{9,13},{13,9},{2,6},{6,2},{1... | collective-permute-start | bytes 497672 | tf_op jit(solution)/shard_map/ppermute | solution.py:307
  161.7 15.1 %collective-permute-start.42 = (bf16[288,1076]{1,0:T(8,128)(2,1)S(1)}, bf16[288,1076]{1,0:T(8,128)(2,1)S(1)}, u32[]{:S(2)}, u32[]{:S(2)}) collective-permute-start(bf16[288,1076]{1,0:T(8,128)(2,1)S(1)} %collective-permute-done.41), channel_id=1, source_target_pairs={{0,4},{4,0},{8,12},{12,8},{1,5},{5,1},{9,13},{13,9},{2,6},{6,2},{1... | collective-permute-start | bytes 1859336 | tf_op jit(solution)/shard_map/ppermute | solution.py:307
  163.1 16.4 %collective-permute-start.43 = (bf16[288,1076]{1,0:T(8,128)(2,1)S(1)}, bf16[288,1076]{1,0:T(8,128)(2,1)S(1)}, u32[]{:S(2)}, u32[]{:S(2)}) collective-permute-start(bf16[288,1076]{1,0:T(8,128)(2,1)S(1)} %collective-permute-done.41), channel_id=1, source_target_pairs={{0,8},{4,12},{8,0},{12,4},{1,9},{5,13},{9,1},{13,5},{2,10},{6,14},... | collective-permute-start | bytes 1859336 | tf_op jit(solution)/shard_map/ppermute | solution.py:307
  171.5 30.6 %collective-permute-start.30 = (f32[368,1152]{1,0:T(8,128)S(1)}, f32[368,1152]{1,0:T(8,128)S(1)}, u32[]{:S(2)}, u32[]{:S(2)}) collective-permute-start(f32[368,1152]{1,0:T(8,128)S(1)} %slice.763), channel_id=1, source_target_pairs={{0,16},{16,0},{1,17},{17,1},{2,18},{18,2},{3,19},{19,3},{4,20},{20... | collective-permute-start | bytes 5087240 | tf_op jit(solution)/shard_map/ppermute | solution.py:303
  179.5 19.9 %collective-permute-start.47 = (bf16[288,1076]{1,0:T(8,128)(2,1)S(1)}, bf16[288,1076]{1,0:T(8,128)(2,1)S(1)}, u32[]{:S(2)}, u32[]{:S(2)}) collective-permute-start(bf16[288,1076]{1,0:T(8,128)(2,1)S(1)} %collective-permute-done.46), channel_id=1, source_target_pairs={{0,4},{4,0},{8,12},{12,8},{1,5},{5,1},{9,13},{13,9},{2,6},{6,2},{1... | collective-permute-start | bytes 1859336 | tf_op jit(solution)/shard_map/ppermute | solution.py:307
  181.6 20.1 %collective-permute-start.48 = (bf16[288,1076]{1,0:T(8,128)(2,1)S(1)}, bf16[288,1076]{1,0:T(8,128)(2,1)S(1)}, u32[]{:S(2)}, u32[]{:S(2)}) collective-permute-start(bf16[288,1076]{1,0:T(8,128)(2,1)S(1)} %collective-permute-done.46), channel_id=1, source_target_pairs={{0,8},{4,12},{8,0},{12,4},{1,9},{5,13},{9,1},{13,5},{2,10},{6,14},... | collective-permute-start | bytes 1859336 | tf_op jit(solution)/shard_map/ppermute | solution.py:307
  229.3 50.6 %collective-permute-start.51 = (f32[368,1152]{1,0:T(8,128)}, f32[368,1152]{1,0:T(8,128)}, u32[]{:S(2)}, u32[]{:S(2)}) collective-permute-start(f32[368,1152]{1,0:T(8,128)} %slice.788), channel_id=1, source_target_pairs={{0,16},{16,0},{1,17},{17,1},{2,18},{18,2},{3,19},{19,3},{4,20},{20... | collective-permute-start | bytes 5087240 | tf_op jit(solution)/shard_map/ppermute | solution.py:303
  239.9 19.3 %collective-permute-start.56 = (bf16[2,368,288]{1,2,0:T(8,128)(2,1)}, bf16[2,368,288]{1,2,0:T(8,128)(2,1)}, u32[]{:S(2)}, u32[]{:S(2)}) collective-permute-start(bf16[2,368,288]{1,2,0:T(8,128)(2,1)} %bitcast.288), channel_id=1, source_target_pairs={{0,16},{16,0},{1,17},{17,1},{2,18},{18,2},{3,19},{19,3},{4,20},{20... | collective-permute-start | bytes 1271816 | tf_op jit(solution)/shard_map/ppermute | solution.py:303
  240.5 18.6 %collective-permute-start.60 = (s32[2,736]{1,0:T(2,128)S(1)}, s32[2,736]{1,0:T(2,128)S(1)}, u32[]{:S(2)}, u32[]{:S(2)}) collective-permute-start(s32[2,736]{1,0:T(2,128)S(1)} %pad.14), channel_id=1, source_target_pairs={{0,16},{16,0},{1,17},{17,1},{2,18},{18,2},{3,19},{19,3},{4,20},{20... | collective-permute-start | bytes 17672 | tf_op jit(solution)/shard_map/ppermute | solution.py:303
  263.2 14.9 %collective-permute-start.58 = (bf16[368,288]{1,0:T(8,128)(2,1)}, bf16[368,288]{1,0:T(8,128)(2,1)}, u32[]{:S(2)}, u32[]{:S(2)}) collective-permute-start(bf16[368,288]{1,0:T(8,128)(2,1)} %bitcast.41), channel_id=1, source_target_pairs={{0,8},{4,12},{8,0},{12,4},{1,9},{5,13},{9,1},{13,5},{2,10},{6,14},... | collective-permute-start | bytes 635912 | tf_op jit(solution)/shard_map/ppermute | solution.py:307
  313.2 35.8 %collective-permute-start.110 = (bf16[144,1076]{1,0:T(8,128)(2,1)S(1)}, bf16[144,1076]{1,0:T(8,128)(2,1)S(1)}, u32[]{:S(2)}, u32[]{:S(2)}) collective-permute-start(bf16[144,1076]{1,0:T(8,128)(2,1)S(1)} %get-tuple-element.215), channel_id=1, source_target_pairs={{0,8},{4,12},{8,0},{12,4},{1,9},{5,13},{9,1},{13,5},{2,10},{6,14},... | collective-permute-start | bytes 929672 | tf_op jit(solution)/shard_map/ppermute | solution.py:307
  314.2 35.7 %collective-permute-start.114 = (bf16[144,1076]{1,0:T(8,128)(2,1)S(1)}, bf16[144,1076]{1,0:T(8,128)(2,1)S(1)}, u32[]{:S(2)}, u32[]{:S(2)}) collective-permute-start(bf16[144,1076]{1,0:T(8,128)(2,1)S(1)} %get-tuple-element.218), channel_id=1, source_target_pairs={{0,4},{4,0},{8,12},{12,8},{1,5},{5,1},{9,13},{13,9},{2,6},{6,2},{1... | collective-permute-start | bytes 929672 | tf_op jit(solution)/shard_map/ppermute | solution.py:307
  319.7 32.0 %collective-permute-start.116 = (bf16[144,1076]{1,0:T(8,128)(2,1)S(1)}, bf16[144,1076]{1,0:T(8,128)(2,1)S(1)}, u32[]{:S(2)}, u32[]{:S(2)}) collective-permute-start(bf16[144,1076]{1,0:T(8,128)(2,1)S(1)} %get-tuple-element.207), channel_id=1, source_target_pairs={{0,8},{4,12},{8,0},{12,4},{1,9},{5,13},{9,1},{13,5},{2,10},{6,14},... | collective-permute-start | bytes 929672 | tf_op jit(solution)/shard_map/ppermute | solution.py:307
  346.6 45.3 %collective-permute-start.118 = (bf16[144,1076]{1,0:T(8,128)(2,1)S(1)}, bf16[144,1076]{1,0:T(8,128)(2,1)S(1)}, u32[]{:S(2)}, u32[]{:S(2)}) collective-permute-start(bf16[144,1076]{1,0:T(8,128)(2,1)S(1)} %get-tuple-element.208), channel_id=1, source_target_pairs={{0,8},{4,12},{8,0},{12,4},{1,9},{5,13},{9,1},{13,5},{2,10},{6,14},... | collective-permute-start | bytes 929672 | tf_op jit(solution)/shard_map/ppermute | solution.py:307
  349.0 24.0 %collective-permute-start.122 = (bf16[144,1076]{1,0:T(8,128)(2,1)S(1)}, bf16[144,1076]{1,0:T(8,128)(2,1)S(1)}, u32[]{:S(2)}, u32[]{:S(2)}) collective-permute-start(bf16[144,1076]{1,0:T(8,128)(2,1)S(1)} %get-tuple-element.199), channel_id=1, source_target_pairs={{0,8},{4,12},{8,0},{12,4},{1,9},{5,13},{9,1},{13,5},{2,10},{6,14},... | collective-permute-start | bytes 929672 | tf_op jit(solution)/shard_map/ppermute | solution.py:307
  349.9 24.7 %collective-permute-start.126 = (bf16[144,1076]{1,0:T(8,128)(2,1)S(1)}, bf16[144,1076]{1,0:T(8,128)(2,1)S(1)}, u32[]{:S(2)}, u32[]{:S(2)}) collective-permute-start(bf16[144,1076]{1,0:T(8,128)(2,1)S(1)} %get-tuple-element.202), channel_id=1, source_target_pairs={{0,4},{4,0},{8,12},{12,8},{1,5},{5,1},{9,13},{13,9},{2,6},{6,2},{1... | collective-permute-start | bytes 929672 | tf_op jit(solution)/shard_map/ppermute | solution.py:307
  351.8 19.4 %collective-permute-start.128 = (bf16[144,1076]{1,0:T(8,128)(2,1)S(1)}, bf16[144,1076]{1,0:T(8,128)(2,1)S(1)}, u32[]{:S(2)}, u32[]{:S(2)}) collective-permute-start(bf16[144,1076]{1,0:T(8,128)(2,1)S(1)} %get-tuple-element.191), channel_id=1, source_target_pairs={{0,8},{4,12},{8,0},{12,4},{1,9},{5,13},{9,1},{13,5},{2,10},{6,14},... | collective-permute-start | bytes 929672 | tf_op jit(solution)/shard_map/ppermute | solution.py:307
  373.1 16.9 %collective-permute-start.129 = (bf16[144,1076]{1,0:T(8,128)(2,1)S(1)}, bf16[144,1076]{1,0:T(8,128)(2,1)S(1)}, u32[]{:S(2)}, u32[]{:S(2)}) collective-permute-start(bf16[144,1076]{1,0:T(8,128)(2,1)S(1)} %get-tuple-element.189), channel_id=1, source_target_pairs={{0,4},{4,0},{8,12},{12,8},{1,5},{5,1},{9,13},{13,9},{2,6},{6,2},{1... | collective-permute-start | bytes 929672 | tf_op jit(solution)/shard_map/ppermute | solution.py:307
  374.6 16.0 %collective-permute-start.133 = (bf16[144,1076]{1,0:T(8,128)(2,1)S(1)}, bf16[144,1076]{1,0:T(8,128)(2,1)S(1)}, u32[]{:S(2)}, u32[]{:S(2)}) collective-permute-start(bf16[144,1076]{1,0:T(8,128)(2,1)S(1)} %get-tuple-element.190), channel_id=1, source_target_pairs={{0,8},{4,12},{8,0},{12,4},{1,9},{5,13},{9,1},{13,5},{2,10},{6,14},... | collective-permute-start | bytes 929672 | tf_op jit(solution)/shard_map/ppermute | solution.py:307
  381.8 15.3 %collective-permute-start.119 = (bf16[144,1076]{1,0:T(8,128)(2,1)S(1)}, bf16[144,1076]{1,0:T(8,128)(2,1)S(1)}, u32[]{:S(2)}, u32[]{:S(2)}) collective-permute-start(bf16[144,1076]{1,0:T(8,128)(2,1)S(1)} %get-tuple-element.209), channel_id=1, source_target_pairs={{0,4},{4,0},{8,12},{12,8},{1,5},{5,1},{9,13},{13,9},{2,6},{6,2},{1... | collective-permute-start | bytes 929672 | tf_op jit(solution)/shard_map/ppermute | solution.py:307
  382.9 14.8 %collective-permute-start.124 = (bf16[144,1076]{1,0:T(8,128)(2,1)S(1)}, bf16[144,1076]{1,0:T(8,128)(2,1)S(1)}, u32[]{:S(2)}, u32[]{:S(2)}) collective-permute-start(bf16[144,1076]{1,0:T(8,128)(2,1)S(1)} %get-tuple-element.200), channel_id=1, source_target_pairs={{0,8},{4,12},{8,0},{12,4},{1,9},{5,13},{9,1},{13,5},{2,10},{6,14},... | collective-permute-start | bytes 929672 | tf_op jit(solution)/shard_map/ppermute | solution.py:307
  390.6 14.6 %collective-permute-start.121 = (bf16[144,1076]{1,0:T(8,128)(2,1)S(1)}, bf16[144,1076]{1,0:T(8,128)(2,1)S(1)}, u32[]{:S(2)}, u32[]{:S(2)}) collective-permute-start(bf16[144,1076]{1,0:T(8,128)(2,1)S(1)} %get-tuple-element.206), channel_id=1, source_target_pairs={{0,8},{4,12},{8,0},{12,4},{1,9},{5,13},{9,1},{13,5},{2,10},{6,14},... | collective-permute-start | bytes 929672 | tf_op jit(solution)/shard_map/ppermute | solution.py:307
  391.9 28.9 %collective-permute-start.62 = (f32[368,1152]{1,0:T(8,128)S(1)}, f32[368,1152]{1,0:T(8,128)S(1)}, u32[]{:S(2)}, u32[]{:S(2)}) collective-permute-start(f32[368,1152]{1,0:T(8,128)S(1)} %slice.796), channel_id=1, source_target_pairs={{0,16},{16,0},{1,17},{17,1},{2,18},{18,2},{3,19},{19,3},{4,20},{20... | collective-permute-start | bytes 5087240 | tf_op jit(solution)/shard_map/ppermute | solution.py:303
  397.7 19.1 %collective-permute-start.123 = (bf16[144,1076]{1,0:T(8,128)(2,1)S(1)}, bf16[144,1076]{1,0:T(8,128)(2,1)S(1)}, u32[]{:S(2)}, u32[]{:S(2)}) collective-permute-start(bf16[144,1076]{1,0:T(8,128)(2,1)S(1)} %get-tuple-element.197), channel_id=1, source_target_pairs={{0,4},{4,0},{8,12},{12,8},{1,5},{5,1},{9,13},{13,9},{2,6},{6,2},{1... | collective-permute-start | bytes 929672 | tf_op jit(solution)/shard_map/ppermute | solution.py:307
  411.4 25.8 %collective-permute-start.112 = (bf16[144,1076]{1,0:T(8,128)(2,1)S(1)}, bf16[144,1076]{1,0:T(8,128)(2,1)S(1)}, u32[]{:S(2)}, u32[]{:S(2)}) collective-permute-start(bf16[144,1076]{1,0:T(8,128)(2,1)S(1)} %get-tuple-element.216), channel_id=1, source_target_pairs={{0,8},{4,12},{8,0},{12,4},{1,9},{5,13},{9,1},{13,5},{2,10},{6,14},... | collective-permute-start | bytes 929672 | tf_op jit(solution)/shard_map/ppermute | solution.py:307
  416.9 21.3 %collective-permute-start.113 = (bf16[144,1076]{1,0:T(8,128)(2,1)S(1)}, bf16[144,1076]{1,0:T(8,128)(2,1)S(1)}, u32[]{:S(2)}, u32[]{:S(2)}) collective-permute-start(bf16[144,1076]{1,0:T(8,128)(2,1)S(1)} %get-tuple-element.217), channel_id=1, source_target_pairs={{0,4},{4,0},{8,12},{12,8},{1,5},{5,1},{9,13},{13,9},{2,6},{6,2},{1... | collective-permute-start | bytes 929672 | tf_op jit(solution)/shard_map/ppermute | solution.py:307
  417.5 22.2 %collective-permute-start.111 = (bf16[144,1076]{1,0:T(8,128)(2,1)S(1)}, bf16[144,1076]{1,0:T(8,128)(2,1)S(1)}, u32[]{:S(2)}, u32[]{:S(2)}) collective-permute-start(bf16[144,1076]{1,0:T(8,128)(2,1)S(1)} %get-tuple-element.213), channel_id=1, source_target_pairs={{0,4},{4,0},{8,12},{12,8},{1,5},{5,1},{9,13},{13,9},{2,6},{6,2},{1... | collective-permute-start | bytes 929672 | tf_op jit(solution)/shard_map/ppermute | solution.py:307
  419.6 20.3 %collective-permute-start.115 = (bf16[144,1076]{1,0:T(8,128)(2,1)S(1)}, bf16[144,1076]{1,0:T(8,128)(2,1)S(1)}, u32[]{:S(2)}, u32[]{:S(2)}) collective-permute-start(bf16[144,1076]{1,0:T(8,128)(2,1)S(1)} %get-tuple-element.214), channel_id=1, source_target_pairs={{0,8},{4,12},{8,0},{12,4},{1,9},{5,13},{9,1},{13,5},{2,10},{6,14},... | collective-permute-start | bytes 929672 | tf_op jit(solution)/shard_map/ppermute | solution.py:307
  420.8 15.1 %collective-permute-start.135 = (bf16[288,1076]{1,0:T(8,128)(2,1)S(1)}, bf16[288,1076]{1,0:T(8,128)(2,1)S(1)}, u32[]{:S(2)}, u32[]{:S(2)}) collective-permute-start(bf16[288,1076]{1,0:T(8,128)(2,1)S(1)} %fusion.81), channel_id=1, source_target_pairs={{0,1},{2,0},{3,2},{1,3},{4,5},{6,4},{7,6},{5,7},{8,9},{10,8},{11,1... | collective-permute-start | bytes 1859336 | tf_op jit(solution)/shard_map/ppermute | solution.py:317
  497.0 37.7 %collective-permute-start.76 = (bf16[144,576]{0,1:T(8,128)(2,1)}, bf16[144,576]{0,1:T(8,128)(2,1)}, u32[]{:S(2)}, u32[]{:S(2)}) collective-permute-start(bf16[144,576]{0,1:T(8,128)(2,1)} %get-tuple-element.248), channel_id=1, source_target_pairs={{0,8},{4,12},{8,0},{12,4},{1,9},{5,13},{9,1},{13,5},{2,10},{6,14},... | collective-permute-start | bytes 497672 | tf_op jit(solution)/shard_map/ppermute | solution.py:307
  498.2 37.3 %collective-permute-start.80 = (bf16[144,576]{0,1:T(8,128)(2,1)}, bf16[144,576]{0,1:T(8,128)(2,1)}, u32[]{:S(2)}, u32[]{:S(2)}) collective-permute-start(bf16[144,576]{0,1:T(8,128)(2,1)} %get-tuple-element.251), channel_id=1, source_target_pairs={{0,4},{4,0},{8,12},{12,8},{1,5},{5,1},{9,13},{13,9},{2,6},{6,2},{1... | collective-permute-start | bytes 497672 | tf_op jit(solution)/shard_map/ppermute | solution.py:307
  502.4 65.2 %collective-permute-start.82 = (bf16[144,576]{0,1:T(8,128)(2,1)}, bf16[144,576]{0,1:T(8,128)(2,1)}, u32[]{:S(2)}, u32[]{:S(2)}) collective-permute-start(bf16[144,576]{0,1:T(8,128)(2,1)} %get-tuple-element.240), channel_id=1, source_target_pairs={{0,8},{4,12},{8,0},{12,4},{1,9},{5,13},{9,1},{13,5},{2,10},{6,14},... | collective-permute-start | bytes 497672 | tf_op jit(solution)/shard_map/ppermute | solution.py:307
  506.6 43.5 %collective-permute-start.88 = (bf16[144,576]{0,1:T(8,128)(2,1)}, bf16[144,576]{0,1:T(8,128)(2,1)}, u32[]{:S(2)}, u32[]{:S(2)}) collective-permute-start(bf16[144,576]{0,1:T(8,128)(2,1)} %get-tuple-element.232), channel_id=1, source_target_pairs={{0,8},{4,12},{8,0},{12,4},{1,9},{5,13},{9,1},{13,5},{2,10},{6,14},... | collective-permute-start | bytes 497672 | tf_op jit(solution)/shard_map/ppermute | solution.py:307
  533.0 18.2 %collective-permute-start.92 = (bf16[144,576]{0,1:T(8,128)(2,1)S(1)}, bf16[144,576]{0,1:T(8,128)(2,1)S(1)}, u32[]{:S(2)}, u32[]{:S(2)}) collective-permute-start(bf16[144,576]{0,1:T(8,128)(2,1)S(1)} %copy-done.65), channel_id=1, source_target_pairs={{0,4},{4,0},{8,12},{12,8},{1,5},{5,1},{9,13},{13,9},{2,6},{6,2},{1... | collective-permute-start | bytes 497672 | tf_op jit(solution)/shard_map/ppermute | solution.py:307
  550.1 14.9 %collective-permute-start.95 = (bf16[144,576]{0,1:T(8,128)(2,1)S(1)}, bf16[144,576]{0,1:T(8,128)(2,1)S(1)}, u32[]{:S(2)}, u32[]{:S(2)}) collective-permute-start(bf16[144,576]{0,1:T(8,128)(2,1)S(1)} %get-tuple-element.222), channel_id=1, source_target_pairs={{0,4},{4,0},{8,12},{12,8},{1,5},{5,1},{9,13},{13,9},{2,6},{6,2},{1... | collective-permute-start | bytes 497672 | tf_op jit(solution)/shard_map/ppermute | solution.py:307
  551.3 14.7 %collective-permute-start.99 = (bf16[144,576]{0,1:T(8,128)(2,1)S(1)}, bf16[144,576]{0,1:T(8,128)(2,1)S(1)}, u32[]{:S(2)}, u32[]{:S(2)}) collective-permute-start(bf16[144,576]{0,1:T(8,128)(2,1)S(1)} %get-tuple-element.223), channel_id=1, source_target_pairs={{0,8},{4,12},{8,0},{12,4},{1,9},{5,13},{9,1},{13,5},{2,10},{6,14},... | collective-permute-start | bytes 497672 | tf_op jit(solution)/shard_map/ppermute | solution.py:307
  553.4 17.9 %collective-permute-start.86 = (bf16[144,576]{0,1:T(8,128)(2,1)S(1)}, bf16[144,576]{0,1:T(8,128)(2,1)S(1)}, u32[]{:S(2)}, u32[]{:S(2)}) collective-permute-start(bf16[144,576]{0,1:T(8,128)(2,1)S(1)} %copy-done.63), channel_id=1, source_target_pairs={{0,4},{4,0},{8,12},{12,8},{1,5},{5,1},{9,13},{13,9},{2,6},{6,2},{1... | collective-permute-start | bytes 497672 | tf_op jit(solution)/shard_map/ppermute | solution.py:307
  558.7 14.6 %collective-permute-start.90 = (bf16[144,576]{0,1:T(8,128)(2,1)S(1)}, bf16[144,576]{0,1:T(8,128)(2,1)S(1)}, u32[]{:S(2)}, u32[]{:S(2)}) collective-permute-start(bf16[144,576]{0,1:T(8,128)(2,1)S(1)} %copy-done.64), channel_id=1, source_target_pairs={{0,8},{4,12},{8,0},{12,4},{1,9},{5,13},{9,1},{13,5},{2,10},{6,14},... | collective-permute-start | bytes 497672 | tf_op jit(solution)/shard_map/ppermute | solution.py:307
  566.0 16.7 %collective-permute-start.89 = (bf16[144,576]{0,1:T(8,128)(2,1)S(1)}, bf16[144,576]{0,1:T(8,128)(2,1)S(1)}, u32[]{:S(2)}, u32[]{:S(2)}) collective-permute-start(bf16[144,576]{0,1:T(8,128)(2,1)S(1)} %get-tuple-element.230), channel_id=1, source_target_pairs={{0,4},{4,0},{8,12},{12,8},{1,5},{5,1},{9,13},{13,9},{2,6},{6,2},{1... | collective-permute-start | bytes 497672 | tf_op jit(solution)/shard_map/ppermute | solution.py:307
  567.6 16.0 %collective-permute-start.93 = (bf16[144,576]{0,1:T(8,128)(2,1)S(1)}, bf16[144,576]{0,1:T(8,128)(2,1)S(1)}, u32[]{:S(2)}, u32[]{:S(2)}) collective-permute-start(bf16[144,576]{0,1:T(8,128)(2,1)S(1)} %get-tuple-element.231), channel_id=1, source_target_pairs={{0,8},{4,12},{8,0},{12,4},{1,9},{5,13},{9,1},{13,5},{2,10},{6,14},... | collective-permute-start | bytes 497672 | tf_op jit(solution)/shard_map/ppermute | solution.py:307
  587.2 25.8 %collective-permute-start.64 = (f32[368,1152]{1,0:T(8,128)S(1)}, f32[368,1152]{1,0:T(8,128)S(1)}, u32[]{:S(2)}, u32[]{:S(2)}) collective-permute-start(f32[368,1152]{1,0:T(8,128)S(1)} %slice.798), channel_id=1, source_target_pairs={{0,16},{16,0},{1,17},{17,1},{2,18},{18,2},{3,19},{19,3},{4,20},{20... | collective-permute-start | bytes 5087240 | tf_op jit(solution)/shard_map/ppermute | solution.py:303
  (222 other events, 2451.9 us)

commit v2 on v0

--- a/solution.py
+++ b/solution.py
@@ -1,6 +1,8 @@
 import jax
 import jax.numpy as jnp
 from jax import lax
+from jax.experimental import pallas as pl
+from jax.experimental.pallas import tpu as pltpu
 from jax.sharding import PartitionSpec as P
 
 D = 1152
@@ -299,6 +301,1129 @@
     )
 
 
+def pair_swap(values):
+    return lax.ppermute(values, "dp", [(0, 1), (1, 0)])
+
+
+def row_swap(values, bit):
+    return lax.ppermute(values, "row", [(i, i ^ bit) for i in range(lax.axis_size("row"))])
+
+
+def ring_order(size):
+    return [0, 1, 3, 2] if size == 4 else list(range(size))
+
+
+def ring_shift(values, step):
+    order = ring_order(lax.axis_size("col"))
+    size = len(order)
+    return lax.ppermute(
+        values, "col", [(order[i], order[(i + step) % size]) for i in range(size)]
+    )
+
+
+def gather_ring(shard):
+    shards = [shard]
+    for _ in range(lax.axis_size("col") - 1):
+        shards.append(ring_shift(shards[-1], 1))
+    return shards
+
+
+MESH = pl.DeviceIdType.MESH
+F32 = jnp.float32
+BF16 = jnp.bfloat16
+LOG2E = 1.4426950408889634
+GELU_ROOT = 0.7978845608028654
+
+
+def neighbours():
+    dp, row, col = lax.axis_index("dp"), lax.axis_index("row"), lax.axis_index("col")
+    return dict(
+        core=(1 - dp, row, col),
+        x=(dp, row + 1 - 2 * lax.rem(row, 2), col),
+        y=(dp, lax.rem(row + 2, 4), col),
+        next=(dp, row, lax.rem(2 * col + 3 * (col // 2) + 1, 4)),
+        prev=(dp, row, lax.rem(2 * col + col // 2 + 2, 4)),
+    )
+
+
+def meet(peers):
+    barrier = pltpu.get_barrier_semaphore()
+    for peer in peers.values():
+        pl.semaphore_signal(barrier, inc=1, device_id=peer, device_id_type=MESH)
+    pl.semaphore_wait(barrier, len(peers))
+
+
+def mm(left, right):
+    return jnp.dot(left, right, preferred_element_type=F32)
+
+
+def mm_nt(left, right):
+    return lax.dot_general(left, right, (((1,), (1,)), ((), ())), preferred_element_type=F32)
+
+
+def each_rows(count, size, body):
+    @pl.loop(0, count // size)
+    def _(step):
+        body(pl.ds(pl.multiple_of(step * size, size), size))
+
+
+def transpose_into(target, source):
+    @pl.loop(0, source.shape[1] // 128)
+    def _(step):
+        at = pl.ds(pl.multiple_of(step * 128, 128), 128)
+        target[at, :] = source[:, at].T
+
+
+class Sender:
+    def __init__(self, send_sems, recv_sems):
+        self.sems = (send_sems, recv_sems)
+        self.count = 0
+        self.copies = []
+
+    def __call__(self, source, target, peer):
+        copy = pltpu.make_async_remote_copy(
+            source,
+            target,
+            self.sems[0].at[self.count],
+            self.sems[1].at[self.count],
+            device_id=peer,
+            device_id_type=MESH,
+        )
+        self.count += 1
+        copy.start()
+        self.copies.append(copy)
+        return copy
+
+    def finish(self):
+        for copy in self.copies:
+            copy.wait_send()
+
+
+class Copier:
+    def __init__(self, sems):
+        self.sems = sems
+        self.count = 0
+
+    def __call__(self, source, target):
+        copy = pltpu.make_async_copy(source, target, self.sems.at[self.count])
+        self.count += 1
+        copy.start()
+        return copy
+
+
+def norm_stats(values):
+    mean_rows = jnp.mean(values, axis=-1, keepdims=True)
+    centered = values - mean_rows
+    inv_scale = lax.rsqrt(jnp.mean(centered * centered, axis=-1, keepdims=True) + EPS)
+    return centered * inv_scale, inv_scale
+
+
+def forward_kernel(
+    x_ref,
+    teacher_ref,
+    mask_ref,
+    key_ref,
+    feature_ref,
+    qkv_bias_ref,
+    key_lane_ref,
+    up_bias_ref,
+    rest_bias_ref,
+    factor_ref,
+    spread_ref,
+    rest_spread_ref,
+    attn_ref,
+    ff_ref,
+    wpad_out,
+    wff_out,
+    triple_out,
+    mixed_out,
+    act_out,
+    slope_out,
+    norm1t_out,
+    norm2t_out,
+    rest_out,
+    lse_out,
+    act_rest_out,
+    slope_rest_out,
+    resid_out,
+    grad_out,
+    branch_out,
+    brancht_out,
+    result_out,
+    err_out,
+    wattn,
+    wff,
+    wpad,
+    triple,
+    mixed,
+    act,
+    slope,
+    norm1,
+    norm2,
+    turned,
+    part,
+    got1,
+    got2,
+    local_sems,
+    send_sems,
+    recv_sems,
+):
+    peers = neighbours()
+    meet(peers)
+    feat = attn_ref.shape[0]
+    half = feat // 2
+    depth = 4 * feat
+    tokens = norm1.shape[0]
+    own = tokens // 2
+    main = ff_ref.shape[1] // 2
+    qkv = triple.shape[2]
+    send = Sender(send_sems, recv_sems)
+    keep = Copier(local_sems)
+
+    def rows(block, low=0, size=None):
+        return pl.ds(block * feat + low, feat if size is None else size)
+
+    own_attn = keep(attn_ref, wattn.at[0, rows(0)])
+    own_ff = keep(ff_ref, wff.at[0, rows(0)])
+    az, ax, ay, a_low, a_high = ([None] * 4 for _ in range(5))
+
+    def attn_source(s):
+        return attn_ref if s == 0 else wattn.at[s, rows(0)]
+
+    def attn_ring(s):
+        az[s + 1] = send(attn_source(s), wattn.at[s + 1, rows(0)], peers["next"])
+
+    def attn_plane(s):
+        ax[s] = send(attn_source(s), wattn.at[s, rows(1)], peers["x"])
+        ay[s] = send(attn_source(s), wattn.at[s, rows(2)], peers["y"])
+
+    def attn_last(s):
+        ax[s].wait_recv()
+        a_low[s] = send(
+            wattn.at[s, rows(1, 0, half)], wattn.at[s, rows(3, 0, half)], peers["y"]
+        )
+        ay[s].wait_recv()
+        a_high[s] = send(
+            wattn.at[s, rows(2, half, half)], wattn.at[s, rows(3, half, half)], peers["x"]
+        )
+
+    fz, fy, fx = ([None] * 4 for _ in range(3))
+
+    def ff_first():
+        return (
+            send(ff_ref.at[pl.ds(0, half)], wff.at[0, rows(1, 0, half)], peers["x"]),
+            send(ff_ref.at[pl.ds(half, half)], wff.at[0, rows(2, half, half)], peers["y"]),
+        )
+
+    def ff_ring(s):
+        fz[s + 1] = [
+            send(wff.at[s, piece], wff.at[s + 1, piece], peers["next"])
+            for piece in (rows(0), rows(1, 0, half), rows(2, half, half))
+        ]
+
+    def ff_last(s):
+        fy[s] = [
+            send(wff.at[s, rows(k, 0, half)], wff.at[s, rows(k + 2, 0, half)], peers["y"])
+            for k in (0, 1)
+        ]
+        fx[s] = [
+            send(wff.at[s, rows(k, half, half)], wff.at[s, rows(k + 1, half, half)], peers["x"])
+            for k in (0, 2)
+        ]
+
+    def arrive(copies):
+        for copy in copies:
+            copy.wait_recv()
+
+    def attn_compute(s):
+        arrive([a_low[s], a_high[s]])
+        slot = s % 2
+        if s == 0:
+            own_attn.wait()
+        if s >= 2:
+            for copy in saved[s - 2]:
+                copy.wait()
+
+        def unpack(at):
+            block = wattn[s, at, :]
+            wpad[slot, at, :] = mm(block, spread_ref[...]).astype(BF16)
+            extra = mm(block[:, block.shape[1] - 128 :], rest_spread_ref[s]).astype(BF16)
+            if s == 0:
+                rest_out[at, :] = extra
+            else:
+                rest_out[at, :] = rest_out[at, :] + extra
+
+        each_rows(depth, feat, unpack)
+
+        def project(at):
+            values = mm(norm1[at, :], wpad[slot, :, :qkv]) + qkv_bias_ref[s]
+            values = values + key_ref[at, :] * key_lane_ref[...]
+            triple[slot, at, :] = values.astype(BF16)
+
+        each_rows(tokens, own, project)
+        scale = LOG2E * HD**-0.5
+        for h in range(qkv // 384):
+            query_at, key_at, value_at = (pl.ds((3 * h + j) * 128, 128) for j in range(3))
+            value_turned = triple[slot, :, value_at].T
+
+            def head(at, h=h, query_at=query_at, key_at=key_at, value_turned=value_turned):
+                scores = mm_nt(triple[slot, :, key_at], triple[slot, at, query_at])
+                peak = jnp.max(scores, axis=0, keepdims=True)
+                weights = jnp.exp2((scores - peak) * scale)
+                total = jnp.sum(weights, axis=0, keepdims=True)
+                lse_out[2 * s + h, :, at] = peak * scale + jnp.log2(total)
+                values = mm(value_turned, weights.astype(BF16)) / total
+                mixed[s, at, pl.ds(h * 128, 128)] = values.T.astype(BF16)
+
+            each_rows(tokens, 256, head)
+
+        def out(at):
+            values = mm_nt(mixed[s, at, :], wpad[slot, :, qkv:])
+            part[at, :] = values if s == 0 else part[at, :] + values
+
+        each_rows(tokens, own, out)
+        saved.append(
+            [
+                keep(wpad.at[slot], wpad_out.at[s]),
+                keep(triple.at[slot], triple_out.at[s]),
+                keep(mixed.at[s], mixed_out.at[s]),
+            ]
+        )
+
+    def gelu(pre):
+        inner = GELU_ROOT * (pre + 0.044715 * pre * pre * pre)
+        tanh = jnp.tanh(inner)
+        rise = 0.5 * (1.0 + tanh)
+        bend = 0.5 * pre * (1.0 - tanh * tanh) * (GELU_ROOT * (1.0 + 0.134145 * pre * pre))
+        return (pre * rise).astype(BF16), (rise + bend).astype(BF16)
+
+    def ff_compute(s):
+        arrive(fy[s] + fx[s])
+
+        def block(at):
+            pre = mm(norm2[at, :], wff[s, :, :main]) + up_bias_ref[s]
+            low, bent = gelu(pre)
+            act[s, at, :] = low
+            slope[s, at, :] = bent
+            part[at, :] = part[at, :] + mm_nt(low, wff[s, :, main:])
+
+        each_rows(tokens, own, block)
+        ff_saved.extend(
+            [
+                keep(act.at[s], act_out.at[s]),
+                keep(slope.at[s], slope_out.at[s]),
+                keep(wff.at[s], wff_out.at[s]),
+            ]
+        )
+
+    def rest_compute():
+        def block(at):
+            pre = mm(norm2[at, :], rest_out[:, :128]) + rest_bias_ref[...]
+            low, bent = gelu(pre)
+            act_rest_out[at, :] = low
+            slope_rest_out[at, :] = bent
+            part[at, :] = mm_nt(low, rest_out[:, 128:])
+
+        each_rows(tokens, own, block)
+
+    saved, ff_saved = [], []
+    attn_ring(0)
+    attn_plane(0)
+
+    def first_norm(at):
+        normed, _ = norm_stats(x_ref[at, :].astype(F32))
+        norm1[at, :] = (normed * feature_ref[0:1] + feature_ref[1:2]).astype(BF16)
+
+    each_rows(own, 16, first_norm)
+    swap1 = send(norm1.at[pl.ds(0, own)], norm1.at[pl.ds(own, own)], peers["core"])
+    az[1].wait_recv()
+    attn_ring(1)
+    attn_plane(1)
+    attn_last(0)
+    swap1.wait_recv()
+    az[2].wait_recv()
+    attn_ring(2)
+    attn_plane(2)
+    attn_last(1)
+    first = ff_first()
+    attn_compute(0)
+    az[3].wait_recv()
+    attn_plane(3)
+    attn_last(2)
+    own_ff.wait()
+    arrive(first)
+    ff_ring(0)
+    attn_compute(1)
+    attn_last(3)
+    ff_last(0)
+    attn_compute(2)
+    attn_compute(3)
+    swap2 = send(part.at[pl.ds(own, own)], got1, peers["core"])
+    arrive([swap2])
+
+    def second_norm(at):
+        values = x_ref[at, :].astype(F32) + part[at, :] + got1[at, :] + feature_ref[4:5]
+        resid_out[at, :] = values
+        normed, _ = norm_stats(values)
+        norm2[at, :] = (normed * feature_ref[2:3] + feature_ref[3:4]).astype(BF16)
+
+    each_rows(own, 16, second_norm)
+    swap2.wait_send()
+    swap3 = send(norm2.at[pl.ds(0, own)], norm2.at[pl.ds(own, own)], peers["core"])
+    arrive(fz[1])
+    ff_ring(1)
+    ff_last(1)
+    transpose_into(turned, norm1)
+    turn1 = keep(turned, norm1t_out)
+    arrive([swap3])
+    rest_compute()
+    turn1.wait()
+    transpose_into(turned, norm2)
+    turn2 = keep(turned, norm2t_out)
+    arrive(fz[2])
+    ff_ring(2)
+    ff_last(2)
+    ff_compute(0)
+    ff_compute(1)
+    arrive(fz[3])
+    ff_last(3)
+    ff_compute(2)
+    ff_compute(3)
+    swap4 = send(part.at[pl.ds(own, own)], got2, peers["core"])
+    arrive([swap4])
+    err_out[...] = jnp.zeros_like(err_out)
+
+    def finish(at):
+        values = resid_out[at, :] + part[at, :] + got2[at, :] + feature_ref[5:6]
+        result_out[at, :] = values.astype(BF16)
+        error = values - teacher_ref[at, :].astype(F32)
+        masked = error * mask_ref[at, :]
+        err_out[...] = err_out[...] + error * masked
+        grad = masked * factor_ref[...]
+        grad_out[at, :] = grad
+        branch_out[at, :] = grad.astype(BF16)
+
+    each_rows(own, 16, finish)
+    swap5 = send(branch_out.at[pl.ds(0, own)], branch_out.at[pl.ds(own, own)], peers["core"])
+    arrive([swap5])
+    transpose_into(brancht_out, branch_out)
+    turn2.wait()
+    for copies in saved[2:]:
+        for copy in copies:
+            copy.wait()
+    for copy in ff_saved:
+        copy.wait()
+    for copy in send.copies:
+        if copy is not swap2:
+            copy.wait_send()
+
+
+def forward_call(arrays, feat, lanes, main, qkv, mix, own, depth):
+    tokens = 2 * own
+    anywhere = pl.BlockSpec(memory_space=pl.ANY)
+    local = pl.BlockSpec(memory_space=pltpu.VMEM)
+    shapes = [
+        ((4, depth, qkv + mix), BF16, anywhere),
+        ((4, depth, 2 * main), BF16, anywhere),
+        ((4, tokens, qkv), BF16, anywhere),
+        ((4, tokens, mix), BF16, anywhere),
+        ((4, tokens, main), BF16, anywhere),
+        ((4, tokens, main), BF16, anywhere),
+        ((depth, tokens), BF16, anywhere),
+        ((depth, tokens), BF16, anywhere),
+        ((depth, 256), BF16, local),
+        ((8, 1, tokens), F32, local),
+        ((tokens, 128), BF16, local),
+        ((tokens, 128), BF16, local),
+        ((own, depth), F32, local),
+        ((own, depth), F32, local),
+        ((tokens, depth), BF16, local),
+        ((depth, tokens), BF16, local),
+        ((own, depth), BF16, local),
+        ((16, depth), F32, local),
+    ]
+    return pl.pallas_call(
+        forward_kernel,
+        out_shape=[jax.ShapeDtypeStruct(shape, dtype) for shape, dtype, _ in shapes],
+        in_specs=[local] * 12 + [anywhere] * 2,
+        out_specs=[spec for _, _, spec in shapes],
+        scratch_shapes=[
+            pltpu.VMEM((4, depth, lanes), BF16),
+            pltpu.VMEM((4, depth, 2 * main), BF16),
+            pltpu.VMEM((2, depth, qkv + mix), BF16),
+            pltpu.VMEM((2, tokens, qkv), BF16),
+            pltpu.VMEM((4, tokens, mix), BF16),
+            pltpu.VMEM((4, tokens, main), BF16),
+            pltpu.VMEM((4, tokens, main), BF16),
+            pltpu.VMEM((tokens, depth), BF16),
+            pltpu.VMEM((tokens, depth), BF16),
+            pltpu.VMEM((depth, tokens), BF16),
+            pltpu.VMEM((tokens, depth), F32),
+            pltpu.VMEM((own, depth), F32),
+            pltpu.VMEM((own, depth), F32),
+            pltpu.SemaphoreType.DMA((32,)),
+            pltpu.SemaphoreType.DMA((64,)),
+            pltpu.SemaphoreType.DMA((64,)),
+        ],
+        compiler_params=pltpu.CompilerParams(
+            collective_id=1, has_side_effects=True, vmem_limit_bytes=62 << 20
+        ),
+    )(*arrays)
+
+
+def backward_kernel(
+    branch2_ref,
+    rest_ref,
+    act_rest_ref,
+    slope_rest_ref,
+    lse_ref,
+    feature_ref,
+    spread_ref,
+    rest_spread_ref,
+    x_ref,
+    resid_ref,
+    grad_hbm,
+    norm1t_hbm,
+    norm2t_hbm,
+    branch2t_hbm,
+    wpad_hbm,
+    wff_hbm,
+    triple_hbm,
+    mixed_hbm,
+    act_hbm,
+    slope_hbm,
+    grad_in_out,
+    terms_out,
+    units_out,
+    units_rest_out,
+    heads_out,
+    attn_out,
+    ff_out,
+    gattn,
+    gff,
+    wslot,
+    kept,
+    grad_pre,
+    grad_rest,
+    normt,
+    brancht,
+    branch1,
+    part,
+    got,
+    grad_mid,
+    dtriple,
+    grad_mixed,
+    grad_key,
+    grad_value,
+    inner_row,
+    ra,
+    rb,
+    r1,
+    r2,
+    rz,
+    ry,
+    rx,
+    rzl,
+    rzh,
+    rfx,
+    rfy,
+    local_sems,
+    send_sems,
+    recv_sems,
+):
+    peers = neighbours()
+    feat = attn_out.shape[0]
+    half = feat // 2
+    depth = 4 * feat
+    tokens = branch2_ref.shape[0]
+    own = tokens // 2
+    main = gff.shape[2] // 2
+    qkv = triple_hbm.shape[2]
+    send = Sender(send_sems, recv_sems)
+    keep = Copier(local_sems)
+
+    def rows(block, low=0, size=None):
+        return pl.ds(block * feat + low, feat if size is None else size)
+
+    def load_ff(s):
+        slot = s % 2
+        return [
+            keep(wff_hbm.at[s], wslot.at[slot]),
+            keep(act_hbm.at[s], kept.at[slot, :, pl.ds(0, main)]),
+            keep(slope_hbm.at[s], kept.at[slot, :, pl.ds(main, main)]),
+        ]
+
+    def load_attn(s):
+        slot = s % 2
+        return [
+            keep(wpad_hbm.at[s], wslot.at[slot]),
+            keep(triple_hbm.at[s], kept.at[slot, :, pl.ds(0, qkv)]),
+            keep(mixed_hbm.at[s], kept.at[slot, :, pl.ds(qkv, grad_mixed.shape[1])]),
+        ]
+
+    loads = {3: load_ff(3)}
+    turns = [keep(norm2t_hbm, normt), keep(branch2t_hbm, brancht)]
+    loads[2] = load_ff(2)
+    load_grad = keep(grad_hbm, grad_mid)
+    meet(peers)
+    cy, cx, zl, zh = ([None] * 4 for _ in range(4))
+    ca, cb, c1, c2, cz = ([None] * 4 for _ in range(5))
+
+    def add_into(target, at, *sources):
+        size = at.size
+
+        @pl.loop(0, size // 16)
+        def _(step):
+            here = pl.ds(pl.multiple_of(at.start + step * 16, 16), 16)
+            there = pl.ds(pl.multiple_of(step * 16, 16), 16)
+            total = target[here, :].astype(F32)
+            for source in sources:
+                total = total + source[there, :].astype(F32)
+            target[here, :] = total.astype(BF16)
+
+    def column_sum(values):
+        return jnp.sum(values.astype(F32), axis=0, keepdims=True)
+
+    def ff_compute(s):
+        slot = s % 2
+        for copy in loads[s]:
+            copy.wait()
+        units_out[s] = jnp.zeros((1, main), F32)
+
+        def block(at):
+            grad = mm(branch2_ref[at, :], wslot[slot, :, main : 2 * main])
+            low = (grad * kept[slot, at, main:].astype(F32)).astype(BF16)
+            grad_pre[at, :] = low
+            units_out[s] = units_out[s] + column_sum(low)
+            values = mm_nt(low, wslot[slot, :, :main])
+            part[at, :] = values if s == 3 else part[at, :] + values
+
+        each_rows(tokens, own, block)
+        if s == 3:
+            for copy in turns:
+                copy.wait()
+
+        def grads(at):
+            gff[s, at, :main] = mm(normt[at, :], grad_pre[...]).astype(BF16)
+            gff[s, at, main:] = mm(brancht[at, :], kept[slot, :, :main]).astype(BF16)
+
+        each_rows(depth, feat, grads)
+        cy[s] = [
+            send(gff.at[s, rows(k, 0, half)], ry.at[s, k - 2], peers["y"]) for k in (2, 3)
+        ]
+        cx[s] = [
+            send(gff.at[s, rows(k, half, half)], rx.at[s, k // 2], peers["x"]) for k in (1, 3)
+        ]
+        if s >= 2:
+            loads[s - 2] = load_ff(s - 2)
+
+    def rest_compute():
+        units_rest_out[...] = jnp.zeros_like(units_rest_out)
+
+        def block(at):
+            grad = mm(branch2_ref[at, :], rest_ref[:, 128:])
+            low = (grad * slope_rest_ref[at, :].astype(F32)).astype(BF16)
+            grad_pre[at, :128] = low
+            units_rest_out[...] = units_rest_out[...] + column_sum(low)
+            part[at, :] = part[at, :] + mm_nt(low, rest_ref[:, :128])
+
+        each_rows(tokens, own, block)
+
+        def grads(at):
+            grad_rest[at, :128] = mm(normt[at, :], grad_pre[:, :128]).astype(BF16)
+            grad_rest[at, 128:] = mm(brancht[at, :], act_rest_ref[...]).astype(BF16)
+
+        each_rows(depth, feat, grads)
+
+    def ff_add(s):
+        for copy in cy[s] + cx[s]:
+            copy.wait_recv()
+        last = s == 3
+        if not last:
+            for copy in zl[s] + zh[s]:
+                copy.wait_recv()
+        lows, highs = [], []
+        for i, k in enumerate((0, 1)):
+            piece = rows(k, 0, half)
+            add_into(gff.at[s], piece, ry.at[s, i], *([] if last else [rzl.at[s, i]]))
+            lows.append((piece, i))
+        for i, k in enumerate((0, 2)):
+            piece = rows(k, half, half)
+            add_into(gff.at[s], piece, rx.at[s, i], *([] if last else [rzh.at[s, i]]))
+            highs.append((piece, i))
+        if s:
+            zl[s - 1] = [
+                send(gff.at[s, piece], rzl.at[s - 1, i], peers["prev"]) for piece, i in lows
+            ]
+            zh[s - 1] = [
+                send(gff.at[s, piece], rzh.at[s - 1, i], peers["prev"]) for piece, i in highs
+            ]
+
+    def attn_compute(s):
+        slot = s % 2
+        for copy in attn_loads[s]:
+            copy.wait()
+
+        def back_out(at):
+            grad_mixed[at, :] = mm(branch1[at, :], wslot[slot, :, qkv:]).astype(BF16)
+
+        each_rows(tokens, own, back_out)
+        scale = HD**-0.5
+        for h in range(qkv // 384):
+            query_at, key_at, value_at = (pl.ds((3 * h + j) * 128, 128) for j in range(3))
+            mix_at = pl.ds(h * 128, 128)
+            value_of_mix = pl.ds(qkv + h * 128, 128)
+            key_turned = kept[slot, :, key_at].T
+            product = grad_mixed[:, mix_at].astype(F32) * kept[slot, :, value_of_mix].astype(F32)
+            inner_row[...] = jnp.sum(product.T, axis=0, keepdims=True)
+            grad_key[...] = jnp.zeros_like(grad_key)
+            grad_value[...] = jnp.zeros_like(grad_value)
+
+            def head(at, h=h, query_at=query_at, key_at=key_at, value_at=value_at,
+                     mix_at=mix_at, key_turned=key_turned):
+                query = kept[slot, at, query_at]
+                grad = grad_mixed[at, mix_at]
+                scores = mm_nt(kept[slot, :, key_at], query)
+                weights = jnp.exp2(scores * (scale * LOG2E) - lse_ref[2 * s + h, :, at])
+                grad_soft = mm_nt(kept[slot, :, value_at], grad)
+                grad_raw = (weights * (grad_soft - inner_row[:, at]) * scale).astype(BF16)
+                grad_value[...] += mm(weights.astype(BF16), grad)
+                grad_key[...] += mm(grad_raw, query)
+                dtriple[at, query_at] = mm(key_turned, grad_raw).T.astype(BF16)
+
+            each_rows(tokens, 256, head)
+            dtriple[:, key_at] = grad_key[...].astype(BF16)
+            dtriple[:, value_at] = grad_value[...].astype(BF16)
+        heads_out[s] = jnp.zeros((1, qkv), F32)
+
+        def back_in(at):
+            values = mm_nt(dtriple[at, :], wslot[slot, :, :qkv])
+            part[at, :] = values if s == 3 else part[at, :] + values
+            heads_out[s] = heads_out[s] + column_sum(dtriple[at, :])
+
+        each_rows(tokens, own, back_in)
+
+        def grads(at):
+            first = mm(normt[at, :], dtriple[...]).astype(BF16)
+            second = mm(brancht[at, :], kept[slot, :, qkv:]).astype(BF16)
+            packed = mm_nt(first, spread_ref[:, :qkv]) + mm_nt(second, spread_ref[:, qkv:])
+            gattn[s, at, :] = packed.astype(BF16)
+            tail = pl.ds(packed.shape[1] - 128, 128)
+            extra = mm_nt(grad_rest[at, :], rest_spread_ref[s])
+            gattn[s, at, tail] = (gattn[s, at, tail].astype(F32) + extra).astype(BF16)
+
+        each_rows(depth, feat, grads)
+        ca[s] = send(gattn.at[s, rows(3, 0, half)], ra.at[s], peers["y"])
+        cb[s] = send(gattn.at[s, rows(3, half, half)], rb.at[s], peers["x"])
+        if s >= 2:
+            attn_loads[s - 2] = load_attn(s - 2)
+
+    def attn_plane(s):
+        ca[s].wait_recv()
+        add_into(gattn.at[s], rows(1, 0, half), ra.at[s])
+        c1[s] = send(gattn.at[s, rows(1)], r1.at[s], peers["x"])
+        cb[s].wait_recv()
+        add_into(gattn.at[s], rows(2, half, half), rb.at[s])
+        c2[s] = send(gattn.at[s, rows(2)], r2.at[s], peers["y"])
+
+    def attn_ring(s):
+        c1[s].wait_recv()
+        c2[s].wait_recv()
+        if s < 3:
+            cz[s].wait_recv()
+        add_into(gattn.at[s], rows(0), r1.at[s], r2.at[s], *([rz.at[s]] if s < 3 else []))
+        if s:
+            cz[s - 1] = send(gattn.at[s, rows(0)], rz.at[s - 1], peers["prev"])
+
+    terms_out[...] = jnp.zeros_like(terms_out)
+
+    def add_term(index, values):
+        terms_out[index] = terms_out[index] + values
+
+    ff_compute(3)
+    ff_compute(2)
+    ff_compute(1)
+    ff_add(3)
+    ff_compute(0)
+    attn_loads = {3: load_attn(3), 2: load_attn(2)}
+    rest_compute()
+    load_norm = keep(norm1t_hbm, normt)
+    swap1 = send(part.at[pl.ds(own, own)], got, peers["core"])
+    swap1.wait_recv()
+    load_grad.wait()
+
+    def mid(at):
+        normed, inv_scale = norm_stats(resid_ref[at, :])
+        grad_norm = part[at, :] + got[at, :]
+        add_term(2, grad_norm * normed)
+        add_term(3, grad_norm)
+        scaled = grad_norm * feature_ref[2:3]
+        first = jnp.mean(scaled, axis=-1, keepdims=True)
+        second = jnp.mean(scaled * normed, axis=-1, keepdims=True)
+        grad = grad_mid[at, :] + inv_scale * (scaled - first - normed * second)
+        grad_mid[at, :] = grad
+        low = grad.astype(BF16)
+        branch1[at, :] = low
+        add_term(4, low.astype(F32))
+        add_term(5, branch2_ref[at, :].astype(F32))
+
+    each_rows(own, 16, mid)
+    swap1.wait_send()
+    swap2 = send(branch1.at[pl.ds(0, own)], branch1.at[pl.ds(own, own)], peers["core"])
+    swap2.wait_recv()
+    load_norm.wait()
+    transpose_into(brancht, branch1)
+    attn_compute(3)
+    ff_add(2)
+    attn_compute(2)
+    attn_plane(3)
+    attn_compute(1)
+    attn_plane(2)
+    ff_add(1)
+    attn_ring(3)
+    attn_compute(0)
+    swap3 = send(part.at[pl.ds(own, own)], got, peers["core"])
+    attn_plane(1)
+    attn_ring(2)
+    attn_plane(0)
+    swap3.wait_recv()
+
+    def last(at):
+        normed, inv_scale = norm_stats(x_ref[at, :].astype(F32))
+        grad_norm = part[at, :] + got[at, :]
+        add_term(0, grad_norm * normed)
+        add_term(1, grad_norm)
+        scaled = grad_norm * feature_ref[0:1]
+        first = jnp.mean(scaled, axis=-1, keepdims=True)
+        second = jnp.mean(scaled * normed, axis=-1, keepdims=True)
+        grad = grad_mid[at, :] + inv_scale * (scaled - first - normed * second)
+        grad_in_out[at, :] = grad.astype(BF16)
+
+    each_rows(own, 16, last)
+    ff_add(0)
+    end_low = send(gff.at[0, rows(1, 0, half)], rfx, peers["x"])
+    end_high = send(gff.at[0, rows(2, half, half)], rfy, peers["y"])
+    attn_ring(1)
+    end_low.wait_recv()
+    end_high.wait_recv()
+    add_into(gff.at[0], rows(0, 0, half), rfx)
+    add_into(gff.at[0], rows(0, half, half), rfy)
+    ff_done = keep(gff.at[0, rows(0)], ff_out)
+    attn_ring(0)
+    attn_done = keep(gattn.at[0, rows(0)], attn_out)
+    ff_done.wait()
+    attn_done.wait()
+    for copy in send.copies:
+        if copy is not swap1:
+            copy.wait_send()
+
+
+def backward_call(arrays, feat, lanes, main, qkv, mix, own, depth):
+    tokens = 2 * own
+    half = feat // 2
+    anywhere = pl.BlockSpec(memory_space=pl.ANY)
+    local = pl.BlockSpec(memory_space=pltpu.VMEM)
+    shapes = [
+        ((own, depth), BF16, local),
+        ((6, 16, depth), F32, local),
+        ((4, 1, main), F32, local),
+        ((1, 128), F32, local),
+        ((4, 1, qkv), F32, local),
+        ((feat, lanes), BF16, anywhere),
+        ((feat, 2 * main), BF16, anywhere),
+    ]
+    return pl.pallas_call(
+        backward_kernel,
+        out_shape=[jax.ShapeDtypeStruct(shape, dtype) for shape, dtype, _ in shapes],
+        in_specs=[local] * 10 + [anywhere] * 10,
+        out_specs=[spec for _, _, spec in shapes],
+        scratch_shapes=[
+            pltpu.VMEM((4, depth, lanes), BF16),
+            pltpu.VMEM((4, depth, 2 * main), BF16),
+            pltpu.VMEM((2, depth, 2 * main), BF16),
+            pltpu.VMEM((2, tokens, qkv + mix), BF16),
+            pltpu.VMEM((tokens, main), BF16),
+            pltpu.VMEM((depth, 256), BF16),
+            pltpu.VMEM((depth, tokens), BF16),
+            pltpu.VMEM((depth, tokens), BF16),
+            pltpu.VMEM((tokens, depth), BF16),
+            pltpu.VMEM((tokens, depth), F32),
+            pltpu.VMEM((own, depth), F32),
+            pltpu.VMEM((own, depth), F32),
+            pltpu.VMEM((tokens, qkv), BF16),
+            pltpu.VMEM((tokens, mix), BF16),
+            pltpu.VMEM((tokens, 128), F32),
+            pltpu.VMEM((tokens, 128), F32),
+            pltpu.VMEM((1, tokens), F32),
+            pltpu.VMEM((4, half, lanes), BF16),
+            pltpu.VMEM((4, half, lanes), BF16),
+            pltpu.VMEM((4, feat, lanes), BF16),
+            pltpu.VMEM((4, feat, lanes), BF16),
+            pltpu.VMEM((3, feat, lanes), BF16),
+            pltpu.VMEM((4, 2, half, 2 * main), BF16),
+            pltpu.VMEM((4, 2, half, 2 * main), BF16),
+            pltpu.VMEM((3, 2, half, 2 * main), BF16),
+            pltpu.VMEM((3, 2, half, 2 * main), BF16),
+            pltpu.VMEM((half, 2 * main), BF16),
+            pltpu.VMEM((half, 2 * main), BF16),
+            pltpu.SemaphoreType.DMA((32,)),
+            pltpu.SemaphoreType.DMA((72,)),
+            pltpu.SemaphoreType.DMA((72,)),
+        ],
+        compiler_params=pltpu.CompilerParams(
+            collective_id=2, has_side_effects=True, vmem_limit_bytes=63 << 20
+        ),
+    )(*arrays)
+
+
+def on_chip(
+    layer_input,
+    teacher,
+    valid,
+    proj_in,
+    bias_query,
+    bias_value,
+    proj_out,
+    bias_out,
+    norm1_gain,
+    norm1_shift,
+    norm2_gain,
+    norm2_shift,
+    w_up,
+    bias_up,
+    w_down,
+    bias_down,
+):
+    core = lax.axis_index("dp")
+    row = lax.axis_index("row")
+    cols = lax.axis_size("col")
+    feat = layer_input.shape[1]
+    images = layer_input.shape[0] // SEQ
+    half_seq = (SEQ + 255) // 256 * 128
+    pad_seq = 2 * half_seq
+    units = w_up.shape[1] // 2
+    width = proj_out.shape[0] // 2
+    heads = width // HD
+
+    def core_half(values, axis):
+        size = values.shape[axis] // 2
+        return lax.dynamic_slice_in_dim(values, core * size, size, axis)
+
+    def to_chip(values):
+        imgs = jnp.pad(values.reshape(images, SEQ, -1), ((0, 0), (0, pad_seq - SEQ), (0, 0)))
+        imgs = imgs.reshape(images, 2, half_seq, -1)
+        keep = lax.dynamic_index_in_dim(imgs, core, 1, False)
+        give = lax.dynamic_index_in_dim(imgs, 1 - core, 1, False)
+        got = pair_swap(give)
+        first = core == 0
+        every = jnp.concatenate([jnp.where(first, keep, got), jnp.where(first, got, keep)], axis=0)
+        parts = []
+        for k in range(4):
+            part = lax.dynamic_index_in_dim(every, row ^ k, 0, False)
+            parts.append(row_swap(part, k) if k else part)
+        return jnp.concatenate(parts, axis=1)
+
+    def from_chip(values):
+        parts = []
+        for k in range(4):
+            part = values[:, k * feat : (k + 1) * feat]
+            parts.append(row_swap(part, k) if k else part)
+        stacked = jnp.stack(parts)
+        every = jnp.stack([lax.dynamic_index_in_dim(stacked, row ^ i, 0, False) for i in range(4)])
+        every = every.reshape(2, images, half_seq, feat)
+        mine = lax.dynamic_index_in_dim(every, core, 0, False)
+        got = pair_swap(lax.dynamic_index_in_dim(every, 1 - core, 0, False))
+        first = core == 0
+        both = jnp.stack([jnp.where(first, mine, got), jnp.where(first, got, mine)], axis=1)
+        return both.reshape(images, pad_seq, feat)[:, :SEQ].reshape(images * SEQ, feat)
+
+    main = units // 128 * 128
+    rest = units - main
+    at = 4 * width
+    lanes = (at + 2 * rest + 127) // 128 * 128
+    qkv, mix = 3 * heads * 128, heads * 128
+    up_half, down_half = core_half(w_up, 1), core_half(w_down, 0).T
+    attn_shard = jnp.concatenate(
+        [
+            core_half(proj_in, 1),
+            core_half(proj_out, 0).T,
+            up_half[:, main:],
+            down_half[:, main:],
+            jnp.zeros((feat, lanes - at - 2 * rest), jnp.bfloat16),
+        ],
+        axis=1,
+    )
+    ff_shard = jnp.concatenate([up_half[:, :main], down_half[:, :main]], axis=1)
+    lane = jnp.arange(lanes)
+    spread_at = jnp.where(lane < at, lane // HD * 128 + lane % HD, -1)
+    spread = (spread_at[:, None] == jnp.arange(qkv + mix)[None]).astype(jnp.bfloat16)
+    tail = lane[-128:]
+    rest_spread = []
+    for s in range(cols):
+        up_at = jnp.where((tail >= at) & (tail < at + rest), tail - at + s * rest, -1)
+        down_at = jnp.where(
+            (tail >= at + rest) & (tail < at + 2 * rest), tail - at - rest + s * rest + 128, -1
+        )
+        place = jnp.arange(256)[None]
+        rest_spread.append((up_at[:, None] == place) | (down_at[:, None] == place))
+    rest_spread = jnp.stack(rest_spread).astype(jnp.bfloat16)
+    features = jnp.stack([norm1_gain, norm1_shift, norm2_gain, norm2_shift, bias_out, bias_down])
+    features = jnp.concatenate([features] + [row_swap(features, k) for k in (1, 2, 3)], axis=1)
+    features = jnp.pad(features.astype(jnp.float32), ((0, 2), (0, 0)))
+    col_biases = gather_ring(
+        jnp.concatenate([core_half(bias_query, 0), core_half(bias_value, 0), core_half(bias_up, 0)])[None]
+    )
+
+    x_half = to_chip(layer_input)
+    teacher_half = to_chip(teacher)
+    count = jnp.sum(valid.astype(jnp.float32)).reshape(1, 1)
+    count = count + pair_swap(count)
+    for bit in (1, 2):
+        count = count + lax.ppermute(count, "col", [(i, i ^ bit) for i in range(cols)])
+    valid_imgs = jnp.pad(valid.reshape(images, SEQ), ((0, 0), (0, pad_seq - SEQ)))
+    other_valid = pair_swap(valid_imgs)
+    from_here = (row // images) == core
+    chip_valid = lax.dynamic_index_in_dim(
+        jnp.where(from_here, valid_imgs, other_valid), lax.rem(row, images), 0, False
+    )
+    mask_half = lax.dynamic_slice_in_dim(chip_valid, core * half_seq, half_seq, 0)
+    mask_half = mask_half.astype(jnp.float32)[:, None]
+
+    place = jnp.arange(pad_seq)
+    token = jnp.where(place < half_seq, place + core * half_seq, place - core * half_seq)
+    key_column = jnp.where(token < SEQ, 0.0, -1e30).astype(jnp.float32)[:, None]
+    lane = jnp.arange(qkv)
+    key_lane = (lane % 384 == 128 + HD).astype(jnp.float32)[None]
+    one_lane = (lane % 384 == HD).astype(jnp.float32)[None]
+    qkv_biases, up_biases, rest_biases = [], [], []
+    for s in range(cols):
+        bias = col_biases[s][0].astype(jnp.float32)
+        query, value = bias[:width].reshape(heads, HD), bias[width : 2 * width].reshape(heads, HD)
+        spaced = jnp.stack([query, jnp.zeros_like(query), value], axis=1)
+        spaced = jnp.pad(spaced, ((0, 0), (0, 0), (0, 128 - HD))).reshape(1, qkv)
+        qkv_biases.append(spaced + one_lane)
+        up_biases.append(bias[None, 2 * width : 2 * width + main])
+        rest_biases.append(bias[2 * width + main :])
+    rest_bias = jnp.pad(jnp.concatenate(rest_biases), (0, 128 - cols * rest))[None]
+    tokens_all = layer_input.shape[0] * lax.axis_size("dp") * cols
+    factor = tokens_all / count
+
+    sizes = (feat, lanes, main, qkv, mix, half_seq, 4 * feat)
+    (
+        wpad, wff, triple, mixed, act, slope, norm1t, norm2t, rest_weight, lse, act_rest,
+        slope_rest, resid1, grad_result, branch2, branch2t, result, err_rows,
+    ) = forward_call(
+        (
+            x_half, teacher_half, mask_half, key_column, features, jnp.stack(qkv_biases),
+            key_lane, jnp.stack(up_biases), rest_bias, jnp.broadcast_to(factor, (1, 4 * feat)),
+            spread, rest_spread, attn_shard, ff_shard,
+        ),
+        *sizes,
+    )
+    layer_output = from_chip(result)
+    err_part = jnp.sum(err_rows)
+    grad_in, terms, unit_main, unit_rest, head_rows, attn_sum, ff_sum = backward_call(
+        (
+            branch2, rest_weight, act_rest, slope_rest, lse, features, spread, rest_spread,
+            x_half, resid1, grad_result, norm1t, norm2t, branch2t, wpad, wff, triple, mixed,
+            act, slope,
+        ),
+        *sizes,
+    )
+    grad_input = from_chip(grad_in).astype(jnp.float32)
+    terms = jnp.sum(terms, axis=1)
+    head_rows = head_rows.reshape(cols, heads, 3, 128)[..., :HD]
+    bias_rows = [
+        jnp.concatenate(
+            [
+                head_rows[s, :, 0].reshape(1, width),
+                head_rows[s, :, 2].reshape(1, width),
+                unit_main[s],
+                unit_rest[:, s * rest : (s + 1) * rest],
+            ],
+            axis=1,
+        )
+        for s in range(cols)
+    ]
+    bias_sum = bias_rows[cols - 1]
+    for s in reversed(range(cols - 1)):
+        bias_sum = bias_rows[s] + ring_shift(bias_sum, -1)
+    near = terms[:, : 2 * feat] + row_swap(terms[:, 2 * feat :], 2)
+    terms = near[:, :feat] + row_swap(near[:, feat:], 1)
+
+    def plane_sum(values):
+        values = values + row_swap(values, 1)
+        return values + row_swap(values, 2)
+
+    err_plane = plane_sum(err_part.reshape(1, 1))
+    sums = jnp.concatenate([terms, jnp.broadcast_to(err_plane, (1, feat))], axis=0)
+    for bit in (1, 2):
+        sums = sums + lax.ppermute(sums, "col", [(i, i ^ bit) for i in range(cols)])
+    sums = sums + pair_swap(sums)
+    loss_value = sums[6, 0] / (count[0, 0] * D)
+
+    def both_halves(values):
+        got = pair_swap(values)
+        first = core == 0
+        return jnp.concatenate(
+            [jnp.where(first, values, got), jnp.where(first, got, values)], axis=-1
+        )
+
+    bias_sum = plane_sum(bias_sum)[0]
+    head_mine = both_halves(bias_sum[: 2 * width].reshape(2, width))
+    unit_mine = both_halves(bias_sum[2 * width :])
+
+    def weight_rows(total):
+        size = feat // 2
+        keep = lax.dynamic_slice_in_dim(total, core * size, size, 0)
+        give = lax.dynamic_slice_in_dim(total, (1 - core) * size, size, 0)
+        return keep, pair_swap(give)
+
+    def joined(keep, got, axis):
+        first = core == 0
+        return jnp.concatenate(
+            [jnp.where(first, keep, got), jnp.where(first, got, keep)], axis=axis
+        ).astype(jnp.float32)
+
+    ff_keep, ff_got = weight_rows(ff_sum)
+    attn_keep, attn_got = weight_rows(attn_sum)
+
+    def up_of(attn, ff):
+        return jnp.concatenate([ff[:, :main], attn[:, at : at + rest]], axis=1)
+
+    def down_of(attn, ff):
+        return jnp.concatenate([ff[:, main:], attn[:, at + rest : at + 2 * rest]], axis=1).T
+
+    grad_w_up = joined(up_of(attn_keep, ff_keep), up_of(attn_got, ff_got), 1)
+    grad_w_down = joined(down_of(attn_keep, ff_keep), down_of(attn_got, ff_got), 0)
+    grad_proj_in = joined(attn_keep[:, : 3 * width], attn_got[:, : 3 * width], 1)
+    grad_proj_out = joined(attn_keep[:, 3 * width : at].T, attn_got[:, 3 * width : at].T, 0)
+    return (
+        layer_output,
+        loss_value,
+        grad_input,
+        grad_proj_in[None],
+        head_mine[0],
+        head_mine[1],
+        grad_proj_out[:, None],
+        sums[4],
+        sums[0],
+        sums[1],
+        sums[2],
+        sums[3],
+        grad_w_up[None],
+        unit_mine,
+        grad_w_down[:, None],
+        sums[5],
+    )
+
+
+def one_image_a_chip(mesh, tokens):
+    sizes = mesh.shape
+    pairs = sizes["dp"] == 2 and sizes["row"] == 4 and sizes["col"] == 4
+    return pairs and tokens == SEQ * sizes["row"] * sizes["col"]
+
+
 def solution(mesh):
     placed = (
         P(("dp", "col"), "row"),
@@ -318,11 +1443,7 @@
         P("col", "row"),
         P("row"),
     )
-    return jax.shard_map(
-        on_device,
-        mesh=mesh,
-        in_specs=placed,
-        out_specs=(
+    returned = (
             P(("dp", "col"), "row"),
             P(),
             P(("dp", "col"), "row"),
@@ -339,6 +1460,12 @@
             P("col"),
             P("col", "row", "dp"),
             P("row"),
-        ),
-        check_vma=False,
-    )
+        )
+
+    def whole(layer_input, *others):
+        body = on_chip if one_image_a_chip(mesh, layer_input.shape[0]) else on_device
+        return jax.shard_map(
+            body, mesh=mesh, in_specs=placed, out_specs=returned, check_vma=False
+        )(layer_input, *others)
+
+    return whole

time: 3450 us -> 513 us (0.15)
  waiting for transfers between devices: 2220 us -> 50.5 us
  blocking collectives: 600 us -> 0 us
  Pallas kernels: 0 us -> 313 us
  local copies, waits for them, and re-layouts: 332 us -> 59.5 us
  matrix products: 164 us -> 0 us
  other arithmetic: 98.6 us -> 23.8 us
  starting transfers between devices: 4.27 us -> 48.2 us
    unnamed x25 -> x0, waiting for transfers between devices: 1560 us -> none
    all_gather x8 -> x0, waiting for transfers between devices: 652 us -> none  [the longest x2 203 us: first_section_back(): grad_all = lax.all_gather(grad_quarter, 'row', axis=0, tiled=True)]
    unnamed x2 -> x0, blocking collectives: 448 us -> none
    pallas_call x0 -> x2, Pallas kernels: none -> 313 us  [the longest x1 162 us: forward_call(): pl.pallas_call(forward_kernel, out_shape=[jax.ShapeDtypeStruct(shape, dty...]
    dot_general x26 -> x0, matrix products: 164 us -> none  [the longest x4 44 us: partial_term(): return jnp.dot(gathered, weight, preferred_element_type=jnp.float32)]
    unnamed x82 -> x53, local copies, waits for them, and re-layouts: 163 us -> 2.56 us
    psum x6 -> x0, blocking collectives: 151 us -> none  [the longest x2 85.5 us: on_device(): lax.psum((err_part, count_part), ('dp', 'row', 'col'))]
    all_gather x7 -> x0, local copies, waits for them, and re-layouts: 117 us -> none  [the longest x2 48.7 us: second_section(): gathered = lax.all_gather(quarter_rows, 'row', axis=0, tiled=True)]
  transfers between devices with their start and end apart: 19 -> 42, of which waited for: 15 -> 22; matrix products, arithmetic and copies ran while one was open for 3% -> 14% of each run, Pallas kernels for 0% -> 0%
where the time goes in v2:
time: 513 us; the launch traced here: 503 us
  Pallas kernels  313 us (61%)
  local copies, waits for them, and re-layouts  59.5 us (12%)
  waiting for transfers between devices  50.5 us (10%)
  starting transfers between devices  48.2 us (9%)
  other arithmetic  23.8 us (5%)
  between operations  8.21 us (2%)
    pallas_call x1, Pallas kernels, forward_call(): pl.pallas_call(forward_kernel, out_shape=[jax.ShapeDtypeStruct(shape, dty...  162 us
    pallas_call x1, Pallas kernels, backward_call(): pl.pallas_call(backward_kernel, out_shape=[jax.ShapeDtypeStruct(shape, dt...  151 us
    ppermute x21, waiting for transfers between devices, row_swap(): lax.ppermute(values, 'row', [(i, i ^ bit) for i in range(lax.axis_size('r...  33.1 us
    ppermute x21, starting transfers between devices, row_swap(): lax.ppermute(values, 'row', [(i, i ^ bit) for i in range(lax.axis_size('r...  28.5 us
  transfers between devices with their start and end apart: 42, of which 22 were waited for; matrix products, arithmetic and copies ran while one was open for 14% of the time, Pallas kernels for 0%

profile of v2, /device:TPU:0, one launch (start us, length us, event | category | flops | bytes accessed | tf_op | source)
XLA Modules:
  0.0 503.5 jit_solution(16339835862801094913)
XLA Ops:
  4.9 3.0 collective-permute-start.10
  7.9 1.4 collective-permute-start.11
  12.4 2.0 collective-permute-start.12
  14.4 1.3 convert_reduce_fusion
  25.5 4.5 constant_dynamic-slice_fusion.19
  32.7 1.1 constant_dynamic-slice_fusion.14
  33.8 1.1 constant_dynamic-slice_fusion.20
  34.9 1.3 fusion.spread_ref
  36.3 1.1 constant_dynamic-slice_fusion.16
  42.5 4.0 collective-permute-start.16
  47.3 1.8 collective-permute-start.17
  49.1 2.6 collective-permute-done.17
  53.8 2.0 collective-permute-start.13
  56.1 2.4 collective-permute-done.13
  60.0 1.1 collective-permute-start.14
  62.6 1.9 collective-permute-done.14
  67.1 1.6 collective-permute-start.5
  68.9 1.6 collective-permute-start.6
  72.0 1.6 collective-permute-start.1
  74.1 1.6 collective-permute-start.2
  75.6 1.6 collective-permute-done.5
  77.2 2.4 collective-permute-start.3
  82.3 2.9 collective-permute-done.6
  85.2 2.6 concatenate.143.teacher_ref
  87.8 2.0 collective-permute-done.1
  89.8 5.7 %collective-permute-done.2 = bf16[384,288]{1,0:T(8,128)(2,1)S(1)} collective-permute-done((bf16[384,288]{1,0:T(8,128)(2,1)S(1)}, bf16[384,288]{1,0:T(8,128)(2,1)S(1)}, u32[]{:S(2)}, u32[]{:S(2)}) %collective-permute-start.2) | collective-permute-done | bytes 221216 | tf_op jit(solution)/shard_map/ppermute | solution.py:309
  95.5 1.4 concatenate.141.x_ref
  97.5 162.2 %shard_map.279 = (bf16[4,1152,1024]{2,1,0:T(8,128)(2,1)}, bf16[4,1152,1024]{2,1,0:T(8,128)(2,1)}, bf16[4,768,768]{2,1,0:T(8,128)(2,1)}, bf16[4,768,256]{2,1,0:T(...) custom-call(bf16[384,1152]{1,0:T(8,128)(2,1)} %concatenate.141.x_ref, ...), custom_call_target="tpu_custom_call" | custom-call | tf_op jit(solution)/shard_map/pallas_call | solution.py:745
  259.7 151.0 %shard_map.280 = (bf16[384,1152]{1,0:T(8,128)(2,1)}, f32[6,16,1152]{2,1,0:T(8,128)}, f32[4,1,512]{2,1,0:T(1,128)}, f32[1,128]{1,0:T(1,128)}, f32[4,1,768]{2,1,0:...) custom-call(bf16[768,1152]{1,0:T(8,128)(2,1)} %get-tuple-element.42.branch2_ref, ...), custom_call_target="tpu_custom_call" | custom-call | tf_op jit(solution)/shard_map/pallas_call | solution.py:1135
  410.7 1.8 constant_dynamic-slice_fusion
  416.2 1.4 fusion.43
  417.6 1.7 collective-permute-start.34
  419.3 1.1 slice_bitcast_fusion
  421.9 2.6 collective-permute-start.35
  426.8 2.0 collective-permute-start.22
  430.3 1.3 slice_bitcast_fusion.1
  431.7 1.6 collective-permute-done.36
  435.5 3.4 collective-permute-start.25
  439.2 2.0 collective-permute-start.29
  441.9 2.0 collective-permute-start.38
  444.0 4.6 collective-permute-done.38
  448.9 3.4 collective-permute-done.23
  452.3 1.1 collective-permute-done.39
  453.4 1.0 collective-permute-start.26
  455.2 2.0 collective-permute-done.26
  457.2 1.2 collective-permute-done.41
  458.3 1.5 collective-permute-start.27
  459.8 3.1 collective-permute-done.27
  464.1 1.5 collective-permute-start.31
  469.4 2.0 collective-permute-start.19
  471.4 1.5 collective-permute-start.20
  472.9 1.9 collective-permute-done.31
  476.0 3.8 collective-permute-done.18
  479.9 1.3 collective-permute-done.19
  481.2 5.5 %collective-permute-done.20 = bf16[384,288]{1,0:T(8,128)(2,1)S(1)} collective-permute-done((bf16[384,288]{1,0:T(8,128)(2,1)}, bf16[384,288]{1,0:T(8,128)(2,1)S(1)}, u32[]{:S(2)}, u32[]{:S(2)}) %collective-permute-start.20) | collective-permute-done | bytes 221216 | tf_op jit(solution)/shard_map/ppermute | solution.py:309
  486.7 1.2 pad_maximum_fusion
  489.4 1.0 fusion.40
  490.6 1.0 maximum_convert_fusion.1
  491.6 1.0 maximum_convert_fusion
  492.5 1.1 fusion.1
  494.0 1.4 copy.148
  495.3 2.7 reshape.730
  498.1 1.1 fusion.3
  500.3 1.6 reshape.724
  (251 shorter events, 56.1 us)
Async XLA Ops:
  0.6 17.7 %copy-start = (bf16[1076,288]{0,1:T(8,128)(2,1)S(1)}, bf16[1076,288]{0,1:T(8,128)(2,1)}, u32[]{:S(2)}) copy-start(bf16[1076,288]{0,1:T(8,128)(2,1)} %param.30) | copy-start | bytes 1859332
  0.7 21.3 %copy-start.6 = (bf16[1458,288]{0,1:T(8,128)(2,1)S(1)}, bf16[1458,288]{0,1:T(8,128)(2,1)}, u32[]{:S(2)}) copy-start(bf16[1458,288]{0,1:T(8,128)(2,1)} %param.16) | copy-start | bytes 2519428
  4.9 54.6 %collective-permute-start.10 = (bf16[6,288]{1,0:T(8,128)(2,1)S(1)}, bf16[6,288]{1,0:T(8,128)(2,1)}, u32[]{:S(2)}, u32[]{:S(2)}) collective-permute-start(bf16[6,288]{1,0:T(8,128)(2,1)S(1)} %stack.118), channel_id=1, source_target_pairs={{0,8},{4,12},{8,0},{12,4},{1,9},{5,13},{9,1},{13,5},{2,10},{6,14},... | collective-permute-start | bytes 10376 | tf_op jit(solution)/shard_map/ppermute | solution.py:309
  7.9 52.1 %collective-permute-start.11 = (bf16[6,288]{1,0:T(8,128)(2,1)S(1)}, bf16[6,288]{1,0:T(8,128)(2,1)}, u32[]{:S(2)}, u32[]{:S(2)}) collective-permute-start(bf16[6,288]{1,0:T(8,128)(2,1)S(1)} %stack.118), channel_id=1, source_target_pairs={{0,12},{4,8},{8,4},{12,0},{1,13},{5,9},{9,5},{13,1},{2,14},{6,10},... | collective-permute-start | bytes 10376 | tf_op jit(solution)/shard_map/ppermute | solution.py:309
  9.4 51.7 %collective-permute-start.9 = (bf16[6,288]{1,0:T(8,128)(2,1)S(1)}, bf16[6,288]{1,0:T(8,128)(2,1)}, u32[]{:S(2)}, u32[]{:S(2)}) collective-permute-start(bf16[6,288]{1,0:T(8,128)(2,1)S(1)} %stack.118), channel_id=1, source_target_pairs={{0,4},{4,0},{8,12},{12,8},{1,5},{5,1},{9,13},{13,9},{2,6},{6,2},{1... | collective-permute-start | bytes 10376 | tf_op jit(solution)/shard_map/ppermute | solution.py:309
  12.4 40.1 %collective-permute-start.12 = (bf16[1,826]{1,0:T(2,128)(2,1)}, bf16[1,826]{1,0:T(2,128)(2,1)}, u32[]{:S(2)}, u32[]{:S(2)}) collective-permute-start(bf16[1,826]{1,0:T(2,128)(2,1)} %broadcast_in_dim.35), channel_id=1, source_target_pairs={{0,1},{1,3},{3,2},{2,0},{4,5},{5,7},{7,6},{6,4},{8,9},{9,11},{11,1... | collective-permute-start | bytes 4964 | tf_op jit(solution)/shard_map/ppermute | solution.py:319
  15.7 25.4 %collective-permute-start.15 = (f32[1,1]{1,0:T(1,128)}, f32[1,1]{1,0:T(1,128)}, u32[]{:S(2)}, u32[]{:S(2)}) collective-permute-start(f32[1,1]{1,0:T(1,128)} %bitcast.23), channel_id=1, source_target_pairs={{0,16},{16,0},{1,17},{17,1},{2,18},{18,2},{3,19},{19,3},{4,20},{20... | collective-permute-start | bytes 20 | tf_op jit(solution)/shard_map/ppermute | solution.py:305
  30.0 2.0 copy-start.19
  30.0 2.7 copy-start.14
  30.8 4.1 copy-start.15
  33.8 3.6 copy-start.5
  37.4 2.8 copy-start.11
  38.3 26.5 %copy-start.17 = (f32[2,1,72]{2,1,0:T(1,128)S(1)}, f32[2,1,72]{2,1,0:T(1,128)}, u32[]{:S(2)}) copy-start(f32[2,1,72]{2,1,0:T(1,128)} %stack_reshape.24) | copy-start | bytes 1732
  38.3 26.5 %copy-start.18 = (f32[2,1,72]{2,1,0:T(1,128)S(1)}, f32[2,1,72]{2,1,0:T(1,128)}, u32[]{:S(2)}) copy-start(f32[2,1,72]{2,1,0:T(1,128)} %stack_reshape.25) | copy-start | bytes 1732
  38.3 27.4 %copy-start.16 = (f32[512]{0:T(512)S(1)}, f32[512]{0:T(512)}, u32[]{:S(2)}) copy-start(f32[512]{0:T(512)} %slice.267) | copy-start | bytes 6148
  42.5 4.1 collective-permute-start.16
  47.3 4.5 collective-permute-start.17
  51.8 14.6 %collective-permute-start.4 = (bf16[2,384,288]{1,2,0:T(8,128)(2,1)}, bf16[2,384,288]{1,2,0:T(8,128)(2,1)S(1)}, u32[]{:S(2)}, u32[]{:S(2)}) collective-permute-start(bf16[2,384,288]{1,2,0:T(8,128)(2,1)} %bitcast.152), channel_id=1, source_target_pairs={{0,16},{16,0},{1,17},{17,1},{2,18},{18,2},{3,19},{19,3},{4,20},{20... | collective-permute-start | bytes 1327112 | tf_op jit(solution)/shard_map/ppermute | solution.py:305
  53.8 4.7 collective-permute-start.13
  58.6 12.7 %collective-permute-start = (bf16[2,384,288]{1,2,0:T(8,128)(2,1)S(1)}, bf16[2,384,288]{1,2,0:T(8,128)(2,1)S(1)}, u32[]{:S(2)}, u32[]{:S(2)}) collective-permute-start(bf16[2,384,288]{1,2,0:T(8,128)(2,1)S(1)} %bitcast.151), channel_id=1, source_target_pairs={{0,16},{16,0},{1,17},{17,1},{2,18},{18,2},{3,19},{19,3},{4,20},{20... | collective-permute-start | bytes 1327112 | tf_op jit(solution)/shard_map/ppermute | solution.py:305
  59.5 14.6 %collective-permute-start.8 = (s32[2,768]{1,0:T(2,128)}, s32[2,768]{1,0:T(2,128)}, u32[]{:S(2)}, u32[]{:S(2)}) collective-permute-start(s32[2,768]{1,0:T(2,128)} %pad.37), channel_id=1, source_target_pairs={{0,16},{16,0},{1,17},{17,1},{2,18},{18,2},{3,19},{19,3},{4,20},{20... | collective-permute-start | bytes 18440 | tf_op jit(solution)/shard_map/ppermute | solution.py:305
  60.0 4.5 collective-permute-start.14
  67.1 10.1 %collective-permute-start.5 = (bf16[384,288]{1,0:T(8,128)(2,1)S(1)}, bf16[384,288]{1,0:T(8,128)(2,1)}, u32[]{:S(2)}, u32[]{:S(2)}) collective-permute-start(bf16[384,288]{1,0:T(8,128)(2,1)S(1)} %bitcast.163), channel_id=1, source_target_pairs={{0,4},{4,0},{8,12},{12,8},{1,5},{5,1},{9,13},{13,9},{2,6},{6,2},{1... | collective-permute-start | bytes 663560 | tf_op jit(solution)/shard_map/ppermute | solution.py:309
  68.9 16.3 %collective-permute-start.6 = (bf16[384,288]{1,0:T(8,128)(2,1)S(1)}, bf16[384,288]{1,0:T(8,128)(2,1)}, u32[]{:S(2)}, u32[]{:S(2)}) collective-permute-start(bf16[384,288]{1,0:T(8,128)(2,1)S(1)} %bitcast.158), channel_id=1, source_target_pairs={{0,8},{4,12},{8,0},{12,4},{1,9},{5,13},{9,1},{13,5},{2,10},{6,14},... | collective-permute-start | bytes 663560 | tf_op jit(solution)/shard_map/ppermute | solution.py:309
  70.7 14.5 %collective-permute-start.7 = (bf16[384,288]{1,0:T(8,128)(2,1)S(1)}, bf16[384,288]{1,0:T(8,128)(2,1)}, u32[]{:S(2)}, u32[]{:S(2)}) collective-permute-start(bf16[384,288]{1,0:T(8,128)(2,1)S(1)} %bitcast.159), channel_id=1, source_target_pairs={{0,12},{4,8},{8,4},{12,0},{1,13},{5,9},{9,5},{13,1},{2,14},{6,10},... | collective-permute-start | bytes 663560 | tf_op jit(solution)/shard_map/ppermute | solution.py:309
  71.8 7.9 %copy-start.22 = (f32[26]{0:T(128)S(1)}, f32[26]{0:T(128)}, u32[]{:S(2)}) copy-start(f32[26]{0:T(128)} %slice.271) | copy-start | bytes 316
  71.8 7.9 %copy-start.23 = (f32[26]{0:T(128)S(1)}, f32[26]{0:T(128)}, u32[]{:S(2)}) copy-start(f32[26]{0:T(128)} %slice_bitcast_fusion.11) | copy-start | bytes 316
  71.8 7.9 %copy-start.24 = (f32[26]{0:T(128)S(1)}, f32[26]{0:T(128)}, u32[]{:S(2)}) copy-start(f32[26]{0:T(128)} %slice_bitcast_fusion.10) | copy-start | bytes 316
  72.0 17.8 %collective-permute-start.1 = (bf16[384,288]{1,0:T(8,128)(2,1)S(1)}, bf16[384,288]{1,0:T(8,128)(2,1)S(1)}, u32[]{:S(2)}, u32[]{:S(2)}) collective-permute-start(bf16[384,288]{1,0:T(8,128)(2,1)S(1)} %bitcast.160), channel_id=1, source_target_pairs={{0,4},{4,0},{8,12},{12,8},{1,5},{5,1},{9,13},{13,9},{2,6},{6,2},{1... | collective-permute-start | bytes 663560 | tf_op jit(solution)/shard_map/ppermute | solution.py:309
  74.1 21.4 %collective-permute-start.2 = (bf16[384,288]{1,0:T(8,128)(2,1)S(1)}, bf16[384,288]{1,0:T(8,128)(2,1)S(1)}, u32[]{:S(2)}, u32[]{:S(2)}) collective-permute-start(bf16[384,288]{1,0:T(8,128)(2,1)S(1)} %bitcast.162), channel_id=1, source_target_pairs={{0,8},{4,12},{8,0},{12,4},{1,9},{5,13},{9,1},{13,5},{2,10},{6,14},... | collective-permute-start | bytes 663560 | tf_op jit(solution)/shard_map/ppermute | solution.py:309
  77.2 18.2 %collective-permute-start.3 = (bf16[384,288]{1,0:T(8,128)(2,1)S(1)}, bf16[384,288]{1,0:T(8,128)(2,1)S(1)}, u32[]{:S(2)}, u32[]{:S(2)}) collective-permute-start(bf16[384,288]{1,0:T(8,128)(2,1)S(1)} %bitcast.161), channel_id=1, source_target_pairs={{0,12},{4,8},{8,4},{12,0},{1,13},{5,9},{9,5},{13,1},{2,14},{6,10},... | collective-permute-start | bytes 663560 | tf_op jit(solution)/shard_map/ppermute | solution.py:309
  410.7 8.6 %copy-start.4 = (bf16[384,1152]{1,0:T(8,128)(2,1)S(1)}, bf16[384,1152]{1,0:T(8,128)(2,1)}, u32[]{:S(2)}) copy-start(bf16[384,1152]{1,0:T(8,128)(2,1)} %get-tuple-element.60) | copy-start | bytes 2654212
  412.5 76.9 %collective-permute-start.40 = (bf16[144,1024]{1,0:T(8,128)(2,1)}, bf16[144,1024]{1,0:T(8,128)(2,1)}, u32[]{:S(2)}, u32[]{:S(2)}) collective-permute-start(bf16[144,1024]{1,0:T(8,128)(2,1)} %constant_dynamic-slice_fusion), channel_id=1, source_target_pairs={{0,16},{16,0},{1,17},{17,1},{2,18},{18,2},{3,19},{19,3},{4,20},{20... | collective-permute-start | bytes 884744 | tf_op jit(solution)/shard_map/ppermute | solution.py:305
  413.5 54.0 %collective-permute-start.33 = (bf16[144,640]{1,0:T(8,128)(2,1)S(1)}, bf16[144,640]{1,0:T(8,128)(2,1)S(1)}, u32[]{:S(2)}, u32[]{:S(2)}) collective-permute-start(bf16[144,640]{1,0:T(8,128)(2,1)S(1)} %constant_dynamic-slice_fusion.1), channel_id=1, source_target_pairs={{0,16},{16,0},{1,17},{17,1},{2,18},{18,2},{3,19},{19,3},{4,20},{20... | collective-permute-start | bytes 552968 | tf_op jit(solution)/shard_map/ppermute | solution.py:305
  417.6 3.6 collective-permute-start.34
  419.3 5.2 %copy-start.9 = (bf16[288,1024]{1,0:T(8,128)(2,1)S(1)}, bf16[288,1024]{1,0:T(8,128)(2,1)}, u32[]{:S(2)}) copy-start(bf16[288,1024]{1,0:T(8,128)(2,1)} %get-tuple-element.65) | copy-start | bytes 1769476
  419.3 6.7 %copy-start.13 = (f32[16,1152]{1,0:T(8,128)S(1)}, f32[16,1152]{1,0:T(8,128)}, u32[]{:S(2)}) copy-start(f32[16,1152]{1,0:T(8,128)} %get-tuple-element.59) | copy-start | bytes 221188
  419.3 7.3 %copy-start.10 = (f32[6,16,1152]{2,1,0:T(8,128)S(1)}, f32[6,16,1152]{2,1,0:T(8,128)}, u32[]{:S(2)}) copy-start(f32[6,16,1152]{2,1,0:T(8,128)} %get-tuple-element.58) | copy-start | bytes 1327108
  420.4 9.9 %copy-start.3 = (bf16[384,1152]{1,0:T(8,128)(2,1)S(1)}, bf16[384,1152]{1,0:T(8,128)(2,1)}, u32[]{:S(2)}) copy-start(bf16[384,1152]{1,0:T(8,128)(2,1)} %get-tuple-element.41) | copy-start | bytes 2654212
  421.9 6.9 %collective-permute-start.35 = (f32[1,826]{1,0:T(1,128)}, f32[1,826]{1,0:T(1,128)}, u32[]{:S(2)}, u32[]{:S(2)}) collective-permute-start(f32[1,826]{1,0:T(1,128)} %maximum_add_fusion.2), channel_id=1, source_target_pairs={{0,2},{1,0},{3,1},{2,3},{4,6},{5,4},{7,5},{6,7},{8,10},{9,8},{11,9... | collective-permute-start | bytes 9920 | tf_op jit(solution)/shard_map/ppermute | solution.py:319
  426.6 7.6 %collective-permute-start.24 = (f32[1,1]{1,0:T(1,128)}, f32[1,1]{1,0:T(1,128)}, u32[]{:S(2)}, u32[]{:S(2)}) collective-permute-start(f32[1,1]{1,0:T(1,128)} %bitcast.36), channel_id=1, source_target_pairs={{0,4},{4,0},{8,12},{12,8},{1,5},{5,1},{9,13},{13,9},{2,6},{6,2},{1... | collective-permute-start | bytes 20 | tf_op jit(solution)/shard_map/ppermute | solution.py:309
  426.8 15.2 %collective-permute-start.22 = (f32[6,576]{1,0:T(8,128)S(1)}, f32[6,576]{1,0:T(8,128)S(1)}, u32[]{:S(2)}, u32[]{:S(2)}) collective-permute-start(f32[6,576]{1,0:T(8,128)S(1)} %slice.353), channel_id=1, source_target_pairs={{0,8},{4,12},{8,0},{12,4},{1,9},{5,13},{9,1},{13,5},{2,10},{6,14},... | collective-permute-start | bytes 41480 | tf_op jit(solution)/shard_map/ppermute | solution.py:309
  429.5 3.9 collective-permute-start.36
  430.3 3.1 copy-start.21
  430.3 3.2 copy-start.8
  433.5 8.3 %collective-permute-start.37 = (f32[1,826]{1,0:T(1,128)S(1)}, f32[1,826]{1,0:T(1,128)S(1)}, u32[]{:S(2)}, u32[]{:S(2)}) collective-permute-start(f32[1,826]{1,0:T(1,128)S(1)} %maximum_add_fusion), channel_id=1, source_target_pairs={{0,4},{4,0},{8,12},{12,8},{1,5},{5,1},{9,13},{13,9},{2,6},{6,2},{1... | collective-permute-start | bytes 9920 | tf_op jit(solution)/shard_map/ppermute | solution.py:309
  435.5 3.7 collective-permute-start.25
  439.2 30.2 %collective-permute-start.29 = (bf16[384,288]{1,0:T(8,128)(2,1)}, bf16[384,288]{1,0:T(8,128)(2,1)S(1)}, u32[]{:S(2)}, u32[]{:S(2)}) collective-permute-start(bf16[384,288]{1,0:T(8,128)(2,1)} %get-tuple-element.109), channel_id=1, source_target_pairs={{0,4},{4,0},{8,12},{12,8},{1,5},{5,1},{9,13},{13,9},{2,6},{6,2},{1... | collective-permute-start | bytes 663560 | tf_op jit(solution)/shard_map/ppermute | solution.py:309
  441.8 29.7 %collective-permute-start.30 = (bf16[384,288]{1,0:T(8,128)(2,1)S(1)}, bf16[384,288]{1,0:T(8,128)(2,1)S(1)}, u32[]{:S(2)}, u32[]{:S(2)}) collective-permute-start(bf16[384,288]{1,0:T(8,128)(2,1)S(1)} %get-tuple-element.108), channel_id=1, source_target_pairs={{0,8},{4,12},{8,0},{12,4},{1,9},{5,13},{9,1},{13,5},{2,10},{6,14},... | collective-permute-start | bytes 663560 | tf_op jit(solution)/shard_map/ppermute | solution.py:309
  441.9 6.7 %collective-permute-start.38 = (f32[1,826]{1,0:T(1,128)S(1)}, f32[1,826]{1,0:T(1,128)S(1)}, u32[]{:S(2)}, u32[]{:S(2)}) collective-permute-start(f32[1,826]{1,0:T(1,128)S(1)} %add.378), channel_id=1, source_target_pairs={{0,8},{4,12},{8,0},{12,4},{1,9},{5,13},{9,1},{13,5},{2,10},{6,14},... | collective-permute-start | bytes 9920 | tf_op jit(solution)/shard_map/ppermute | solution.py:309
  448.6 3.7 collective-permute-start.23
  452.3 1.2 collective-permute-start.39
  453.4 3.7 collective-permute-start.26
  457.1 1.2 collective-permute-start.41
  458.3 4.6 collective-permute-start.27
  462.9 1.2 collective-permute-start.28
  464.1 10.8 %collective-permute-start.31 = (bf16[384,288]{1,0:T(8,128)(2,1)S(1)}, bf16[384,288]{1,0:T(8,128)(2,1)S(1)}, u32[]{:S(2)}, u32[]{:S(2)}) collective-permute-start(bf16[384,288]{1,0:T(8,128)(2,1)S(1)} %get-tuple-element.107), channel_id=1, source_target_pairs={{0,12},{4,8},{8,4},{12,0},{1,13},{5,9},{9,5},{13,1},{2,14},{6,10},... | collective-permute-start | bytes 663560 | tf_op jit(solution)/shard_map/ppermute | solution.py:309
  467.4 12.5 %collective-permute-start.18 = (bf16[384,288]{1,0:T(8,128)(2,1)}, bf16[384,288]{1,0:T(8,128)(2,1)}, u32[]{:S(2)}, u32[]{:S(2)}) collective-permute-start(bf16[384,288]{1,0:T(8,128)(2,1)} %get-tuple-element.115), channel_id=1, source_target_pairs={{0,4},{4,0},{8,12},{12,8},{1,5},{5,1},{9,13},{13,9},{2,6},{6,2},{1... | collective-permute-start | bytes 663560 | tf_op jit(solution)/shard_map/ppermute | solution.py:309
  469.4 11.7 %collective-permute-start.19 = (bf16[384,288]{1,0:T(8,128)(2,1)}, bf16[384,288]{1,0:T(8,128)(2,1)S(1)}, u32[]{:S(2)}, u32[]{:S(2)}) collective-permute-start(bf16[384,288]{1,0:T(8,128)(2,1)} %get-tuple-element.114), channel_id=1, source_target_pairs={{0,8},{4,12},{8,0},{12,4},{1,9},{5,13},{9,1},{13,5},{2,10},{6,14},... | collective-permute-start | bytes 663560 | tf_op jit(solution)/shard_map/ppermute | solution.py:309
  471.4 15.3 %collective-permute-start.20 = (bf16[384,288]{1,0:T(8,128)(2,1)}, bf16[384,288]{1,0:T(8,128)(2,1)S(1)}, u32[]{:S(2)}, u32[]{:S(2)}) collective-permute-start(bf16[384,288]{1,0:T(8,128)(2,1)} %get-tuple-element.113), channel_id=1, source_target_pairs={{0,12},{4,8},{8,4},{12,0},{1,13},{5,9},{9,5},{13,1},{2,14},{6,10},... | collective-permute-start | bytes 663560 | tf_op jit(solution)/shard_map/ppermute | solution.py:309
  475.9 16.6 %collective-permute-start.32 = (bf16[2,384,288]{1,2,0:T(8,128)(2,1)S(1)}, bf16[2,384,288]{1,2,0:T(8,128)(2,1)}, u32[]{:S(2)}, u32[]{:S(2)}) collective-permute-start(bf16[2,384,288]{1,2,0:T(8,128)(2,1)S(1)} %bitcast.149), channel_id=1, source_target_pairs={{0,16},{16,0},{1,17},{17,1},{2,18},{18,2},{3,19},{19,3},{4,20},{20... | collective-permute-start | bytes 1327112 | tf_op jit(solution)/shard_map/ppermute | solution.py:305
  488.8 1.7 copy-start.12
  489.1 9.0 %collective-permute-start.21 = (bf16[2,384,288]{1,2,0:T(8,128)(2,1)S(1)}, bf16[2,384,288]{1,2,0:T(8,128)(2,1)}, u32[]{:S(2)}, u32[]{:S(2)}) collective-permute-start(bf16[2,384,288]{1,2,0:T(8,128)(2,1)S(1)} %bitcast.150), channel_id=1, source_target_pairs={{0,16},{16,0},{1,17},{17,1},{2,18},{18,2},{3,19},{19,3},{4,20},{20... | collective-permute-start | bytes 1327112 | tf_op jit(solution)/shard_map/ppermute | solution.py:305
  499.4 2.5 copy-start.1
  (3 other events, 3.9 us)

commit v3 on v2

--- a/solution.py
+++ b/solution.py
@@ -1,3 +1,5 @@
+import functools
+
 import jax
 import jax.numpy as jnp
 from jax import lax
@@ -301,33 +303,6 @@
     )
 
 
-def pair_swap(values):
-    return lax.ppermute(values, "dp", [(0, 1), (1, 0)])
-
-
-def row_swap(values, bit):
-    return lax.ppermute(values, "row", [(i, i ^ bit) for i in range(lax.axis_size("row"))])
-
-
-def ring_order(size):
-    return [0, 1, 3, 2] if size == 4 else list(range(size))
-
-
-def ring_shift(values, step):
-    order = ring_order(lax.axis_size("col"))
-    size = len(order)
-    return lax.ppermute(
-        values, "col", [(order[i], order[(i + step) % size]) for i in range(size)]
-    )
-
-
-def gather_ring(shard):
-    shards = [shard]
-    for _ in range(lax.axis_size("col") - 1):
-        shards.append(ring_shift(shards[-1], 1))
-    return shards
-
-
 MESH = pl.DeviceIdType.MESH
 F32 = jnp.float32
 BF16 = jnp.bfloat16
@@ -335,22 +310,109 @@
 GELU_ROOT = 0.7978845608028654
 
 
+def place():
+    return lax.axis_index("dp"), lax.axis_index("row"), lax.axis_index("col")
+
+
+def flip(row, other):
+    return lax.rem(row // 2 + other // 2, 2) * 2 + lax.rem(row + other, 2)
+
+
 def neighbours():
-    dp, row, col = lax.axis_index("dp"), lax.axis_index("row"), lax.axis_index("col")
+    dp, row, col = place()
     return dict(
         core=(1 - dp, row, col),
-        x=(dp, row + 1 - 2 * lax.rem(row, 2), col),
-        y=(dp, lax.rem(row + 2, 4), col),
+        x=(dp, flip(row, 1), col),
+        y=(dp, flip(row, 2), col),
+        diagonal=(dp, flip(row, 3), col),
         next=(dp, row, lax.rem(2 * col + 3 * (col // 2) + 1, 4)),
         prev=(dp, row, lax.rem(2 * col + col // 2 + 2, 4)),
     )
 
 
-def meet(peers):
+def images_group():
+    dp, row, col = place()
+    steps = [(core, step) for core in (0, 1) for step in range(4)][1:]
+    return [(lax.rem(dp + core, 2), row, lax.rem(col + step, 4)) for core, step in steps]
+
+
+def meet():
+    dp, row, col = place()
+    plane = [(core, k) for core in (0, 1) for k in range(4)][1:]
+    peers = [(lax.rem(dp + core, 2), flip(row, k), col) for core, k in plane]
+    peers += [peer for i, peer in enumerate(images_group()) if i != 3]
     barrier = pltpu.get_barrier_semaphore()
-    for peer in peers.values():
+    for peer in peers:
         pl.semaphore_signal(barrier, inc=1, device_id=peer, device_id_type=MESH)
     pl.semaphore_wait(barrier, len(peers))
+
+
+class Shuffle:
+    def __init__(self, send_sems, recv_sems, local_sem):
+        self.sems = send_sems, recv_sems, local_sem
+        self.pending = []
+
+    def remote(self, source, target, i, slot, peer):
+        return pltpu.make_async_remote_copy(
+            source, target, self.sems[0].at[i], self.sems[1].at[slot],
+            device_id=peer, device_id_type=MESH,
+        )
+
+    def spread(self, pieces, blocks):
+        dp, row, col = place()
+        for image in (0, 1):
+            for half in (0, 1):
+                chip = 2 * dp + image
+                slot = flip(chip, row)
+                mine = (dp == half) & (chip == row)
+                index = 2 * image + half
+                copy = self.remote(
+                    pieces.at[image, half], blocks.at[slot], index, slot, (half, chip, col)
+                )
+                here = pltpu.make_async_copy(
+                    pieces.at[image, half], blocks.at[0], self.sems[2]
+                )
+                self.start(copy, here, mine)
+        own = dp == row // 2
+        self.into = [(blocks.at[k], k, own if k == 0 else None) for k in range(4)]
+
+    def collect(self, blocks, pieces):
+        dp, row, col = place()
+        image = lax.rem(row, 2)
+        for k in range(4):
+            owner = flip(row, k)
+            index = 2 * image + dp
+            mine = (dp == row // 2) & (owner == row)
+            copy = self.remote(
+                blocks.at[k], pieces.at[image, dp], k, index, (row // 2, owner, col)
+            )
+            here = pltpu.make_async_copy(blocks.at[k], pieces.at[image, dp], self.sems[2])
+            self.start(copy, here, mine)
+        self.into = []
+        for image in (0, 1):
+            for half in (0, 1):
+                own = (dp == half) & (2 * dp + image == row)
+                self.into.append((pieces.at[image, half], 2 * image + half, own))
+
+    def start(self, copy, here, mine):
+        pl.when(jnp.logical_not(mine))(copy.start)
+        pl.when(mine)(here.start)
+        self.pending.append((copy, here, mine))
+
+    def arrive(self):
+        dp, row, col = place()
+        here = self.pending[0][1]
+        for target, slot, own in self.into:
+            copy = self.remote(target, target, 0, slot, (1 - dp, row, col))
+            if own is None:
+                copy.wait_recv()
+            else:
+                pl.when(jnp.logical_not(own))(copy.wait_recv)
+                pl.when(own)(here.wait)
+
+    def finish(self):
+        for copy, _, mine in self.pending:
+            pl.when(jnp.logical_not(mine))(copy.wait_send)
 
 
 def mm(left, right):
@@ -419,16 +481,13 @@
 
 
 def forward_kernel(
-    x_ref,
-    teacher_ref,
-    mask_ref,
+    own_tokens,
+    x_pieces,
+    teacher_pieces,
+    count_ref,
+    params_ref,
     key_ref,
-    feature_ref,
-    qkv_bias_ref,
     key_lane_ref,
-    up_bias_ref,
-    rest_bias_ref,
-    factor_ref,
     spread_ref,
     rest_spread_ref,
     attn_ref,
@@ -451,6 +510,13 @@
     brancht_out,
     result_out,
     err_out,
+    x_ref,
+    feature_ref,
+    count_out,
+    teacher_ref,
+    features_in,
+    biases_in,
+    counts_in,
     wattn,
     wff,
     wpad,
@@ -467,9 +533,10 @@
     local_sems,
     send_sems,
     recv_sems,
+    shuffle_sems,
 ):
     peers = neighbours()
-    meet(peers)
+    meet()
     feat = attn_ref.shape[0]
     half = feat // 2
     depth = 4 * feat
@@ -477,6 +544,8 @@
     own = tokens // 2
     main = ff_ref.shape[1] // 2
     qkv = triple.shape[2]
+    wide = features_in.shape[2]
+    pitch = wide // 6
     send = Sender(send_sems, recv_sems)
     keep = Copier(local_sems)
 
@@ -556,7 +625,7 @@
         each_rows(depth, feat, unpack)
 
         def project(at):
-            values = mm(norm1[at, :], wpad[slot, :, :qkv]) + qkv_bias_ref[s]
+            values = mm(norm1[at, :], wpad[slot, :, :qkv]) + biases_in[s, 0:1, :qkv]
             values = values + key_ref[at, :] * key_lane_ref[...]
             triple[slot, at, :] = values.astype(BF16)
 
@@ -601,7 +670,7 @@
         arrive(fy[s] + fx[s])
 
         def block(at):
-            pre = mm(norm2[at, :], wff[s, :, :main]) + up_bias_ref[s]
+            pre = mm(norm2[at, :], wff[s, :, :main]) + biases_in[s, 0:1, qkv : qkv + main]
             low, bent = gelu(pre)
             act[s, at, :] = low
             slope[s, at, :] = bent
@@ -617,8 +686,13 @@
         )
 
     def rest_compute():
+        bias = mm(biases_in[0, :, qkv + main :].astype(BF16), rest_spread_ref[0, :, :128])
+        for s in (1, 2, 3):
+            values = biases_in[s, :, qkv + main :].astype(BF16)
+            bias = bias + mm(values, rest_spread_ref[s, :, :128])
+
         def block(at):
-            pre = mm(norm2[at, :], rest_out[:, :128]) + rest_bias_ref[...]
+            pre = mm(norm2[at, :], rest_out[:, :128]) + bias[0:1]
             low, bent = gelu(pre)
             act_rest_out[at, :] = low
             slope_rest_out[at, :] = bent
@@ -627,11 +701,45 @@
         each_rows(tokens, own, block)
 
     saved, ff_saved = [], []
+    x_move = Shuffle(shuffle_sems.at[0], shuffle_sems.at[1], shuffle_sems.at[2, 0])
+    x_move.spread(x_pieces, x_ref)
     attn_ring(0)
     attn_plane(0)
+    own_params = [
+        keep(params_ref.at[:, pl.ds(0, wide)], features_in.at[0]),
+        keep(params_ref.at[:, pl.ds(wide, biases_in.shape[2])], biases_in.at[0]),
+        keep(count_ref, counts_in.at[0]),
+    ]
+    smalls = [
+        send(params_ref.at[:, pl.ds(0, wide)], features_in.at[k], peers[name])
+        for k, name in ((1, "x"), (2, "y"), (3, "diagonal"))
+    ]
+    dp, row, col = place()
+    ring_two = (dp, row, 3 - col)
+    smalls += [
+        send(params_ref.at[:, pl.ds(wide, biases_in.shape[2])], biases_in.at[s], peer)
+        for s, peer in ((1, peers["next"]), (2, ring_two), (3, peers["prev"]))
+    ]
+    counts = [
+        send(count_ref, counts_in.at[1 + i], peer) for i, peer in enumerate(images_group())
+    ]
+    teacher_move = Shuffle(shuffle_sems.at[3], shuffle_sems.at[4], shuffle_sems.at[2, 1])
+
+    def token_rows(at):
+        return jnp.concatenate([x_ref[k, at, :].astype(F32) for k in range(4)], axis=1)
+
+    for copy in own_params:
+        copy.wait()
+    arrive(smalls)
+    feature_ref[...] = jnp.zeros_like(feature_ref)
+    for i in range(6):
+        feature_ref[i : i + 1, :] = jnp.concatenate(
+            [features_in[k, 0:1, pitch * i : pitch * i + feat] for k in range(4)], axis=1
+        )
+    x_move.arrive()
 
     def first_norm(at):
-        normed, _ = norm_stats(x_ref[at, :].astype(F32))
+        normed, _ = norm_stats(token_rows(at))
         norm1[at, :] = (normed * feature_ref[0:1] + feature_ref[1:2]).astype(BF16)
 
     each_rows(own, 16, first_norm)
@@ -653,6 +761,7 @@
     own_ff.wait()
     arrive(first)
     ff_ring(0)
+    teacher_move.spread(teacher_pieces, teacher_ref)
     attn_compute(1)
     attn_last(3)
     ff_last(0)
@@ -662,7 +771,7 @@
     arrive([swap2])
 
     def second_norm(at):
-        values = x_ref[at, :].astype(F32) + part[at, :] + got1[at, :] + feature_ref[4:5]
+        values = token_rows(at) + part[at, :] + got1[at, :] + feature_ref[4:5]
         resid_out[at, :] = values
         normed, _ = norm_stats(values)
         norm2[at, :] = (normed * feature_ref[2:3] + feature_ref[3:4]).astype(BF16)
@@ -692,14 +801,23 @@
     swap4 = send(part.at[pl.ds(own, own)], got2, peers["core"])
     arrive([swap4])
     err_out[...] = jnp.zeros_like(err_out)
+    teacher_move.arrive()
+    arrive(counts)
+    count = counts_in[0]
+    for i in range(1, 8):
+        count = count + counts_in[i]
+    count_out[...] = count
+    factor = (own_tokens * 8.0) / count[0:1, 0:1]
 
     def finish(at):
         values = resid_out[at, :] + part[at, :] + got2[at, :] + feature_ref[5:6]
-        result_out[at, :] = values.astype(BF16)
-        error = values - teacher_ref[at, :].astype(F32)
-        masked = error * mask_ref[at, :]
+        for k in range(4):
+            result_out[k, at, :] = values[:, k * feat : (k + 1) * feat].astype(BF16)
+        target = [teacher_ref[k, at, :feat].astype(F32) for k in range(4)]
+        error = values - jnp.concatenate(target, axis=1)
+        masked = error * teacher_ref[0, at, feat : feat + 1].astype(F32)
         err_out[...] = err_out[...] + error * masked
-        grad = masked * factor_ref[...]
+        grad = masked * factor
         grad_out[at, :] = grad
         branch_out[at, :] = grad.astype(BF16)
 
@@ -716,10 +834,13 @@
     for copy in send.copies:
         if copy is not swap2:
             copy.wait_send()
-
-
-def forward_call(arrays, feat, lanes, main, qkv, mix, own, depth):
+    x_move.finish()
+    teacher_move.finish()
+
+
+def forward_call(arrays, own_tokens, feat, lanes, main, qkv, mix, own, depth):
     tokens = 2 * own
+    wide, narrow = 6 * ((feat + 127) // 128 * 128), qkv + main + 128
     anywhere = pl.BlockSpec(memory_space=pl.ANY)
     local = pl.BlockSpec(memory_space=pltpu.VMEM)
     shapes = [
@@ -739,15 +860,22 @@
         ((own, depth), F32, local),
         ((tokens, depth), BF16, local),
         ((depth, tokens), BF16, local),
-        ((own, depth), BF16, local),
+        ((4, own, feat), BF16, local),
         ((16, depth), F32, local),
+        ((4, own, feat), BF16, local),
+        ((8, depth), F32, local),
+        ((8, 128), F32, local),
     ]
     return pl.pallas_call(
-        forward_kernel,
+        functools.partial(forward_kernel, own_tokens),
         out_shape=[jax.ShapeDtypeStruct(shape, dtype) for shape, dtype, _ in shapes],
-        in_specs=[local] * 12 + [anywhere] * 2,
+        in_specs=[anywhere] * 2 + [local] * 6 + [anywhere] * 2,
         out_specs=[spec for _, _, spec in shapes],
         scratch_shapes=[
+            pltpu.VMEM((4, own, arrays[1].shape[-1]), BF16),
+            pltpu.VMEM((4, 8, wide), F32),
+            pltpu.VMEM((4, 8, narrow), F32),
+            pltpu.VMEM((8, 8, 128), F32),
             pltpu.VMEM((4, depth, lanes), BF16),
             pltpu.VMEM((4, depth, 2 * main), BF16),
             pltpu.VMEM((2, depth, qkv + mix), BF16),
@@ -762,8 +890,9 @@
             pltpu.VMEM((own, depth), F32),
             pltpu.VMEM((own, depth), F32),
             pltpu.SemaphoreType.DMA((32,)),
-            pltpu.SemaphoreType.DMA((64,)),
-            pltpu.SemaphoreType.DMA((64,)),
+            pltpu.SemaphoreType.DMA((72,)),
+            pltpu.SemaphoreType.DMA((72,)),
+            pltpu.SemaphoreType.DMA((5, 4)),
         ],
         compiler_params=pltpu.CompilerParams(
             collective_id=1, has_side_effects=True, vmem_limit_bytes=62 << 20
@@ -782,6 +911,8 @@
     rest_spread_ref,
     x_ref,
     resid_ref,
+    err_ref,
+    result_blocks,
     grad_hbm,
     norm1t_hbm,
     norm2t_hbm,
@@ -792,13 +923,24 @@
     mixed_hbm,
     act_hbm,
     slope_hbm,
-    grad_in_out,
-    terms_out,
+    grad_pieces,
+    result_pieces,
+    sums_out,
+    bias_out,
+    attn_out,
+    ff_out,
+    grad_blocks,
+    terms,
+    terms_mine,
+    terms_in,
+    sums_in,
+    bias_mine,
+    bias_turn,
+    bias_in,
+    bias_plane,
     units_out,
     units_rest_out,
     heads_out,
-    attn_out,
-    ff_out,
     gattn,
     gff,
     wslot,
@@ -830,9 +972,10 @@
     local_sems,
     send_sems,
     recv_sems,
+    shuffle_sems,
 ):
     peers = neighbours()
-    feat = attn_out.shape[0]
+    feat = 2 * attn_out.shape[1]
     half = feat // 2
     depth = 4 * feat
     tokens = branch2_ref.shape[0]
@@ -865,7 +1008,9 @@
     turns = [keep(norm2t_hbm, normt), keep(branch2t_hbm, brancht)]
     loads[2] = load_ff(2)
     load_grad = keep(grad_hbm, grad_mid)
-    meet(peers)
+    meet()
+    result_move = Shuffle(shuffle_sems.at[0], shuffle_sems.at[1], shuffle_sems.at[2, 0])
+    grad_move = Shuffle(shuffle_sems.at[3], shuffle_sems.at[4], shuffle_sems.at[2, 1])
     cy, cx, zl, zh = ([None] * 4 for _ in range(4))
     ca, cb, c1, c2, cz = ([None] * 4 for _ in range(5))
 
@@ -1035,13 +1180,14 @@
         if s:
             cz[s - 1] = send(gattn.at[s, rows(0)], rz.at[s - 1], peers["prev"])
 
-    terms_out[...] = jnp.zeros_like(terms_out)
+    terms[...] = jnp.zeros_like(terms)
 
     def add_term(index, values):
-        terms_out[index] = terms_out[index] + values
+        terms[index] = terms[index] + values
 
     ff_compute(3)
     ff_compute(2)
+    result_move.collect(result_blocks, result_pieces)
     ff_compute(1)
     ff_add(3)
     ff_compute(0)
@@ -1088,8 +1234,11 @@
     attn_plane(0)
     swap3.wait_recv()
 
+    def token_rows(at):
+        return jnp.concatenate([x_ref[k, at, :].astype(F32) for k in range(4)], axis=1)
+
     def last(at):
-        normed, inv_scale = norm_stats(x_ref[at, :].astype(F32))
+        normed, inv_scale = norm_stats(token_rows(at))
         grad_norm = part[at, :] + got[at, :]
         add_term(0, grad_norm * normed)
         add_term(1, grad_norm)
@@ -1097,47 +1246,113 @@
         first = jnp.mean(scaled, axis=-1, keepdims=True)
         second = jnp.mean(scaled * normed, axis=-1, keepdims=True)
         grad = grad_mid[at, :] + inv_scale * (scaled - first - normed * second)
-        grad_in_out[at, :] = grad.astype(BF16)
+        for k in range(4):
+            grad_blocks[k, at, :] = grad[:, k * feat : (k + 1) * feat].astype(BF16)
 
     each_rows(own, 16, last)
+    grad_move.collect(grad_blocks, grad_pieces)
+    terms_mine[...] = jnp.zeros_like(terms_mine)
+    bias_mine[...] = jnp.zeros_like(bias_mine)
+    for i in range(7):
+        if i < 6:
+            row_sum = jnp.sum(terms[i], axis=0, keepdims=True)
+        else:
+            err = jnp.sum(jnp.sum(err_ref[...], axis=0, keepdims=True), axis=1, keepdims=True)
+            row_sum = jnp.broadcast_to(err, (1, depth))
+        for k in range(4):
+            terms_mine[k, i : i + 1, :] = row_sum[:, k * feat : (k + 1) * feat]
+    wide = bias_mine.shape[2]
+    for s in range(4):
+        bias_mine[s, 0:1, :qkv] = heads_out[s]
+        bias_mine[s, 0:1, qkv : qkv + main] = units_out[s]
+        bias_mine[s, 0:1, qkv + main :] = units_rest_out[...]
+    dp, row, col = place()
+    ring_two = (dp, row, 3 - col)
+    sides = ((1, "x"), (2, "y"), (3, "diagonal"))
+    term_sends = [send(terms_mine.at[k], terms_in.at[k - 1], peers[name]) for k, name in sides]
+    bias_sends = [
+        send(bias_mine.at[s], bias_turn.at[s - 1], peer)
+        for s, peer in ((1, peers["prev"]), (2, ring_two), (3, peers["next"]))
+    ]
     ff_add(0)
     end_low = send(gff.at[0, rows(1, 0, half)], rfx, peers["x"])
     end_high = send(gff.at[0, rows(2, half, half)], rfy, peers["y"])
     attn_ring(1)
+    for copy in term_sends + bias_sends:
+        copy.wait_recv()
+    terms_mine[0] = terms_mine[0] + terms_in[0] + terms_in[1] + terms_in[2]
+    sum_sends = [
+        send(terms_mine.at[0], sums_in.at[i], peer) for i, peer in enumerate(images_group())
+    ]
+    bias_plane[...] = bias_mine[0]
+    for s in (1, 2, 3):
+        bias_plane[s : s + 1, :] = bias_turn[s - 1, 0:1, :]
+    plane_sends = [send(bias_plane, bias_in.at[k - 1], peers[name]) for k, name in sides]
     end_low.wait_recv()
     end_high.wait_recv()
     add_into(gff.at[0], rows(0, 0, half), rfx)
     add_into(gff.at[0], rows(0, half, half), rfy)
-    ff_done = keep(gff.at[0, rows(0)], ff_out)
+    quarter = feat // 2
+    keep_at = pl.ds(pl.multiple_of(dp * quarter, 16), quarter)
+    give_at = pl.ds(pl.multiple_of((1 - dp) * quarter, 16), quarter)
+    done = [keep(gff.at[0, keep_at], ff_out.at[0])]
+    pair_sends = [send(gff.at[0, give_at], ff_out.at[1], peers["core"])]
+    for copy in plane_sends + sum_sends:
+        copy.wait_recv()
+    bias_out[0] = bias_plane[...] + bias_in[0] + bias_in[1] + bias_in[2]
+    pair_sends.append(send(bias_out.at[0], bias_out.at[1], peers["core"]))
+    total = terms_mine[0]
+    for i in range(7):
+        total = total + sums_in[i]
+    sums_out[...] = total
     attn_ring(0)
-    attn_done = keep(gattn.at[0, rows(0)], attn_out)
-    ff_done.wait()
-    attn_done.wait()
+    done.append(keep(gattn.at[0, keep_at], attn_out.at[0]))
+    pair_sends.append(send(gattn.at[0, give_at], attn_out.at[1], peers["core"]))
+    for copy in pair_sends:
+        copy.wait_recv()
+    for copy in done:
+        copy.wait()
+    result_move.arrive()
+    grad_move.arrive()
     for copy in send.copies:
         if copy is not swap1:
             copy.wait_send()
+    result_move.finish()
+    grad_move.finish()
 
 
 def backward_call(arrays, feat, lanes, main, qkv, mix, own, depth):
     tokens = 2 * own
     half = feat // 2
+    narrow = qkv + main + 128
     anywhere = pl.BlockSpec(memory_space=pl.ANY)
     local = pl.BlockSpec(memory_space=pltpu.VMEM)
     shapes = [
-        ((own, depth), BF16, local),
-        ((6, 16, depth), F32, local),
-        ((4, 1, main), F32, local),
-        ((1, 128), F32, local),
-        ((4, 1, qkv), F32, local),
-        ((feat, lanes), BF16, anywhere),
-        ((feat, 2 * main), BF16, anywhere),
+        ((2, 2, own, feat), BF16, anywhere),
+        ((2, 2, own, feat), BF16, anywhere),
+        ((8, feat), F32, local),
+        ((2, 8, narrow), F32, local),
+        ((2, half, lanes), BF16, anywhere),
+        ((2, half, 2 * main), BF16, anywhere),
     ]
     return pl.pallas_call(
         backward_kernel,
         out_shape=[jax.ShapeDtypeStruct(shape, dtype) for shape, dtype, _ in shapes],
-        in_specs=[local] * 10 + [anywhere] * 10,
+        in_specs=[local] * 11 + [anywhere] * 11,
         out_specs=[spec for _, _, spec in shapes],
         scratch_shapes=[
+            pltpu.VMEM((4, own, feat), BF16),
+            pltpu.VMEM((6, 16, depth), F32),
+            pltpu.VMEM((4, 8, feat), F32),
+            pltpu.VMEM((3, 8, feat), F32),
+            pltpu.VMEM((7, 8, feat), F32),
+            pltpu.VMEM((4, 8, narrow), F32),
+            pltpu.VMEM((3, 8, narrow), F32),
+            pltpu.VMEM((3, 8, narrow), F32),
+            pltpu.VMEM((8, narrow), F32),
+            pltpu.VMEM((4, 1, main), F32),
+            pltpu.VMEM((1, 128), F32),
+            pltpu.VMEM((4, 1, qkv), F32),
             pltpu.VMEM((4, depth, lanes), BF16),
             pltpu.VMEM((4, depth, 2 * main), BF16),
             pltpu.VMEM((2, depth, 2 * main), BF16),
@@ -1167,15 +1382,14 @@
             pltpu.VMEM((half, 2 * main), BF16),
             pltpu.VMEM((half, 2 * main), BF16),
             pltpu.SemaphoreType.DMA((32,)),
-            pltpu.SemaphoreType.DMA((72,)),
-            pltpu.SemaphoreType.DMA((72,)),
+            pltpu.SemaphoreType.DMA((104,)),
+            pltpu.SemaphoreType.DMA((104,)),
+            pltpu.SemaphoreType.DMA((5, 4)),
         ],
         compiler_params=pltpu.CompilerParams(
             collective_id=2, has_side_effects=True, vmem_limit_bytes=63 << 20
         ),
     )(*arrays)
-
-
 def on_chip(
     layer_input,
     teacher,
@@ -1195,7 +1409,7 @@
     bias_down,
 ):
     core = lax.axis_index("dp")
-    row = lax.axis_index("row")
+    first = core == 0
     cols = lax.axis_size("col")
     feat = layer_input.shape[1]
     images = layer_input.shape[0] // SEQ
@@ -1204,44 +1418,20 @@
     units = w_up.shape[1] // 2
     width = proj_out.shape[0] // 2
     heads = width // HD
-
-    def core_half(values, axis):
-        size = values.shape[axis] // 2
-        return lax.dynamic_slice_in_dim(values, core * size, size, axis)
-
-    def to_chip(values):
-        imgs = jnp.pad(values.reshape(images, SEQ, -1), ((0, 0), (0, pad_seq - SEQ), (0, 0)))
-        imgs = imgs.reshape(images, 2, half_seq, -1)
-        keep = lax.dynamic_index_in_dim(imgs, core, 1, False)
-        give = lax.dynamic_index_in_dim(imgs, 1 - core, 1, False)
-        got = pair_swap(give)
-        first = core == 0
-        every = jnp.concatenate([jnp.where(first, keep, got), jnp.where(first, got, keep)], axis=0)
-        parts = []
-        for k in range(4):
-            part = lax.dynamic_index_in_dim(every, row ^ k, 0, False)
-            parts.append(row_swap(part, k) if k else part)
-        return jnp.concatenate(parts, axis=1)
-
-    def from_chip(values):
-        parts = []
-        for k in range(4):
-            part = values[:, k * feat : (k + 1) * feat]
-            parts.append(row_swap(part, k) if k else part)
-        stacked = jnp.stack(parts)
-        every = jnp.stack([lax.dynamic_index_in_dim(stacked, row ^ i, 0, False) for i in range(4)])
-        every = every.reshape(2, images, half_seq, feat)
-        mine = lax.dynamic_index_in_dim(every, core, 0, False)
-        got = pair_swap(lax.dynamic_index_in_dim(every, 1 - core, 0, False))
-        first = core == 0
-        both = jnp.stack([jnp.where(first, mine, got), jnp.where(first, got, mine)], axis=1)
-        return both.reshape(images, pad_seq, feat)[:, :SEQ].reshape(images * SEQ, feat)
-
     main = units // 128 * 128
     rest = units - main
     at = 4 * width
     lanes = (at + 2 * rest + 127) // 128 * 128
     qkv, mix = 3 * heads * 128, heads * 128
+
+    def core_half(values, axis):
+        low, high = jnp.split(values, 2, axis=axis)
+        return jnp.where(first, low, high)
+
+    def pieces(values):
+        values = jnp.pad(values.reshape(images, SEQ, -1), ((0, 0), (0, pad_seq - SEQ), (0, 0)))
+        return values.reshape(images, 2, half_seq, -1)
+
     up_half, down_half = core_half(w_up, 1), core_half(w_down, 0).T
     attn_shard = jnp.concatenate(
         [
@@ -1258,162 +1448,110 @@
     spread_at = jnp.where(lane < at, lane // HD * 128 + lane % HD, -1)
     spread = (spread_at[:, None] == jnp.arange(qkv + mix)[None]).astype(jnp.bfloat16)
     tail = lane[-128:]
-    rest_spread = []
-    for s in range(cols):
-        up_at = jnp.where((tail >= at) & (tail < at + rest), tail - at + s * rest, -1)
-        down_at = jnp.where(
-            (tail >= at + rest) & (tail < at + 2 * rest), tail - at - rest + s * rest + 128, -1
-        )
-        place = jnp.arange(256)[None]
-        rest_spread.append((up_at[:, None] == place) | (down_at[:, None] == place))
-    rest_spread = jnp.stack(rest_spread).astype(jnp.bfloat16)
-    features = jnp.stack([norm1_gain, norm1_shift, norm2_gain, norm2_shift, bias_out, bias_down])
-    features = jnp.concatenate([features] + [row_swap(features, k) for k in (1, 2, 3)], axis=1)
-    features = jnp.pad(features.astype(jnp.float32), ((0, 2), (0, 0)))
-    col_biases = gather_ring(
-        jnp.concatenate([core_half(bias_query, 0), core_half(bias_value, 0), core_half(bias_up, 0)])[None]
-    )
-
-    x_half = to_chip(layer_input)
-    teacher_half = to_chip(teacher)
-    count = jnp.sum(valid.astype(jnp.float32)).reshape(1, 1)
-    count = count + pair_swap(count)
-    for bit in (1, 2):
-        count = count + lax.ppermute(count, "col", [(i, i ^ bit) for i in range(cols)])
-    valid_imgs = jnp.pad(valid.reshape(images, SEQ), ((0, 0), (0, pad_seq - SEQ)))
-    other_valid = pair_swap(valid_imgs)
-    from_here = (row // images) == core
-    chip_valid = lax.dynamic_index_in_dim(
-        jnp.where(from_here, valid_imgs, other_valid), lax.rem(row, images), 0, False
-    )
-    mask_half = lax.dynamic_slice_in_dim(chip_valid, core * half_seq, half_seq, 0)
-    mask_half = mask_half.astype(jnp.float32)[:, None]
-
-    place = jnp.arange(pad_seq)
-    token = jnp.where(place < half_seq, place + core * half_seq, place - core * half_seq)
+    part = jnp.arange(cols)[:, None]
+    up_at = jnp.where((tail >= at) & (tail < at + rest), tail - at + part * rest, -1)
+    down_at = jnp.where(
+        (tail >= at + rest) & (tail < at + 2 * rest), tail - at - rest + part * rest + 128, -1
+    )
+    spot = jnp.arange(256)
+    rest_spread = (up_at[..., None] == spot) | (down_at[..., None] == spot)
+    rest_spread = rest_spread.astype(jnp.bfloat16)
+
+    place_of = jnp.arange(pad_seq)
+    token = jnp.where(
+        place_of < half_seq, place_of + core * half_seq, place_of - core * half_seq
+    )
     key_column = jnp.where(token < SEQ, 0.0, -1e30).astype(jnp.float32)[:, None]
-    lane = jnp.arange(qkv)
-    key_lane = (lane % 384 == 128 + HD).astype(jnp.float32)[None]
-    one_lane = (lane % 384 == HD).astype(jnp.float32)[None]
-    qkv_biases, up_biases, rest_biases = [], [], []
-    for s in range(cols):
-        bias = col_biases[s][0].astype(jnp.float32)
-        query, value = bias[:width].reshape(heads, HD), bias[width : 2 * width].reshape(heads, HD)
-        spaced = jnp.stack([query, jnp.zeros_like(query), value], axis=1)
-        spaced = jnp.pad(spaced, ((0, 0), (0, 0), (0, 128 - HD))).reshape(1, qkv)
-        qkv_biases.append(spaced + one_lane)
-        up_biases.append(bias[None, 2 * width : 2 * width + main])
-        rest_biases.append(bias[2 * width + main :])
-    rest_bias = jnp.pad(jnp.concatenate(rest_biases), (0, 128 - cols * rest))[None]
-    tokens_all = layer_input.shape[0] * lax.axis_size("dp") * cols
-    factor = tokens_all / count
-
+    key_lane = (jnp.arange(qkv) % 384 == 128 + HD).astype(jnp.float32)[None]
+
+    query_bias, value_bias = core_half(bias_query, 0), core_half(bias_value, 0)
+    unit_bias = core_half(bias_up, 0)
+    pitch = (feat + 127) // 128 * 128
+    one = jnp.ones((1,), jnp.bfloat16)
+
+    def gap(size):
+        return jnp.zeros((size,), jnp.bfloat16)
+
+    params = []
+    for vector in (norm1_gain, norm1_shift, norm2_gain, norm2_shift, bias_out, bias_down):
+        params += [vector, gap(pitch - feat)]
+    for h in range(heads):
+        head_at = slice(h * HD, (h + 1) * HD)
+        params += [query_bias[head_at], one, gap(127 - HD + 128)]
+        params += [value_bias[head_at], gap(128 - HD)]
+    params += [unit_bias[:main], gap(at - lanes + 128), unit_bias[main:]]
+    params.append(gap(lanes - at - rest))
+    params = jnp.concatenate(params).astype(jnp.float32)
+    params = jnp.broadcast_to(params[None], (8, params.shape[0]))
+    count = jnp.broadcast_to(jnp.sum(valid).astype(jnp.float32), (8, 128))
+
+    marked = jnp.concatenate(
+        [
+            teacher,
+            valid.astype(jnp.bfloat16)[:, None],
+            jnp.zeros((teacher.shape[0], pitch - feat - 1), jnp.bfloat16),
+        ],
+        axis=1,
+    )
     sizes = (feat, lanes, main, qkv, mix, half_seq, 4 * feat)
     (
         wpad, wff, triple, mixed, act, slope, norm1t, norm2t, rest_weight, lse, act_rest,
-        slope_rest, resid1, grad_result, branch2, branch2t, result, err_rows,
+        slope_rest, resid1, grad_result, branch2, branch2t, result, err_rows, x_blocks,
+        features, counted,
     ) = forward_call(
         (
-            x_half, teacher_half, mask_half, key_column, features, jnp.stack(qkv_biases),
-            key_lane, jnp.stack(up_biases), rest_bias, jnp.broadcast_to(factor, (1, 4 * feat)),
-            spread, rest_spread, attn_shard, ff_shard,
+            pieces(layer_input), pieces(marked), count, params, key_column, key_lane, spread,
+            rest_spread, attn_shard, ff_shard,
+        ),
+        layer_input.shape[0],
+        *sizes,
+    )
+    grad_pieces, result_pieces, sums, bias_rows, attn_sum, ff_sum = backward_call(
+        (
+            branch2, rest_weight, act_rest, slope_rest, lse, features, spread, rest_spread,
+            x_blocks, resid1, err_rows, result, grad_result, norm1t, norm2t, branch2t, wpad,
+            wff, triple, mixed, act, slope,
         ),
         *sizes,
     )
-    layer_output = from_chip(result)
-    err_part = jnp.sum(err_rows)
-    grad_in, terms, unit_main, unit_rest, head_rows, attn_sum, ff_sum = backward_call(
-        (
-            branch2, rest_weight, act_rest, slope_rest, lse, features, spread, rest_spread,
-            x_half, resid1, grad_result, norm1t, norm2t, branch2t, wpad, wff, triple, mixed,
-            act, slope,
-        ),
-        *sizes,
-    )
-    grad_input = from_chip(grad_in).astype(jnp.float32)
-    terms = jnp.sum(terms, axis=1)
-    head_rows = head_rows.reshape(cols, heads, 3, 128)[..., :HD]
-    bias_rows = [
-        jnp.concatenate(
-            [
-                head_rows[s, :, 0].reshape(1, width),
-                head_rows[s, :, 2].reshape(1, width),
-                unit_main[s],
-                unit_rest[:, s * rest : (s + 1) * rest],
-            ],
-            axis=1,
-        )
-        for s in range(cols)
-    ]
-    bias_sum = bias_rows[cols - 1]
-    for s in reversed(range(cols - 1)):
-        bias_sum = bias_rows[s] + ring_shift(bias_sum, -1)
-    near = terms[:, : 2 * feat] + row_swap(terms[:, 2 * feat :], 2)
-    terms = near[:, :feat] + row_swap(near[:, feat:], 1)
-
-    def plane_sum(values):
-        values = values + row_swap(values, 1)
-        return values + row_swap(values, 2)
-
-    err_plane = plane_sum(err_part.reshape(1, 1))
-    sums = jnp.concatenate([terms, jnp.broadcast_to(err_plane, (1, feat))], axis=0)
-    for bit in (1, 2):
-        sums = sums + lax.ppermute(sums, "col", [(i, i ^ bit) for i in range(cols)])
-    sums = sums + pair_swap(sums)
-    loss_value = sums[6, 0] / (count[0, 0] * D)
-
-    def both_halves(values):
-        got = pair_swap(values)
-        first = core == 0
-        return jnp.concatenate(
-            [jnp.where(first, values, got), jnp.where(first, got, values)], axis=-1
-        )
-
-    bias_sum = plane_sum(bias_sum)[0]
-    head_mine = both_halves(bias_sum[: 2 * width].reshape(2, width))
-    unit_mine = both_halves(bias_sum[2 * width :])
-
-    def weight_rows(total):
-        size = feat // 2
-        keep = lax.dynamic_slice_in_dim(total, core * size, size, 0)
-        give = lax.dynamic_slice_in_dim(total, (1 - core) * size, size, 0)
-        return keep, pair_swap(give)
-
-    def joined(keep, got, axis):
-        first = core == 0
+
+    def rows_of(values):
+        return values.reshape(images, pad_seq, feat)[:, :SEQ].reshape(images * SEQ, feat)
+
+    def both(keep, got, axis=-1):
         return jnp.concatenate(
             [jnp.where(first, keep, got), jnp.where(first, got, keep)], axis=axis
         ).astype(jnp.float32)
 
-    ff_keep, ff_got = weight_rows(ff_sum)
-    attn_keep, attn_got = weight_rows(attn_sum)
-
-    def up_of(attn, ff):
-        return jnp.concatenate([ff[:, :main], attn[:, at : at + rest]], axis=1)
-
-    def down_of(attn, ff):
-        return jnp.concatenate([ff[:, main:], attn[:, at + rest : at + 2 * rest]], axis=1).T
-
-    grad_w_up = joined(up_of(attn_keep, ff_keep), up_of(attn_got, ff_got), 1)
-    grad_w_down = joined(down_of(attn_keep, ff_keep), down_of(attn_got, ff_got), 0)
-    grad_proj_in = joined(attn_keep[:, : 3 * width], attn_got[:, : 3 * width], 1)
-    grad_proj_out = joined(attn_keep[:, 3 * width : at].T, attn_got[:, 3 * width : at].T, 0)
+    def up_of(i):
+        return jnp.concatenate([ff_sum[i][:, :main], attn_sum[i][:, at : at + rest]], axis=1)
+
+    def down_of(i):
+        block = [ff_sum[i][:, main:], attn_sum[i][:, at + rest : at + 2 * rest]]
+        return jnp.concatenate(block, axis=1).T
+
+    loss_value = sums[6, 0] / (counted[0, 0] * D)
+    main_rows = jnp.sum(bias_rows[:, :cols, : qkv + main], axis=1)
+    head_rows = main_rows[:, :qkv].reshape(2, heads, 3, 128)[..., :HD]
+    tail_rows = bias_rows[:, :cols, qkv + main :]
+    tail_rows = sum(tail_rows[:, s, s * rest : (s + 1) * rest] for s in range(cols))
+    unit_rows = jnp.concatenate([main_rows[:, qkv:], tail_rows], axis=1)
     return (
-        layer_output,
+        rows_of(result_pieces),
         loss_value,
-        grad_input,
-        grad_proj_in[None],
-        head_mine[0],
-        head_mine[1],
-        grad_proj_out[:, None],
+        rows_of(grad_pieces).astype(jnp.float32),
+        both(attn_sum[0][:, : 3 * width], attn_sum[1][:, : 3 * width])[None],
+        both(head_rows[0, :, 0].reshape(width), head_rows[1, :, 0].reshape(width)),
+        both(head_rows[0, :, 2].reshape(width), head_rows[1, :, 2].reshape(width)),
+        both(attn_sum[0][:, 3 * width : at].T, attn_sum[1][:, 3 * width : at].T, 0)[:, None],
         sums[4],
         sums[0],
         sums[1],
         sums[2],
         sums[3],
-        grad_w_up[None],
-        unit_mine,
-        grad_w_down[:, None],
+        both(up_of(0), up_of(1))[None],
+        both(unit_rows[0], unit_rows[1]),
+        both(down_of(0), down_of(1), 0)[:, None],
         sums[5],
     )
 

time: 513 us -> 427 us (0.83); the launches traced: 503 us -> 423 us
  Pallas kernels: 313 us -> 376 us
  waiting for transfers between devices: 50.5 us -> 0 us
  starting transfers between devices: 48.2 us -> 0 us
  local copies, waits for them, and re-layouts: 59.5 us -> 28.6 us
  other arithmetic: 23.8 us -> 14.9 us
    ppermute x42 -> x0, waiting for transfers between devices: 50.5 us -> none  [the longest x21 33.1 us: row_swap(): lax.ppermute(values, 'row', [(i, i ^ bit) for i in range(lax.axis_size('r...]
    ppermute x42 -> x0, starting transfers between devices: 48.2 us -> none  [the longest x21 28.5 us: row_swap(): lax.ppermute(values, 'row', [(i, i ^ bit) for i in range(lax.axis_size('r...]
    pallas_call x1, Pallas kernels: 162 us -> 204 us  [forward_call(): pl.pallas_call(functools.partial(forward_kernel, own_tokens), out_shape=[...]
    pallas_call x1, Pallas kernels: 151 us -> 171 us  [backward_call(): pl.pallas_call(backward_kernel, out_shape=[jax.ShapeDtypeStruct(shape, dt...]
    dynamic_slice x24 -> x0, local copies, waits for them, and re-layouts: 13.9 us -> none  [the longest x1 4.46 us: to_chip(): keep = lax.dynamic_index_in_dim(imgs, core, 1, False)]
    another operation x29 -> x0, local copies, waits for them, and re-layouts: 10.7 us -> none  [the longest x7 4.24 us: on_chip(): jnp.stack([norm1_gain, norm1_shift, norm2_gain, norm2_shift, bias_out, bi...]
    another operation x9 -> x0, other arithmetic: 5.55 us -> none  [the longest x2 2.2 us: from_chip(): jnp.stack([jnp.where(first, mine, got), jnp.where(first, got, mine)], axi...]
  transfers between devices with their start and end apart: 42 -> 0, of which waited for: 22 -> 0; matrix products, arithmetic and copies ran while one was open for 14% -> 0% of each run, Pallas kernels for 0% -> 0%
where the time goes in v3:
time: 427 us; the launch traced here: 423 us
  Pallas kernels  376 us (88%)
  local copies, waits for them, and re-layouts  28.6 us (7%)
  other arithmetic  14.9 us (3%)
  between operations  4.31 us (1%)
    pallas_call x1, Pallas kernels, forward_call(): pl.pallas_call(functools.partial(forward_kernel, own_tokens), out_shape=[...  204 us
    pallas_call x1, Pallas kernels, backward_call(): pl.pallas_call(backward_kernel, out_shape=[jax.ShapeDtypeStruct(shape, dt...  171 us

profile of v3, /device:TPU:0, one launch (start us, length us, event | category | flops | bytes accessed | tf_op | source)
XLA Modules:
  0.0 423.5 jit_solution(1450022265276210098)
XLA Ops:
  0.6 0.0 copy-start.3
  0.7 0.9 broadcast_select_fusion.7
  1.5 0.8 broadcast_select_fusion.6
  2.4 0.1 pad.38.clone
  2.5 0.1 fusion.27
  2.5 0.1 fusion.28
  2.6 0.8 slice_select_fusion.2
  3.5 4.2 %concatenate.137 = bf16[3712]{0:T(1024)(128)(2,1)S(1)} concatenate(bf16[288]{0:T(512)(128)(2,1)} %param.24, bf16[96]{0:T(256)(128)(2,1)S(1)} %concatenate.134, bf16[288]{0:T(512)(128)(2,1)} %param.25, bf16[96]{0:T(256)(128)(2,1)S(1)} %concatenate.134, bf16[288]{0:T(512)(128)(2,1)} %param.26, bf16[96]{0:T(256)(128)(2,1)S(1)} %concatenate.134, bf16[288]{0:T(512)(128)(2,1)} %param.27, ...), dimensions={0} | concatenate | bytes 14848 | tf_op jit(solution)/shard_map/concatenate | solution.py:1484
  7.7 0.6 compare_convert_fusion.key_lane_ref
  8.4 0.1 add_select_fusion.2
  8.5 1.4 fusion.26
  10.5 0.6 broadcast_in_dim.64.count_ref
  11.1 0.7 broadcast_in_dim.67.params_ref
  11.8 1.0 fusion.23
  12.8 0.1 copy.61
  12.9 0.1 copy.60
  13.0 0.0 copy-start.4
  13.0 0.9 fusion.2.rest_spread_ref
  14.0 0.1 slice_select_fusion.1
  14.1 0.2 slice_select_fusion
  14.3 0.2 select_bitcast_fusion
  14.6 0.0 copy-start.1
  14.6 0.9 concatenate.138.attn_ref
  15.5 0.9 pad_maximum_fusion.ff_ref
  16.4 0.4 concatenate.160
  16.8 0.8 fusion.3.key_ref
  17.6 0.9 reshape.556
  18.5 1.9 copy.52
  20.4 0.0 copy-start.2
  20.5 1.1 pad.8
  21.6 0.3 copy-done.2
  21.9 0.9 concatenate.131
  22.8 1.4 copy.53
  24.2 0.4 maximum_maximum_fusion
  24.6 1.1 pad.9
  25.8 1.3 fusion.spread_ref
  27.1 204.2 %shard_map.279 = (bf16[4,1152,1024]{2,1,0:T(8,128)(2,1)}, bf16[4,1152,1024]{2,1,0:T(8,128)(2,1)}, bf16[4,768,768]{2,1,0:T(8,128)(2,1)}, bf16[4,768,256]{2,1,0:T(...) custom-call(bf16[2,2,384,288]{3,2,1,0:T(8,128)(2,1)} %bitcast.50, ...), custom_call_target="tpu_custom_call" | custom-call | tf_op jit(solution)/shard_map/pallas_call | solution.py:869
  231.3 1.2 slice.183
  233.2 171.5 %shard_map.280 = (bf16[2,2,384,288]{3,2,1,0:T(8,128)(2,1)}, bf16[2,2,384,288]{3,2,1,0:T(8,128)(2,1)}, f32[8,288]{1,0:T(8,128)}, f32[2,8,1408]{2,1,0:T(8,128)}, b...) custom-call(bf16[768,1152]{1,0:T(8,128)(2,1)} %get-tuple-element.43.branch2_ref, ...), custom_call_target="tpu_custom_call" | custom-call | tf_op jit(solution)/shard_map/pallas_call | solution.py:1338
  404.7 1.2 slice.182
  406.5 1.4 slice.224
  407.9 1.3 copy.57
  409.2 1.6 reshape.560
  410.8 0.1 slice.225
  410.9 0.7 copy.62
  411.7 0.1 copy-done.8
  411.8 0.1 slice_add_fusion
  412.0 0.1 select_n.290
  412.0 0.1 select_n.288
  412.1 0.1 select_n.292
  412.2 0.1 select_n.286
  412.3 0.7 pad_maximum_fusion.7
  413.0 0.7 pad_maximum_fusion.5
  413.7 0.6 slice_reduce_fusion.1
  414.3 0.1 fusion.24
  414.4 0.1 fusion.25
  414.5 0.1 select_bitcast_fusion.9
  414.7 0.8 maximum_convert_fusion.3
  415.4 0.9 maximum_convert_fusion.2
  416.4 0.2 select_bitcast_fusion.2
  416.6 1.0 maximum_convert_fusion.1
  417.6 1.0 maximum_convert_fusion
  418.5 0.9 copy.59
  419.4 2.7 reshape.563
  (44 shorter events, 0.4 us)
Async XLA Ops:
  0.6 13.5 %copy-start.3 = (bf16[288,1076]{1,0:T(8,128)(2,1)S(1)}, bf16[288,1076]{1,0:T(8,128)(2,1)}, u32[]{:S(2)}) copy-start(bf16[288,1076]{1,0:T(8,128)(2,1)} %param.28) | copy-start | bytes 1859332
  0.7 13.3 %copy-start.5 = (bf16[288,864]{1,0:T(8,128)(2,1)S(1)}, bf16[288,864]{1,0:T(8,128)(2,1)}, u32[]{:S(2)}) copy-start(bf16[288,864]{1,0:T(8,128)(2,1)} %param.19) | copy-start | bytes 1492996
  13.0 1.3 copy-start.4
  14.6 3.0 copy-start.1
  20.4 1.5 copy-start.2
  407.9 2.9 copy-start
  410.9 0.9 copy-start.8
  410.9 2.8 copy-start.9
  410.9 3.4 copy-start.7
  413.7 2.7 copy-start.6

commit v4 on v3

--- a/solution.py
+++ b/solution.py
@@ -427,6 +427,18 @@
     @pl.loop(0, count // size)
     def _(step):
         body(pl.ds(pl.multiple_of(step * size, size), size))
+
+
+def fold(values):
+    return sum(values[i : i + 16] for i in range(0, values.shape[0], 16))
+
+
+def spread_lanes(source, spread, width):
+    blocks = []
+    for j in range(width // 256):
+        low = 2 * HD * j // 128 * 128
+        blocks.append(mm(source[:, low : low + 256], spread[low : low + 256, 256 * j : 256 * j + 256]))
+    return jnp.concatenate(blocks, axis=1)
 
 
 def transpose_into(target, source):
@@ -528,7 +540,9 @@
     norm2,
     turned,
     part,
+    give1,
     got1,
+    give2,
     got2,
     local_sems,
     send_sems,
@@ -615,7 +629,7 @@
 
         def unpack(at):
             block = wattn[s, at, :]
-            wpad[slot, at, :] = mm(block, spread_ref[...]).astype(BF16)
+            wpad[slot, at, :] = spread_lanes(block, spread_ref, wpad.shape[2]).astype(BF16)
             extra = mm(block[:, block.shape[1] - 128 :], rest_spread_ref[s]).astype(BF16)
             if s == 0:
                 rest_out[at, :] = extra
@@ -629,7 +643,7 @@
             values = values + key_ref[at, :] * key_lane_ref[...]
             triple[slot, at, :] = values.astype(BF16)
 
-        each_rows(tokens, own, project)
+        each_rows(tokens, tokens, project)
         scale = LOG2E * HD**-0.5
         for h in range(qkv // 384):
             query_at, key_at, value_at = (pl.ds((3 * h + j) * 128, 128) for j in range(3))
@@ -644,13 +658,19 @@
                 values = mm(value_turned, weights.astype(BF16)) / total
                 mixed[s, at, pl.ds(h * 128, 128)] = values.T.astype(BF16)
 
-            each_rows(tokens, 256, head)
+            each_rows(tokens, own, head)
 
         def out(at):
             values = mm_nt(mixed[s, at, :], wpad[slot, :, qkv:])
-            part[at, :] = values if s == 0 else part[at, :] + values
-
-        each_rows(tokens, own, out)
+            return values if s == 0 else part[at, :] + values
+
+        swap = None
+        if s < 3:
+            part[...] = out(pl.ds(0, tokens))
+        else:
+            give1[...] = out(pl.ds(own, own)).astype(BF16)
+            swap = send(give1, got1, peers["core"])
+            part[pl.ds(0, own), :] = out(pl.ds(0, own))
         saved.append(
             [
                 keep(wpad.at[slot], wpad_out.at[s]),
@@ -658,6 +678,7 @@
                 keep(mixed.at[s], mixed_out.at[s]),
             ]
         )
+        return swap
 
     def gelu(pre):
         inner = GELU_ROOT * (pre + 0.044715 * pre * pre * pre)
@@ -674,9 +695,15 @@
             low, bent = gelu(pre)
             act[s, at, :] = low
             slope[s, at, :] = bent
-            part[at, :] = part[at, :] + mm_nt(low, wff[s, :, main:])
-
-        each_rows(tokens, own, block)
+            return part[at, :] + mm_nt(low, wff[s, :, main:])
+
+        swap = None
+        if s < 3:
+            part[...] = block(pl.ds(0, tokens))
+        else:
+            give2[...] = block(pl.ds(own, own)).astype(BF16)
+            swap = send(give2, got2, peers["core"])
+            part[pl.ds(0, own), :] = block(pl.ds(0, own))
         ff_saved.extend(
             [
                 keep(act.at[s], act_out.at[s]),
@@ -684,6 +711,7 @@
                 keep(wff.at[s], wff_out.at[s]),
             ]
         )
+        return swap
 
     def rest_compute():
         bias = mm(biases_in[0, :, qkv + main :].astype(BF16), rest_spread_ref[0, :, :128])
@@ -698,7 +726,7 @@
             slope_rest_out[at, :] = bent
             part[at, :] = mm_nt(low, rest_out[:, 128:])
 
-        each_rows(tokens, own, block)
+        each_rows(tokens, tokens, block)
 
     saved, ff_saved = [], []
     x_move = Shuffle(shuffle_sems.at[0], shuffle_sems.at[1], shuffle_sems.at[2, 0])
@@ -728,6 +756,14 @@
     def token_rows(at):
         return jnp.concatenate([x_ref[k, at, :].astype(F32) for k in range(4)], axis=1)
 
+    az[1].wait_recv()
+    attn_ring(1)
+    attn_plane(1)
+    attn_last(0)
+    az[2].wait_recv()
+    attn_ring(2)
+    attn_plane(2)
+    first = ff_first()
     for copy in own_params:
         copy.wait()
     arrive(smalls)
@@ -742,98 +778,98 @@
         normed, _ = norm_stats(token_rows(at))
         norm1[at, :] = (normed * feature_ref[0:1] + feature_ref[1:2]).astype(BF16)
 
-    each_rows(own, 16, first_norm)
+    each_rows(own, 128, first_norm)
     swap1 = send(norm1.at[pl.ds(0, own)], norm1.at[pl.ds(own, own)], peers["core"])
-    az[1].wait_recv()
-    attn_ring(1)
-    attn_plane(1)
-    attn_last(0)
-    swap1.wait_recv()
-    az[2].wait_recv()
-    attn_ring(2)
-    attn_plane(2)
-    attn_last(1)
-    first = ff_first()
-    attn_compute(0)
     az[3].wait_recv()
     attn_plane(3)
-    attn_last(2)
     own_ff.wait()
     arrive(first)
     ff_ring(0)
-    teacher_move.spread(teacher_pieces, teacher_ref)
+    attn_last(1)
+    swap1.wait_recv()
+    attn_compute(0)
+    attn_last(2)
     attn_compute(1)
     attn_last(3)
     ff_last(0)
+    arrive(fz[1])
+    ff_ring(1)
+    ff_last(1)
     attn_compute(2)
-    attn_compute(3)
-    swap2 = send(part.at[pl.ds(own, own)], got1, peers["core"])
-    arrive([swap2])
+    swap2 = attn_compute(3)
+    swap2.wait_recv()
 
     def second_norm(at):
-        values = token_rows(at) + part[at, :] + got1[at, :] + feature_ref[4:5]
+        values = token_rows(at) + part[at, :] + got1[at, :].astype(F32) + feature_ref[4:5]
         resid_out[at, :] = values
         normed, _ = norm_stats(values)
         norm2[at, :] = (normed * feature_ref[2:3] + feature_ref[3:4]).astype(BF16)
 
-    each_rows(own, 16, second_norm)
-    swap2.wait_send()
+    each_rows(own, 128, second_norm)
     swap3 = send(norm2.at[pl.ds(0, own)], norm2.at[pl.ds(own, own)], peers["core"])
-    arrive(fz[1])
-    ff_ring(1)
-    ff_last(1)
+    arrive(fz[2])
+    ff_ring(2)
+    ff_last(2)
     transpose_into(turned, norm1)
     turn1 = keep(turned, norm1t_out)
-    arrive([swap3])
+    swap3.wait_recv()
     rest_compute()
     turn1.wait()
     transpose_into(turned, norm2)
     turn2 = keep(turned, norm2t_out)
-    arrive(fz[2])
-    ff_ring(2)
-    ff_last(2)
     ff_compute(0)
-    ff_compute(1)
     arrive(fz[3])
     ff_last(3)
+    teacher_move.spread(teacher_pieces, teacher_ref)
+    ff_compute(1)
     ff_compute(2)
-    ff_compute(3)
-    swap4 = send(part.at[pl.ds(own, own)], got2, peers["core"])
-    arrive([swap4])
+    swap4 = ff_compute(3)
     err_out[...] = jnp.zeros_like(err_out)
-    teacher_move.arrive()
     arrive(counts)
     count = counts_in[0]
     for i in range(1, 8):
         count = count + counts_in[i]
     count_out[...] = count
     factor = (own_tokens * 8.0) / count[0:1, 0:1]
+    teacher_move.arrive()
+    swap4.wait_recv()
 
     def finish(at):
-        values = resid_out[at, :] + part[at, :] + got2[at, :] + feature_ref[5:6]
+        values = resid_out[at, :] + part[at, :] + got2[at, :].astype(F32) + feature_ref[5:6]
         for k in range(4):
             result_out[k, at, :] = values[:, k * feat : (k + 1) * feat].astype(BF16)
         target = [teacher_ref[k, at, :feat].astype(F32) for k in range(4)]
         error = values - jnp.concatenate(target, axis=1)
         masked = error * teacher_ref[0, at, feat : feat + 1].astype(F32)
-        err_out[...] = err_out[...] + error * masked
+        err_out[...] = err_out[...] + fold(error * masked)
         grad = masked * factor
         grad_out[at, :] = grad
         branch_out[at, :] = grad.astype(BF16)
 
-    each_rows(own, 16, finish)
-    swap5 = send(branch_out.at[pl.ds(0, own)], branch_out.at[pl.ds(own, own)], peers["core"])
-    arrive([swap5])
-    transpose_into(brancht_out, branch_out)
+    def turn(start):
+        brancht_out[:, pl.ds(start, 128)] = branch_out[pl.ds(start, 128), :].T
+
+    swaps = []
+    for start in range(0, own, 128):
+        finish(pl.ds(start, 128))
+        swaps.append(
+            send(
+                branch_out.at[pl.ds(start, 128)],
+                branch_out.at[pl.ds(own + start, 128)],
+                peers["core"],
+            )
+        )
+        turn(start)
+    for start, swap in zip(range(own, tokens, 128), swaps):
+        swap.wait_recv()
+        turn(start)
     turn2.wait()
     for copies in saved[2:]:
         for copy in copies:
             copy.wait()
     for copy in ff_saved:
         copy.wait()
-    for copy in send.copies:
-        if copy is not swap2:
-            copy.wait_send()
+    send.finish()
     x_move.finish()
     teacher_move.finish()
 
@@ -887,8 +923,10 @@
             pltpu.VMEM((tokens, depth), BF16),
             pltpu.VMEM((depth, tokens), BF16),
             pltpu.VMEM((tokens, depth), F32),
-            pltpu.VMEM((own, depth), F32),
-            pltpu.VMEM((own, depth), F32),
+            pltpu.VMEM((own, depth), BF16),
+            pltpu.VMEM((own, depth), BF16),
+            pltpu.VMEM((own, depth), BF16),
+            pltpu.VMEM((own, depth), BF16),
             pltpu.SemaphoreType.DMA((32,)),
             pltpu.SemaphoreType.DMA((72,)),
             pltpu.SemaphoreType.DMA((72,)),
@@ -951,6 +989,7 @@
     brancht,
     branch1,
     part,
+    give,
     got,
     grad_mid,
     dtriple,
@@ -1052,7 +1091,7 @@
             gff[s, at, :main] = mm(normt[at, :], grad_pre[...]).astype(BF16)
             gff[s, at, main:] = mm(brancht[at, :], kept[slot, :, :main]).astype(BF16)
 
-        each_rows(depth, feat, grads)
+        each_rows(depth, 2 * feat, grads)
         cy[s] = [
             send(gff.at[s, rows(k, 0, half)], ry.at[s, k - 2], peers["y"]) for k in (2, 3)
         ]
@@ -1070,15 +1109,18 @@
             low = (grad * slope_rest_ref[at, :].astype(F32)).astype(BF16)
             grad_pre[at, :128] = low
             units_rest_out[...] = units_rest_out[...] + column_sum(low)
-            part[at, :] = part[at, :] + mm_nt(low, rest_ref[:, :128])
-
-        each_rows(tokens, own, block)
+            return part[at, :] + mm_nt(low, rest_ref[:, :128])
+
+        give[...] = block(pl.ds(own, own)).astype(BF16)
+        swap = send(give, got, peers["core"])
+        part[pl.ds(0, own), :] = block(pl.ds(0, own))
 
         def grads(at):
             grad_rest[at, :128] = mm(normt[at, :], grad_pre[:, :128]).astype(BF16)
             grad_rest[at, 128:] = mm(brancht[at, :], act_rest_ref[...]).astype(BF16)
 
-        each_rows(depth, feat, grads)
+        each_rows(depth, 2 * feat, grads)
+        return swap
 
     def ff_add(s):
         for copy in cy[s] + cx[s]:
@@ -1112,7 +1154,7 @@
         def back_out(at):
             grad_mixed[at, :] = mm(branch1[at, :], wslot[slot, :, qkv:]).astype(BF16)
 
-        each_rows(tokens, own, back_out)
+        each_rows(tokens, tokens, back_out)
         scale = HD**-0.5
         for h in range(qkv // 384):
             query_at, key_at, value_at = (pl.ds((3 * h + j) * 128, 128) for j in range(3))
@@ -1136,32 +1178,44 @@
                 grad_key[...] += mm(grad_raw, query)
                 dtriple[at, query_at] = mm(key_turned, grad_raw).T.astype(BF16)
 
-            each_rows(tokens, 256, head)
+            each_rows(tokens, own, head)
             dtriple[:, key_at] = grad_key[...].astype(BF16)
             dtriple[:, value_at] = grad_value[...].astype(BF16)
         heads_out[s] = jnp.zeros((1, qkv), F32)
 
         def back_in(at):
             values = mm_nt(dtriple[at, :], wslot[slot, :, :qkv])
-            part[at, :] = values if s == 3 else part[at, :] + values
             heads_out[s] = heads_out[s] + column_sum(dtriple[at, :])
-
-        each_rows(tokens, own, back_in)
+            return values if s == 3 else part[at, :] + values
+
+        swap = None
+        if s:
+            for at in (pl.ds(0, own), pl.ds(own, own)):
+                part[at, :] = back_in(at)
+        else:
+            give[...] = back_in(pl.ds(own, own)).astype(BF16)
+            swap = send(give, got, peers["core"])
+            part[pl.ds(0, own), :] = back_in(pl.ds(0, own))
 
         def grads(at):
             first = mm(normt[at, :], dtriple[...]).astype(BF16)
             second = mm(brancht[at, :], kept[slot, :, qkv:]).astype(BF16)
-            packed = mm_nt(first, spread_ref[:, :qkv]) + mm_nt(second, spread_ref[:, qkv:])
-            gattn[s, at, :] = packed.astype(BF16)
-            tail = pl.ds(packed.shape[1] - 128, 128)
-            extra = mm_nt(grad_rest[at, :], rest_spread_ref[s])
-            gattn[s, at, tail] = (gattn[s, at, tail].astype(F32) + extra).astype(BF16)
-
-        each_rows(depth, feat, grads)
+            tiles = [0.0] * (gattn.shape[2] // 128)
+            for j in range((qkv + second.shape[1]) // 256):
+                low, to = 2 * HD * j // 128 * 128, 256 * j
+                block = first[:, to : to + 256] if to < qkv else second[:, to - qkv : to - qkv + 256]
+                moved = mm_nt(block, spread_ref[low : low + 256, to : to + 256])
+                for i in (0, 1):
+                    tiles[low // 128 + i] += moved[:, 128 * i : 128 * i + 128]
+            tiles[-1] += mm_nt(grad_rest[at, :], rest_spread_ref[s])
+            gattn[s, at, :] = jnp.concatenate(tiles, axis=1).astype(BF16)
+
+        each_rows(depth, 2 * feat, grads)
         ca[s] = send(gattn.at[s, rows(3, 0, half)], ra.at[s], peers["y"])
         cb[s] = send(gattn.at[s, rows(3, half, half)], rb.at[s], peers["x"])
         if s >= 2:
             attn_loads[s - 2] = load_attn(s - 2)
+        return swap
 
     def attn_plane(s):
         ca[s].wait_recv()
@@ -1183,24 +1237,23 @@
     terms[...] = jnp.zeros_like(terms)
 
     def add_term(index, values):
-        terms[index] = terms[index] + values
-
+        terms[index] = terms[index] + fold(values)
+
+    result_move.collect(result_blocks, result_pieces)
     ff_compute(3)
     ff_compute(2)
-    result_move.collect(result_blocks, result_pieces)
     ff_compute(1)
     ff_add(3)
     ff_compute(0)
     attn_loads = {3: load_attn(3), 2: load_attn(2)}
-    rest_compute()
+    swap1 = rest_compute()
     load_norm = keep(norm1t_hbm, normt)
-    swap1 = send(part.at[pl.ds(own, own)], got, peers["core"])
     swap1.wait_recv()
     load_grad.wait()
 
     def mid(at):
         normed, inv_scale = norm_stats(resid_ref[at, :])
-        grad_norm = part[at, :] + got[at, :]
+        grad_norm = part[at, :] + got[at, :].astype(F32)
         add_term(2, grad_norm * normed)
         add_term(3, grad_norm)
         scaled = grad_norm * feature_ref[2:3]
@@ -1213,8 +1266,7 @@
         add_term(4, low.astype(F32))
         add_term(5, branch2_ref[at, :].astype(F32))
 
-    each_rows(own, 16, mid)
-    swap1.wait_send()
+    each_rows(own, 64, mid)
     swap2 = send(branch1.at[pl.ds(0, own)], branch1.at[pl.ds(own, own)], peers["core"])
     swap2.wait_recv()
     load_norm.wait()
@@ -1227,8 +1279,8 @@
     attn_plane(2)
     ff_add(1)
     attn_ring(3)
-    attn_compute(0)
-    swap3 = send(part.at[pl.ds(own, own)], got, peers["core"])
+    swap1.wait_send()
+    swap3 = attn_compute(0)
     attn_plane(1)
     attn_ring(2)
     attn_plane(0)
@@ -1239,7 +1291,7 @@
 
     def last(at):
         normed, inv_scale = norm_stats(token_rows(at))
-        grad_norm = part[at, :] + got[at, :]
+        grad_norm = part[at, :] + got[at, :].astype(F32)
         add_term(0, grad_norm * normed)
         add_term(1, grad_norm)
         scaled = grad_norm * feature_ref[0:1]
@@ -1249,7 +1301,7 @@
         for k in range(4):
             grad_blocks[k, at, :] = grad[:, k * feat : (k + 1) * feat].astype(BF16)
 
-    each_rows(own, 16, last)
+    each_rows(own, 64, last)
     grad_move.collect(grad_blocks, grad_pieces)
     terms_mine[...] = jnp.zeros_like(terms_mine)
     bias_mine[...] = jnp.zeros_like(bias_mine)
@@ -1363,7 +1415,8 @@
             pltpu.VMEM((depth, tokens), BF16),
             pltpu.VMEM((tokens, depth), BF16),
             pltpu.VMEM((tokens, depth), F32),
-            pltpu.VMEM((own, depth), F32),
+            pltpu.VMEM((own, depth), BF16),
+            pltpu.VMEM((own, depth), BF16),
             pltpu.VMEM((own, depth), F32),
             pltpu.VMEM((tokens, qkv), BF16),
             pltpu.VMEM((tokens, mix), BF16),

time: 427 us -> 383 us (0.90)
  Pallas kernels: 376 us -> 332 us
    pallas_call x1, Pallas kernels: 204 us -> 178 us  [forward_call(): pl.pallas_call(functools.partial(forward_kernel, own_tokens), out_shape=[...]
    pallas_call x1, Pallas kernels: 171 us -> 154 us  [backward_call(): pl.pallas_call(backward_kernel, out_shape=[jax.ShapeDtypeStruct(shape, dt...]
where the time goes in v4:
time: 383 us; the launch traced here: 380 us
  Pallas kernels  332 us (87%)
  local copies, waits for them, and re-layouts  28.6 us (7%)
  other arithmetic  14.9 us (4%)
  between operations  4.39 us (1%)
    pallas_call x1, Pallas kernels, forward_call(): pl.pallas_call(functools.partial(forward_kernel, own_tokens), out_shape=[...  178 us
    pallas_call x1, Pallas kernels, backward_call(): pl.pallas_call(backward_kernel, out_shape=[jax.ShapeDtypeStruct(shape, dt...  154 us

profile of v4, /device:TPU:0, one launch (start us, length us, event | category | flops | bytes accessed | tf_op | source)
XLA Modules:
  0.0 379.7 jit_solution(18266754933783069985)
XLA Ops:
  0.7 0.9 broadcast_select_fusion.7
  1.5 0.8 broadcast_select_fusion.6
  2.4 0.1 pad.38.clone
  2.5 0.1 fusion.27
  2.5 0.1 fusion.28
  2.6 0.8 slice_select_fusion.2
  3.5 4.2 %concatenate.137 = bf16[3712]{0:T(1024)(128)(2,1)S(1)} concatenate(bf16[288]{0:T(512)(128)(2,1)} %param.24, bf16[96]{0:T(256)(128)(2,1)S(1)} %concatenate.134, bf16[288]{0:T(512)(128)(2,1)} %param.25, bf16[96]{0:T(256)(128)(2,1)S(1)} %concatenate.134, bf16[288]{0:T(512)(128)(2,1)} %param.26, bf16[96]{0:T(256)(128)(2,1)S(1)} %concatenate.134, bf16[288]{0:T(512)(128)(2,1)} %param.27, ...), dimensions={0} | concatenate | bytes 14848 | tf_op jit(solution)/shard_map/concatenate | solution.py:1537
  7.7 0.6 compare_convert_fusion.key_lane_ref
  8.4 0.1 add_select_fusion.2
  8.5 1.4 fusion.26
  10.5 0.6 broadcast_in_dim.64.count_ref
  11.1 0.7 broadcast_in_dim.67.params_ref
  11.8 1.0 fusion.23
  12.8 0.1 copy.61
  12.9 0.1 copy.60
  13.0 0.0 copy-start.4
  13.0 0.9 fusion.2.rest_spread_ref
  13.9 0.0 copy-done.5
  14.0 0.1 slice_select_fusion.1
  14.1 0.2 slice_select_fusion
  14.3 0.2 select_bitcast_fusion
  14.6 0.0 copy-start.1
  14.6 0.9 concatenate.138.attn_ref
  15.5 0.9 pad_maximum_fusion.ff_ref
  16.4 0.4 concatenate.160
  16.8 0.8 fusion.3.key_ref
  17.6 0.9 reshape.556
  18.5 1.9 copy.52
  20.4 0.0 copy-start.2
  20.5 1.1 pad.8
  21.6 0.3 copy-done.2
  21.9 0.9 concatenate.131
  22.8 1.4 copy.53
  24.2 0.4 maximum_maximum_fusion
  24.6 1.1 pad.9
  25.8 1.3 fusion.spread_ref
  27.1 177.6 %shard_map.279 = (bf16[4,1152,1024]{2,1,0:T(8,128)(2,1)}, bf16[4,1152,1024]{2,1,0:T(8,128)(2,1)}, bf16[4,768,768]{2,1,0:T(8,128)(2,1)}, bf16[4,768,256]{2,1,0:T(...) custom-call(bf16[2,2,384,288]{3,2,1,0:T(8,128)(2,1)} %bitcast.50, ...), custom_call_target="tpu_custom_call" | custom-call | tf_op jit(solution)/shard_map/pallas_call | solution.py:905
  204.7 1.2 slice.183
  206.5 154.3 %shard_map.280 = (bf16[2,2,384,288]{3,2,1,0:T(8,128)(2,1)}, bf16[2,2,384,288]{3,2,1,0:T(8,128)(2,1)}, f32[8,288]{1,0:T(8,128)}, f32[2,8,1408]{2,1,0:T(8,128)}, b...) custom-call(bf16[768,1152]{1,0:T(8,128)(2,1)} %get-tuple-element.43.branch2_ref, ...), custom_call_target="tpu_custom_call" | custom-call | tf_op jit(solution)/shard_map/pallas_call | solution.py:1390
  360.8 1.2 slice.182
  362.7 1.4 slice.224
  364.0 1.3 copy.57
  365.3 1.6 reshape.560
  366.9 0.1 slice.225
  367.1 0.8 copy.62
  367.9 0.0 copy-done.8
  367.9 0.1 slice_add_fusion
  368.1 0.1 select_n.290
  368.2 0.1 select_n.288
  368.3 0.1 select_n.292
  368.4 0.1 select_n.286
  368.4 0.7 pad_maximum_fusion.7
  369.1 0.7 pad_maximum_fusion.5
  369.8 0.6 slice_reduce_fusion.1
  370.5 0.1 fusion.24
  370.6 0.1 fusion.25
  370.7 0.1 select_bitcast_fusion.9
  370.8 0.8 maximum_convert_fusion.3
  371.6 0.9 maximum_convert_fusion.2
  372.6 0.2 select_bitcast_fusion.2
  372.7 1.0 maximum_convert_fusion.1
  373.7 1.0 maximum_convert_fusion
  374.7 0.9 copy.59
  375.6 2.7 reshape.563
  (44 shorter events, 0.4 us)
Async XLA Ops:
  0.6 13.5 %copy-start.3 = (bf16[288,1076]{1,0:T(8,128)(2,1)S(1)}, bf16[288,1076]{1,0:T(8,128)(2,1)}, u32[]{:S(2)}) copy-start(bf16[288,1076]{1,0:T(8,128)(2,1)} %param.28) | copy-start | bytes 1859332
  0.7 13.3 %copy-start.5 = (bf16[288,864]{1,0:T(8,128)(2,1)S(1)}, bf16[288,864]{1,0:T(8,128)(2,1)}, u32[]{:S(2)}) copy-start(bf16[288,864]{1,0:T(8,128)(2,1)} %param.19) | copy-start | bytes 1492996
  13.0 1.3 copy-start.4
  14.6 3.0 copy-start.1
  20.4 1.5 copy-start.2
  364.0 2.9 copy-start
  367.0 0.9 copy-start.8
  367.1 2.8 copy-start.9
  367.1 3.4 copy-start.7
  369.8 2.7 copy-start.6

commit v5 on v4

--- a/solution.py
+++ b/solution.py
@@ -2,6 +2,7 @@
 
 import jax
 import jax.numpy as jnp
+import numpy as np
 from jax import lax
 from jax.experimental import pallas as pl
 from jax.experimental.pallas import tpu as pltpu
@@ -360,39 +361,40 @@
 
     def spread(self, pieces, blocks):
         dp, row, col = place()
+        feat, own = pieces.shape[1], blocks.shape[1]
         for image in (0, 1):
             for half in (0, 1):
                 chip = 2 * dp + image
                 slot = flip(chip, row)
                 mine = (dp == half) & (chip == row)
-                index = 2 * image + half
-                copy = self.remote(
-                    pieces.at[image, half], blocks.at[slot], index, slot, (half, chip, col)
-                )
-                here = pltpu.make_async_copy(
-                    pieces.at[image, half], blocks.at[0], self.sems[2]
-                )
+                source = pieces.at[image, :, pl.ds(half * own, own)]
+                target = blocks.at[pl.ds(pl.multiple_of(slot * feat, 16), feat)]
+                copy = self.remote(source, target, 2 * image + half, slot, (half, chip, col))
+                here = pltpu.make_async_copy(source, blocks.at[pl.ds(0, feat)], self.sems[2])
                 self.start(copy, here, mine)
-        own = dp == row // 2
-        self.into = [(blocks.at[k], k, own if k == 0 else None) for k in range(4)]
+        mine = dp == row // 2
+        self.into = [
+            (blocks.at[pl.ds(k * feat, feat)], k, None if k else mine) for k in range(4)
+        ]
 
     def collect(self, blocks, pieces):
         dp, row, col = place()
+        feat, own = pieces.shape[1], blocks.shape[1]
         image = lax.rem(row, 2)
         for k in range(4):
             owner = flip(row, k)
-            index = 2 * image + dp
             mine = (dp == row // 2) & (owner == row)
-            copy = self.remote(
-                blocks.at[k], pieces.at[image, dp], k, index, (row // 2, owner, col)
-            )
-            here = pltpu.make_async_copy(blocks.at[k], pieces.at[image, dp], self.sems[2])
+            source = blocks.at[pl.ds(k * feat, feat)]
+            target = pieces.at[image, :, pl.ds(pl.multiple_of(dp * own, 128), own)]
+            copy = self.remote(source, target, k, 2 * image + dp, (row // 2, owner, col))
+            here = pltpu.make_async_copy(source, target, self.sems[2])
             self.start(copy, here, mine)
         self.into = []
         for image in (0, 1):
             for half in (0, 1):
-                own = (dp == half) & (2 * dp + image == row)
-                self.into.append((pieces.at[image, half], 2 * image + half, own))
+                mine = (dp == half) & (2 * dp + image == row)
+                target = pieces.at[image, :, pl.ds(half * own, own)]
+                self.into.append((target, 2 * image + half, mine))
 
     def start(self, copy, here, mine):
         pl.when(jnp.logical_not(mine))(copy.start)
@@ -497,6 +499,7 @@
     x_pieces,
     teacher_pieces,
     count_ref,
+    valid_ref,
     params_ref,
     key_ref,
     key_lane_ref,
@@ -512,20 +515,27 @@
     slope_out,
     norm1t_out,
     norm2t_out,
+    rest_hbm,
+    lse_hbm,
+    act_rest_hbm,
+    slope_rest_hbm,
+    resid_hbm,
+    x_hbm,
+    branch_out,
+    brancht_out,
+    result_out,
+    err_out,
+    feature_ref,
+    count_out,
     rest_out,
     lse_out,
     act_rest_out,
     slope_rest_out,
     resid_out,
-    grad_out,
-    branch_out,
-    brancht_out,
-    result_out,
-    err_out,
-    x_ref,
-    feature_ref,
-    count_out,
-    teacher_ref,
+    x_rows,
+    x_blocks,
+    teacher_blocks,
+    valid_in,
     features_in,
     biases_in,
     counts_in,
@@ -730,8 +740,9 @@
 
     saved, ff_saved = [], []
     x_move = Shuffle(shuffle_sems.at[0], shuffle_sems.at[1], shuffle_sems.at[2, 0])
-    x_move.spread(x_pieces, x_ref)
+    x_move.spread(x_pieces, x_blocks)
     attn_ring(0)
+    first = ff_first()
     attn_plane(0)
     own_params = [
         keep(params_ref.at[:, pl.ds(0, wide)], features_in.at[0]),
@@ -753,8 +764,7 @@
     ]
     teacher_move = Shuffle(shuffle_sems.at[3], shuffle_sems.at[4], shuffle_sems.at[2, 1])
 
-    def token_rows(at):
-        return jnp.concatenate([x_ref[k, at, :].astype(F32) for k in range(4)], axis=1)
+    valid_move = send(valid_ref, valid_in, peers["core"])
 
     az[1].wait_recv()
     attn_ring(1)
@@ -763,7 +773,6 @@
     az[2].wait_recv()
     attn_ring(2)
     attn_plane(2)
-    first = ff_first()
     for copy in own_params:
         copy.wait()
     arrive(smalls)
@@ -773,9 +782,12 @@
             [features_in[k, 0:1, pitch * i : pitch * i + feat] for k in range(4)], axis=1
         )
     x_move.arrive()
+    for start in range(0, own, 128):
+        x_rows[pl.ds(start, 128), :] = x_blocks[:, pl.ds(start, 128)].T
+    late = [keep(x_rows, x_hbm)]
 
     def first_norm(at):
-        normed, _ = norm_stats(token_rows(at))
+        normed, _ = norm_stats(x_rows[at, :].astype(F32))
         norm1[at, :] = (normed * feature_ref[0:1] + feature_ref[1:2]).astype(BF16)
 
     each_rows(own, 128, first_norm)
@@ -795,17 +807,19 @@
     arrive(fz[1])
     ff_ring(1)
     ff_last(1)
+    teacher_move.spread(teacher_pieces, teacher_blocks)
     attn_compute(2)
     swap2 = attn_compute(3)
     swap2.wait_recv()
 
     def second_norm(at):
-        values = token_rows(at) + part[at, :] + got1[at, :].astype(F32) + feature_ref[4:5]
+        values = x_rows[at, :].astype(F32) + part[at, :] + got1[at, :].astype(F32) + feature_ref[4:5]
         resid_out[at, :] = values
         normed, _ = norm_stats(values)
         norm2[at, :] = (normed * feature_ref[2:3] + feature_ref[3:4]).astype(BF16)
 
     each_rows(own, 128, second_norm)
+    late += [keep(resid_out, resid_hbm), keep(rest_out, rest_hbm), keep(lse_out, lse_hbm)]
     swap3 = send(norm2.at[pl.ds(0, own)], norm2.at[pl.ds(own, own)], peers["core"])
     arrive(fz[2])
     ff_ring(2)
@@ -814,13 +828,13 @@
     turn1 = keep(turned, norm1t_out)
     swap3.wait_recv()
     rest_compute()
+    late += [keep(act_rest_out, act_rest_hbm), keep(slope_rest_out, slope_rest_hbm)]
     turn1.wait()
     transpose_into(turned, norm2)
     turn2 = keep(turned, norm2t_out)
     ff_compute(0)
     arrive(fz[3])
     ff_last(3)
-    teacher_move.spread(teacher_pieces, teacher_ref)
     ff_compute(1)
     ff_compute(2)
     swap4 = ff_compute(3)
@@ -834,24 +848,28 @@
     teacher_move.arrive()
     swap4.wait_recv()
 
-    def finish(at):
+    valid_move.wait_recv()
+    image, from_here = lax.rem(row, 2), dp == row // 2
+
+    def finish(start):
+        at = pl.ds(start, 128)
         values = resid_out[at, :] + part[at, :] + got2[at, :].astype(F32) + feature_ref[5:6]
-        for k in range(4):
-            result_out[k, at, :] = values[:, k * feat : (k + 1) * feat].astype(BF16)
-        target = [teacher_ref[k, at, :feat].astype(F32) for k in range(4)]
-        error = values - jnp.concatenate(target, axis=1)
-        masked = error * teacher_ref[0, at, feat : feat + 1].astype(F32)
+        result_out[:, at] = values.astype(BF16).T
+        error = values - teacher_blocks[:, at].T.astype(F32)
+        lanes_at = pl.ds(pl.multiple_of(dp * own + start, 128), 128)
+        counts_row = jnp.where(
+            from_here, valid_ref[image, :, lanes_at], valid_in[image, :, lanes_at]
+        )
+        masked = error * counts_row.T[:, 0:1]
         err_out[...] = err_out[...] + fold(error * masked)
-        grad = masked * factor
-        grad_out[at, :] = grad
-        branch_out[at, :] = grad.astype(BF16)
+        branch_out[at, :] = (masked * factor).astype(BF16)
 
     def turn(start):
         brancht_out[:, pl.ds(start, 128)] = branch_out[pl.ds(start, 128), :].T
 
     swaps = []
     for start in range(0, own, 128):
-        finish(pl.ds(start, 128))
+        finish(start)
         swaps.append(
             send(
                 branch_out.at[pl.ds(start, 128)],
@@ -869,6 +887,8 @@
             copy.wait()
     for copy in ff_saved:
         copy.wait()
+    for copy in late:
+        copy.wait()
     send.finish()
     x_move.finish()
     teacher_move.finish()
@@ -888,27 +908,34 @@
         ((4, tokens, main), BF16, anywhere),
         ((depth, tokens), BF16, anywhere),
         ((depth, tokens), BF16, anywhere),
-        ((depth, 256), BF16, local),
-        ((8, 1, tokens), F32, local),
-        ((tokens, 128), BF16, local),
-        ((tokens, 128), BF16, local),
-        ((own, depth), F32, local),
-        ((own, depth), F32, local),
+        ((depth, 256), BF16, anywhere),
+        ((8, 1, tokens), F32, anywhere),
+        ((tokens, 128), BF16, anywhere),
+        ((tokens, 128), BF16, anywhere),
+        ((own, depth), F32, anywhere),
+        ((own, depth), BF16, anywhere),
         ((tokens, depth), BF16, local),
         ((depth, tokens), BF16, local),
-        ((4, own, feat), BF16, local),
+        ((depth, own), BF16, local),
         ((16, depth), F32, local),
-        ((4, own, feat), BF16, local),
         ((8, depth), F32, local),
         ((8, 128), F32, local),
     ]
     return pl.pallas_call(
         functools.partial(forward_kernel, own_tokens),
         out_shape=[jax.ShapeDtypeStruct(shape, dtype) for shape, dtype, _ in shapes],
-        in_specs=[anywhere] * 2 + [local] * 6 + [anywhere] * 2,
+        in_specs=[anywhere] * 2 + [local] * 7 + [anywhere] * 2,
         out_specs=[spec for _, _, spec in shapes],
         scratch_shapes=[
-            pltpu.VMEM((4, own, arrays[1].shape[-1]), BF16),
+            pltpu.VMEM((depth, 256), BF16),
+            pltpu.VMEM((8, 1, tokens), F32),
+            pltpu.VMEM((tokens, 128), BF16),
+            pltpu.VMEM((tokens, 128), BF16),
+            pltpu.VMEM((own, depth), F32),
+            pltpu.VMEM((own, depth), BF16),
+            pltpu.VMEM((depth, own), BF16),
+            pltpu.VMEM((depth, own), BF16),
+            pltpu.VMEM((2, 8, tokens), F32),
             pltpu.VMEM((4, 8, wide), F32),
             pltpu.VMEM((4, 8, narrow), F32),
             pltpu.VMEM((8, 8, 128), F32),
@@ -927,7 +954,7 @@
             pltpu.VMEM((own, depth), BF16),
             pltpu.VMEM((own, depth), BF16),
             pltpu.VMEM((own, depth), BF16),
-            pltpu.SemaphoreType.DMA((32,)),
+            pltpu.SemaphoreType.DMA((40,)),
             pltpu.SemaphoreType.DMA((72,)),
             pltpu.SemaphoreType.DMA((72,)),
             pltpu.SemaphoreType.DMA((5, 4)),
@@ -947,11 +974,10 @@
     feature_ref,
     spread_ref,
     rest_spread_ref,
-    x_ref,
-    resid_ref,
     err_ref,
     result_blocks,
-    grad_hbm,
+    x_hbm,
+    resid_hbm,
     norm1t_hbm,
     norm2t_hbm,
     branch2t_hbm,
@@ -967,6 +993,7 @@
     bias_out,
     attn_out,
     ff_out,
+    x_rows,
     grad_blocks,
     terms,
     terms_mine,
@@ -1046,7 +1073,7 @@
     loads = {3: load_ff(3)}
     turns = [keep(norm2t_hbm, normt), keep(branch2t_hbm, brancht)]
     loads[2] = load_ff(2)
-    load_grad = keep(grad_hbm, grad_mid)
+    load_late = [keep(resid_hbm, grad_mid), keep(x_hbm, x_rows)]
     meet()
     result_move = Shuffle(shuffle_sems.at[0], shuffle_sems.at[1], shuffle_sems.at[2, 0])
     grad_move = Shuffle(shuffle_sems.at[3], shuffle_sems.at[4], shuffle_sems.at[2, 1])
@@ -1249,17 +1276,19 @@
     swap1 = rest_compute()
     load_norm = keep(norm1t_hbm, normt)
     swap1.wait_recv()
-    load_grad.wait()
+    for copy in load_late:
+        copy.wait()
 
     def mid(at):
-        normed, inv_scale = norm_stats(resid_ref[at, :])
+        normed, inv_scale = norm_stats(grad_mid[at, :])
         grad_norm = part[at, :] + got[at, :].astype(F32)
         add_term(2, grad_norm * normed)
         add_term(3, grad_norm)
         scaled = grad_norm * feature_ref[2:3]
         first = jnp.mean(scaled, axis=-1, keepdims=True)
         second = jnp.mean(scaled * normed, axis=-1, keepdims=True)
-        grad = grad_mid[at, :] + inv_scale * (scaled - first - normed * second)
+        grad = branch2_ref[at, :].astype(F32)
+        grad = grad + inv_scale * (scaled - first - normed * second)
         grad_mid[at, :] = grad
         low = grad.astype(BF16)
         branch1[at, :] = low
@@ -1277,8 +1306,8 @@
     attn_plane(3)
     attn_compute(1)
     attn_plane(2)
+    attn_ring(3)
     ff_add(1)
-    attn_ring(3)
     swap1.wait_send()
     swap3 = attn_compute(0)
     attn_plane(1)
@@ -1286,11 +1315,8 @@
     attn_plane(0)
     swap3.wait_recv()
 
-    def token_rows(at):
-        return jnp.concatenate([x_ref[k, at, :].astype(F32) for k in range(4)], axis=1)
-
     def last(at):
-        normed, inv_scale = norm_stats(token_rows(at))
+        normed, inv_scale = norm_stats(x_rows[at, :].astype(F32))
         grad_norm = part[at, :] + got[at, :].astype(F32)
         add_term(0, grad_norm * normed)
         add_term(1, grad_norm)
@@ -1298,10 +1324,9 @@
         first = jnp.mean(scaled, axis=-1, keepdims=True)
         second = jnp.mean(scaled * normed, axis=-1, keepdims=True)
         grad = grad_mid[at, :] + inv_scale * (scaled - first - normed * second)
-        for k in range(4):
-            grad_blocks[k, at, :] = grad[:, k * feat : (k + 1) * feat].astype(BF16)
-
-    each_rows(own, 64, last)
+        grad_blocks[:, at] = grad.astype(BF16).T
+
+    each_rows(own, 128, last)
     grad_move.collect(grad_blocks, grad_pieces)
     terms_mine[...] = jnp.zeros_like(terms_mine)
     bias_mine[...] = jnp.zeros_like(bias_mine)
@@ -1380,8 +1405,8 @@
     anywhere = pl.BlockSpec(memory_space=pl.ANY)
     local = pl.BlockSpec(memory_space=pltpu.VMEM)
     shapes = [
-        ((2, 2, own, feat), BF16, anywhere),
-        ((2, 2, own, feat), BF16, anywhere),
+        ((2, feat, tokens), BF16, anywhere),
+        ((2, feat, tokens), BF16, anywhere),
         ((8, feat), F32, local),
         ((2, 8, narrow), F32, local),
         ((2, half, lanes), BF16, anywhere),
@@ -1390,10 +1415,11 @@
     return pl.pallas_call(
         backward_kernel,
         out_shape=[jax.ShapeDtypeStruct(shape, dtype) for shape, dtype, _ in shapes],
-        in_specs=[local] * 11 + [anywhere] * 11,
+        in_specs=[local] * 9 + [anywhere] * 12,
         out_specs=[spec for _, _, spec in shapes],
         scratch_shapes=[
-            pltpu.VMEM((4, own, feat), BF16),
+            pltpu.VMEM((own, depth), BF16),
+            pltpu.VMEM((depth, own), BF16),
             pltpu.VMEM((6, 16, depth), F32),
             pltpu.VMEM((4, 8, feat), F32),
             pltpu.VMEM((3, 8, feat), F32),
@@ -1482,8 +1508,8 @@
         return jnp.where(first, low, high)
 
     def pieces(values):
-        values = jnp.pad(values.reshape(images, SEQ, -1), ((0, 0), (0, pad_seq - SEQ), (0, 0)))
-        return values.reshape(images, 2, half_seq, -1)
+        values = values.reshape(images, SEQ, -1).transpose(0, 2, 1)
+        return jnp.pad(values, ((0, 0), (0, 0), (0, pad_seq - SEQ)))
 
     up_half, down_half = core_half(w_up, 1), core_half(w_down, 0).T
     attn_shard = jnp.concatenate(
@@ -1497,25 +1523,25 @@
         axis=1,
     )
     ff_shard = jnp.concatenate([up_half[:, :main], down_half[:, :main]], axis=1)
-    lane = jnp.arange(lanes)
-    spread_at = jnp.where(lane < at, lane // HD * 128 + lane % HD, -1)
-    spread = (spread_at[:, None] == jnp.arange(qkv + mix)[None]).astype(jnp.bfloat16)
+    lane = np.arange(lanes)
+    spread_at = np.where(lane < at, lane // HD * 128 + lane % HD, -1)
+    spread = jnp.asarray(spread_at[:, None] == np.arange(qkv + mix), jnp.bfloat16)
     tail = lane[-128:]
-    part = jnp.arange(cols)[:, None]
-    up_at = jnp.where((tail >= at) & (tail < at + rest), tail - at + part * rest, -1)
-    down_at = jnp.where(
+    part = np.arange(cols)[:, None]
+    up_at = np.where((tail >= at) & (tail < at + rest), tail - at + part * rest, -1)
+    down_at = np.where(
         (tail >= at + rest) & (tail < at + 2 * rest), tail - at - rest + part * rest + 128, -1
     )
-    spot = jnp.arange(256)
+    spot = np.arange(256)
     rest_spread = (up_at[..., None] == spot) | (down_at[..., None] == spot)
-    rest_spread = rest_spread.astype(jnp.bfloat16)
+    rest_spread = jnp.asarray(rest_spread, jnp.bfloat16)
 
     place_of = jnp.arange(pad_seq)
     token = jnp.where(
         place_of < half_seq, place_of + core * half_seq, place_of - core * half_seq
     )
     key_column = jnp.where(token < SEQ, 0.0, -1e30).astype(jnp.float32)[:, None]
-    key_lane = (jnp.arange(qkv) % 384 == 128 + HD).astype(jnp.float32)[None]
+    key_lane = jnp.asarray(np.arange(qkv) % 384 == 128 + HD, jnp.float32)[None]
 
     query_bias, value_bias = core_half(bias_query, 0), core_half(bias_value, 0)
     unit_bias = core_half(bias_up, 0)
@@ -1538,23 +1564,16 @@
     params = jnp.broadcast_to(params[None], (8, params.shape[0]))
     count = jnp.broadcast_to(jnp.sum(valid).astype(jnp.float32), (8, 128))
 
-    marked = jnp.concatenate(
-        [
-            teacher,
-            valid.astype(jnp.bfloat16)[:, None],
-            jnp.zeros((teacher.shape[0], pitch - feat - 1), jnp.bfloat16),
-        ],
-        axis=1,
-    )
+    valid_rows = jnp.pad(valid.reshape(images, SEQ), ((0, 0), (0, pad_seq - SEQ)))
+    valid_rows = jnp.broadcast_to(valid_rows.astype(jnp.float32)[:, None], (images, 8, pad_seq))
     sizes = (feat, lanes, main, qkv, mix, half_seq, 4 * feat)
     (
         wpad, wff, triple, mixed, act, slope, norm1t, norm2t, rest_weight, lse, act_rest,
-        slope_rest, resid1, grad_result, branch2, branch2t, result, err_rows, x_blocks,
-        features, counted,
+        slope_rest, resid1, x_rows, branch2, branch2t, result, err_rows, features, counted,
     ) = forward_call(
         (
-            pieces(layer_input), pieces(marked), count, params, key_column, key_lane, spread,
-            rest_spread, attn_shard, ff_shard,
+            pieces(layer_input), pieces(teacher), count, valid_rows, params, key_column, key_lane,
+            spread, rest_spread, attn_shard, ff_shard,
         ),
         layer_input.shape[0],
         *sizes,
@@ -1562,14 +1581,14 @@
     grad_pieces, result_pieces, sums, bias_rows, attn_sum, ff_sum = backward_call(
         (
             branch2, rest_weight, act_rest, slope_rest, lse, features, spread, rest_spread,
-            x_blocks, resid1, err_rows, result, grad_result, norm1t, norm2t, branch2t, wpad,
+            err_rows, result, x_rows, resid1, norm1t, norm2t, branch2t, wpad,
             wff, triple, mixed, act, slope,
         ),
         *sizes,
     )
 
     def rows_of(values):
-        return values.reshape(images, pad_seq, feat)[:, :SEQ].reshape(images * SEQ, feat)
+        return values[:, :, :SEQ].transpose(0, 2, 1).reshape(images * SEQ, feat)
 
     def both(keep, got, axis=-1):
         return jnp.concatenate(

time: 383 us -> 353 us (0.922)
  Pallas kernels: 332 us -> 304 us
    pallas_call x1, Pallas kernels: 178 us -> 154 us  [forward_call(): pl.pallas_call(functools.partial(forward_kernel, own_tokens), out_shape=[...]
    pallas_call x1, Pallas kernels: 154 us -> 150 us  [backward_call(): pl.pallas_call(backward_kernel, out_shape=[jax.ShapeDtypeStruct(shape, dt...]
where the time goes in v5:
time: 353 us; the launch traced here: 348 us
  Pallas kernels  304 us (86%)
  local copies, waits for them, and re-layouts  26.3 us (7%)
  other arithmetic  13.4 us (4%)
  between operations  4.28 us (1%)
    pallas_call x1, Pallas kernels, forward_call(): pl.pallas_call(functools.partial(forward_kernel, own_tokens), out_shape=[...  154 us
    pallas_call x1, Pallas kernels, backward_call(): pl.pallas_call(backward_kernel, out_shape=[jax.ShapeDtypeStruct(shape, dt...  150 us

profile of v5, /device:TPU:0, one launch (start us, length us, event | category | flops | bytes accessed | tf_op | source)
XLA Modules:
  0.0 347.8 jit_solution(12754091881007986074)
XLA Ops:
  0.6 0.0 copy-start.4
  0.7 0.0 copy-start.6
  0.7 1.4 reduce_sum.18
  2.8 0.8 broadcast_select_fusion.7
  3.6 0.8 broadcast_select_fusion.6
  4.4 0.1 fusion.13
  4.5 0.1 fusion.14
  4.6 0.8 slice_select_fusion.2
  5.5 4.2 %concatenate.126 = bf16[3712]{0:T(1024)(128)(2,1)S(1)} concatenate(bf16[288]{0:T(512)(128)(2,1)} %param.27, bf16[96]{0:T(256)(128)(2,1)S(1)} %concatenate.123, bf16[288]{0:T(512)(128)(2,1)} %param.28, bf16[96]{0:T(256)(128)(2,1)S(1)} %concatenate.123, bf16[288]{0:T(512)(128)(2,1)} %param.29, bf16[96]{0:T(256)(128)(2,1)S(1)} %concatenate.123, bf16[288]{0:T(512)(128)(2,1)} %param.30, ...), dimensions={0} | concatenate | bytes 14848 | tf_op jit(solution)/shard_map/concatenate | solution.py:1563
  9.7 0.6 broadcast_in_dim.40.count_ref
  10.3 0.8 reshape.420
  11.1 0.6 broadcast_in_dim.41.valid_ref
  11.7 0.7 broadcast_in_dim.44.params_ref
  12.4 1.0 fusion.10
  13.3 0.1 copy.44
  13.5 0.0 copy-start.5
  13.5 0.1 copy.43
  13.6 0.0 copy-done.6
  13.6 0.1 slice_select_fusion.1
  13.8 0.2 slice_select_fusion
  14.0 0.5 copy-done.5
  14.6 0.2 select_bitcast_fusion
  14.7 0.0 copy-start
  14.8 1.0 concatenate.127.attn_ref
  15.7 0.9 pad_maximum_fusion.ff_ref
  16.6 0.8 fusion.key_ref
  17.4 0.0 copy-done
  17.4 0.9 reshape.418
  18.4 0.0 copy-start.1
  18.4 0.1 copy.48
  18.5 1.0 pad.11.x_pieces
  19.5 0.2 copy-done.1
  19.7 0.9 reshape.419
  20.6 0.1 copy.47
  20.7 1.0 pad.12.teacher_pieces
  21.7 154.0 %shard_map.306 = (bf16[4,1152,1024]{2,1,0:T(8,128)(2,1)}, bf16[4,1152,1024]{2,1,0:T(8,128)(2,1)}, bf16[4,768,768]{2,1,0:T(8,128)(2,1)}, bf16[4,768,256]{2,1,0:T(...) custom-call(bf16[2,288,768]{2,1,0:T(8,128)(2,1)} %pad.11.x_pieces, ...), custom_call_target="tpu_custom_call" | custom-call | tf_op jit(solution)/shard_map/pallas_call | solution.py:924
  175.7 1.2 slice.177
  177.5 149.8 %shard_map.307 = (bf16[2,288,768]{2,1,0:T(8,128)(2,1)}, bf16[2,288,768]{2,1,0:T(8,128)(2,1)}, f32[8,288]{1,0:T(8,128)}, f32[2,8,1408]{2,1,0:T(8,128)}, bf16[2,14...) custom-call(bf16[768,1152]{1,0:T(8,128)(2,1)} %get-tuple-element.42.branch2_ref, ...), custom_call_target="tpu_custom_call" | custom-call | tf_op jit(solution)/shard_map/pallas_call | solution.py:1415
  327.3 0.0 copy-start.7
  327.3 1.2 slice.176
  329.2 0.9 slice_add_fusion
  330.2 0.9 slice_reduce_fusion
  331.2 0.1 select_n.218
  331.2 0.1 select_n.216
  331.3 0.1 select_n.220
  331.4 0.1 select_n.214
  331.5 0.7 pad_maximum_fusion.7
  332.2 0.7 pad_maximum_fusion.5
  332.8 1.6 slice_reduce_fusion.1
  334.4 1.0 slice_bitcast_fusion.4
  335.4 0.1 fusion.11
  335.5 0.1 fusion.12
  335.6 0.1 select_bitcast_fusion.9
  335.8 0.8 maximum_convert_fusion.3
  336.6 0.9 maximum_convert_fusion.2
  337.6 0.2 select_bitcast_fusion.2
  337.7 1.0 maximum_convert_fusion.1
  338.7 1.0 maximum_convert_fusion
  339.7 0.0 copy-done.2
  339.7 0.2 convert_bitcast_fusion
  339.9 1.4 copy.42
  341.2 2.7 reshape.423
  343.9 0.9 copy.41
  344.9 1.6 reshape.421
  (28 shorter events, 0.3 us)
Async XLA Ops:
  0.6 13.1 %copy-start.4 = (bf16[288,1076]{1,0:T(8,128)(2,1)S(1)}, bf16[288,1076]{1,0:T(8,128)(2,1)}, u32[]{:S(2)}) copy-start(bf16[288,1076]{1,0:T(8,128)(2,1)} %param.31) | copy-start | bytes 1859332
  0.7 13.0 %copy-start.6 = (bf16[288,864]{1,0:T(8,128)(2,1)S(1)}, bf16[288,864]{1,0:T(8,128)(2,1)}, u32[]{:S(2)}) copy-start(bf16[288,864]{1,0:T(8,128)(2,1)} %param.22) | copy-start | bytes 1492996
  13.5 1.1 copy-start.5
  14.7 2.7 copy-start
  18.4 1.3 copy-start.1
  327.3 10.1 %copy-start.7 = (bf16[2,144,1024]{2,1,0:T(8,128)(2,1)S(1)}, bf16[2,144,1024]{2,1,0:T(8,128)(2,1)}, u32[]{:S(2)}) copy-start(bf16[2,144,1024]{2,1,0:T(8,128)(2,1)} %get-tuple-element.67) | copy-start | bytes 1769476
  337.6 2.1 copy-start.2
  337.6 2.1 copy-start.3
